TPU v7x, 32 devices: a whole 2x2x4 slice. The times are simulated.
32 devices in a mesh: group: 2 (over y), row: 4 (over z), col: 2 (over x), sub: 2 (over core).
Axes of the slice: x: 2, y: 2, z: 4, core: 2. Of those that a mesh axis runs over, the one named last changes fastest.
Arguments:
- anomalies: bfloat16 [2048, 2048], P(('group', 'row', 'sub')), parts along dimension 0, may hold values from -6 to 6
- innovations: float32 [4096], P(('group', 'row', 'col', 'sub')), parts along dimension 0, may hold values from -12 to 12
- obs_error: float32 [4096], P(('group', 'row', 'col', 'sub')), parts along dimension 0, may hold values from 0.5 to 2
- track_pos: float32 [4096], P('group'), parts along dimension 0, may hold values from 0 to 1
- taper_class: int32 [8, 4], P('group'), parts along dimension 0, may hold values from 0 to 3, as said below
Outputs:
- solution: float32 [4096], P(('group', 'row', 'col', 'sub')), parts along dimension 0
- residual: float32 [4096], P(('group', 'row', 'col', 'sub')), parts along dimension 0
There are 2 independent parts, one for each index of `group`. A program takes and returns all parts, laid end to end along the dimension named above; each array names one. Nothing has to cross between parts.
Inputs may be any that keep to these rules, and one draw needn't show every extreme that they name: `taper_class`: tiles are spatial blocks of the region, laid along the plume in an order given by a permutation pos of the 4 tiles; entry (a, b) is the distance |pos[a] - pos[b]| in tiles.
All inputs are finite; a program needn't handle non-finite values.
Results may differ from a plain program's by a relative error of at most 0.0003.
Values may be sent and summed in bfloat16 or wider, within the bound.
No kernel may reach another device: no remote copies, remote signals or barrier semaphores. Data moves between devices by JAX's collectives and lax.ppermute only.
A program may use at most 64 MiB of HBM per device.

v0:
```python
import jax
import jax.numpy as jnp
from jax import lax
from jax.sharding import PartitionSpec as P

ITERS = 2


track_width = 0.0001


def squares(residual):
    return lax.psum(jnp.sum(residual * residual), ("row", "col", "sub"))


def per_device(anomalies, innovations, obs_error, track_pos, taper_class):
    row_count = lax.axis_size("row")
    col_count = lax.axis_size("col")
    sub_count = lax.axis_size("sub")
    row_index = lax.axis_index("row")
    col_index = lax.axis_index("col")
    local_members, total_obs = anomalies.shape
    block_len = total_obs // row_count
    quarter_len = block_len // col_count
    member_total = local_members * row_count * sub_count
    inverse_members = 1.0 / (member_total - 1)
    reach_tiles = max(2, row_count // 4)
    class_row = lax.dynamic_index_in_dim(taper_class, row_index, 0, keepdims=False)
    tile_weight = jnp.maximum(0.0, 1.0 - class_row.astype(jnp.float32) / reach_tiles)
    row_pos = lax.dynamic_slice_in_dim(track_pos, row_index * block_len, block_len, 0)
    col_pos = lax.dynamic_index_in_dim(
        track_pos.reshape(row_count, col_count, quarter_len), col_index, 1, keepdims=False
    )
    own_block = lax.all_to_all(anomalies, "row", split_axis=1, concat_axis=0, tiled=True)
    own_quarter = lax.dynamic_slice_in_dim(own_block, col_index * quarter_len, quarter_len, 1)

    def one_tile(piece, block_index, keep_factor):
        product = jnp.einsum("mi,mq->iq", own_block, piece, preferred_element_type=jnp.float32)
        column_pos = lax.dynamic_index_in_dim(col_pos, block_index, 0, keepdims=False)
        weight_here = lax.dynamic_index_in_dim(tile_weight, block_index, 0, keepdims=False)
        distance = row_pos[:, None] - column_pos[None, :]
        taper = weight_here * keep_factor * jnp.exp(-(distance * distance) / track_width)
        return product * (taper * inverse_members)

    def one_entry(entry):
        return one_tile(entry[0], entry[1], 1.0)

    piece = lax.all_gather(own_quarter[None], "row", axis=0, tiled=True)
    indices = jnp.arange(piece.shape[0], dtype=jnp.int32)
    tiles = lax.map(one_entry, (piece, indices))
    solution = jnp.zeros_like(innovations)
    residual = innovations
    direction_vec = innovations
    norm_now = squares(residual)
    for turn_index in range(ITERS):
        column_vec = lax.all_gather(direction_vec, ("row", "sub"), axis=0, tiled=True).reshape(
            row_count, quarter_len
        )
        direct = jnp.einsum("jiq,jq->i", tiles, column_vec, precision=lax.Precision.HIGHEST)
        extra = obs_error * direction_vec
        own_part = lax.psum_scatter(direct, ("col", "sub"), scatter_dimension=0, tiled=True)
        image = own_part + extra
        alpha = norm_now / lax.psum(jnp.sum(direction_vec * image), ("row", "col", "sub"))
        solution = solution + alpha * direction_vec
        residual = residual - alpha * image
        if turn_index + 1 < ITERS:
            norm_next = squares(residual)
            direction_vec = residual + norm_next / norm_now * direction_vec
            norm_now = norm_next
    return (solution, residual)


def solution(mesh):
    in_specs = (
        P(("group", "row", "sub"), None),
        P(("group", "row", "col", "sub")),
        P(("group", "row", "col", "sub")),
        P("group"),
        P("group", None),
    )
    out_specs = (P(("group", "row", "col", "sub")), P(("group", "row", "col", "sub")))
    return jax.shard_map(
        per_device, mesh=mesh, in_specs=in_specs, out_specs=out_specs, check_vma=False
    )
```

profile of v0, /device:TPU:0, one launch (start us, length us, event | category | flops | bytes accessed | tf_op | source)
XLA Modules:
  0.0 207.6 jit_solution(16276653144272945120)
XLA Ops:
  7.2 1.9 copy.16
  9.1 6.3 %all-to-all-start = ((bf16[128,4,512]{2,0,1:T(8,128)(2,1)}), bf16[128,4,512]{2,0,1:T(8,128)(2,1)S(1)}, u32[]{:S(2)}, u32[]{:S(2)}) async-start(bf16[128,4,512]{2,0,1:T(8,128)(2,1)} %bitcast.41), calls=%async_computation | async-start | bytes 1048576 | tf_op jit(solution)/shard_map/all_to_all | solution.py:34
  15.4 14.5 %all-to-all-done = bf16[128,4,512]{2,0,1:T(8,128)(2,1)S(1)} async-done(((bf16[128,4,512]{2,0,1:T(8,128)(2,1)}), bf16[128,4,512]{2,0,1:T(8,128)(2,1)S(1)}, u32[]{:S(2)}, u32[]{:S(2)}) %all-to-all-start) | async-done | bytes 524320 | tf_op jit(solution)/shard_map/all_to_all | solution.py:34
  29.9 0.7 constant_dynamic-slice_fusion.3
  32.1 9.8 %all-gather.1 = f32[8,1,128]{2,1,0:T(1,128)S(1)} all-gather(f32[1,1,128]{2,1,0:T(1,128)S(1)} %bitcast.64), channel_id=1, replica_groups=mesh['group'=2,'row'=4,'col'=2,'sub'=2] {'row','sub'}, dimensions={0}, use_global_device_ids=true | all-gather | bytes 4608 | tf_op jit(solution)/shard_map/all_gather | solution.py:56
  41.8 0.7 maximum_bitcast_fusion
  42.5 15.3 %all-gather.5.cloned.1.call-done = bf16[2048,256]{1,0:T(8,128)(2,1)} async-done(((bf16[512,256]{1,0:T(8,128)(2,1)}), bf16[2048,256]{1,0:T(8,128)(2,1)}) %all-gather.5.cloned.1.call-update) | async-done | bytes 1048592 | tf_op jit(solution)/shard_map/all_gather | solution.py:48
  57.8 20.4 %while.10 = (s32[]{:T(128)}, f32[4,512,256]{1,2,0:T(8,128)S(1)}, bf16[4,512,256]{2,1,0:T(8,128)(2,1)}, bf16[512,512]{1,0:T(8,128)(2,1)S(1)}, s32[4]{0:T(128)S(1)...) while((s32[]{:T(128)}, f32[4,512,256]{1,2,0:T(8,128)S(1)}, ...), condition=%wide.region_3.4_spmd, body=%wide.region_2.3_spmd.sunk | while | flops 135135232 | bytes 1317547 | solution.py:50
  61.0 1.9 fusion.21
  66.1 1.9 fusion.21
  71.2 1.9 fusion.21
  76.3 1.9 fusion.21
  78.2 1.2 fusion.9
  79.4 6.4 %all-reduce = f32[512]{0:T(512)S(1)} all-reduce(f32[512]{0:T(512)S(1)} %bitcast.66), channel_id=3, replica_groups=mesh['group'=2,'row'=4,'col'=2,'sub'=2] {'col','sub'}, use_global_device_ids=true, to_apply=%region_4.5.clone | all-reduce | flops 512 | bytes 4096
  85.8 0.7 multiply_reduce_fusion.2
  86.5 31.6 %all-reduce.2 = (f32[]{:T(128)}, f32[]{:T(128)}) all-reduce(f32[]{:T(128)} %get-tuple-element.46, f32[]{:T(128)} %get-tuple-element.45), channel_id=1, replica_groups=mesh['group'=2,'row'=4,'col'=2,'sub'=2] {'row','col','sub'}, use_global_device_ids=true, to_apply=%region_1.2 | all-reduce | flops 2 | bytes 16 | tf_op jit(solution)/shard_map/psum | solution.py:13
  119.5 0.7 multiply_reduce_fusion.1
  120.1 30.1 %psum.30 = f32[]{:T(128)} all-reduce(f32[]{:T(128)} %get-tuple-element.65), channel_id=1, replica_groups=mesh['group'=2,'row'=4,'col'=2,'sub'=2] {'row','col','sub'}, use_global_device_ids=true, to_apply=%region_8.9 | all-reduce | flops 1 | bytes 8 | tf_op jit(solution)/shard_map/psum | solution.py:13
  151.6 8.4 %all-gather.2 = f32[8,1,128]{2,1,0:T(1,128)S(1)} all-gather(f32[1,1,128]{2,1,0:T(1,128)S(1)} %bitcast.67), channel_id=1, replica_groups=mesh['group'=2,'row'=4,'col'=2,'sub'=2] {'row','sub'}, dimensions={0}, use_global_device_ids=true | all-gather | bytes 4608 | tf_op jit(solution)/shard_map/all_gather | solution.py:56
  160.0 1.2 fusion.10
  161.2 5.9 %all-reduce.1 = f32[512]{0:T(512)S(1)} all-reduce(f32[512]{0:T(512)S(1)} %bitcast.65), channel_id=4, replica_groups=mesh['group'=2,'row'=4,'col'=2,'sub'=2] {'col','sub'}, use_global_device_ids=true, to_apply=%region_9.10.clone | all-reduce | flops 512 | bytes 4096
  167.1 0.7 multiply_reduce_fusion
  167.8 31.1 %psum.31 = f32[]{:T(128)} all-reduce(f32[]{:T(128)} %multiply_reduce_fusion), channel_id=1, replica_groups=mesh['group'=2,'row'=4,'col'=2,'sub'=2] {'row','col','sub'}, use_global_device_ids=true, to_apply=%region_11.12 | all-reduce | flops 1 | bytes 8 | tf_op jit(solution)/shard_map/psum | solution.py:63
  200.2 0.6 multiply_subtract_fusion
  (30 shorter events, 5.5 us)
Async XLA Ops:
  7.2 23.6 %copy-start.3 = (u32[32]{0:T(128)S(1)}, u32[32]{0:T(128)}, u32[]{:S(2)}) copy-start(u32[32]{0:T(128)} %constant.61) | copy-start | bytes 388
  7.2 23.5 %copy-start = (f32[2048]{0:T(1024)S(1)}, f32[2048]{0:T(1024)}, u32[]{:S(2)}) copy-start(f32[2048]{0:T(1024)} %param.10) | copy-start | bytes 24580
  7.2 24.9 %copy-start.1 = (f32[128]{0:T(128)S(1)}, f32[128]{0:T(128)}, u32[]{:S(2)}) copy-start(f32[128]{0:T(128)} %param.8) | copy-start | bytes 1540
  9.1 20.8 %all-to-all-start = ((bf16[128,4,512]{2,0,1:T(8,128)(2,1)}), bf16[128,4,512]{2,0,1:T(8,128)(2,1)S(1)}, u32[]{:S(2)}, u32[]{:S(2)}) async-start(bf16[128,4,512]{2,0,1:T(8,128)(2,1)} %bitcast.41), calls=%async_computation | async-start | bytes 1048576 | tf_op jit(solution)/shard_map/all_to_all | solution.py:34
  15.4 42.4 %all-gather.5.cloned.1.call-start = ((), (), s32[]{:S(2)}) async-start(), calls=%async_computation.1 | async-start | bytes 1310720 | tf_op jit(solution)/shard_map/all_gather | solution.py:48
  78.2 7.6 %copy-start.2 = (f32[128]{0:T(128)S(1)}, f32[128]{0:T(128)}, u32[]{:S(2)}) copy-start(f32[128]{0:T(128)} %param.9) | copy-start | bytes 1540
Sparse Core Ops, SparseCore 0:
  30.8 27.0 all-gather.4
where the time goes:
time: 208 us
  blocking collectives  123 us (59%)
  waiting for transfers between devices  29.8 us (14%)
  between operations  18.8 us (9%)
  matrix products  10.1 us (5%)
  local copies, waits for them, and re-layouts  8.07 us (4%)
  loops' own time  7.89 us (4%)
  starting transfers between devices  6.32 us (3%)
  other arithmetic  3.32 us (2%)
    psum x2, blocking collectives, squares(): return lax.psum(jnp.sum(residual * residual), ('row', 'col', 'sub'))  61.7 us
    psum x1, blocking collectives, per_device(): lax.psum(jnp.sum(direction_vec * image), ('row', 'col', 'sub'))  31.1 us
    all_gather x2, blocking collectives, per_device(): lax.all_gather(direction_vec, ('row', 'sub'), axis=0, tiled=True)  18.2 us
    all_gather x1, waiting for transfers between devices, per_device(): piece = lax.all_gather(own_quarter[None], 'row', axis=0, tiled=True)  15.3 us
    all_to_all x1, waiting for transfers between devices, per_device(): lax.all_to_all(anomalies, 'row', split_axis=1, concat_axis=0, tiled=True)  14.5 us
    unnamed x2, blocking collectives  12.3 us
    another operation x1, loops' own time, per_device(): tiles = lax.map(one_entry, (piece, indices))  7.89 us
    dot_general x4, matrix products, one_tile(): jnp.einsum('mi,mq->iq', own_block, piece, preferred_element_type=jnp.floa...  7.74 us
  transfers between devices with their start and end apart: 2, of which 2 were waited for; matrix products, arithmetic and copies ran while one was open for 1% of the time, Pallas kernels for 0%

commit v1 on v0

--- a/solution.py
+++ b/solution.py
@@ -1,19 +1,245 @@
+import functools
+
 import jax
 import jax.numpy as jnp
 from jax import lax
+from jax.experimental import pallas as pl
+from jax.experimental.pallas import tpu as pltpu
 from jax.sharding import PartitionSpec as P
 
 ITERS = 2
+LANES = 128
 
 
 track_width = 0.0001
+
+
+def share_kernel(reach_tiles, inverse_members, class_ref, pos_ref, own_ref, mate_ref, share_ref, both, turned, column):
+    tiles = class_ref.shape[0]
+    members, total_obs = own_ref.shape
+    block_len = total_obs // tiles
+    both[:members, :] = own_ref[...]
+    both[members:, :] = mate_ref[...]
+    turned[:, :members] = own_ref[...].T
+    turned[:, members:] = mate_ref[...].T
+    for piece in range(total_obs // LANES):
+        at = piece * LANES
+        row = jnp.broadcast_to(pos_ref[:, at : at + LANES], (LANES, LANES))
+        column[at : at + LANES, :] = row.T
+    rows = 128
+
+    def one_pair(pair, carry):
+        a, b = pair // tiles, pair % tiles
+        klass = class_ref[a, b]
+
+        @pl.when(klass < reach_tiles)
+        def _():
+            weight = jnp.maximum(0.0, 1.0 - klass.astype(jnp.float32) / reach_tiles)
+            columns = pl.ds(pl.multiple_of(b * block_len, LANES), block_len)
+            right = both[:, columns]
+            right_pos = pos_ref[:, columns]
+
+            def one_chunk(chunk, carry):
+                at = pl.ds(pl.multiple_of(a * block_len + chunk * rows, rows), rows)
+                product = jnp.dot(turned[at, :], right, preferred_element_type=jnp.float32)
+                left_pos = jnp.concatenate([column[at, :]] * (block_len // LANES), axis=1)
+                distance = left_pos - right_pos
+                taper = weight * jnp.exp(-(distance * distance) * (1.0 / track_width))
+                share_ref[at, columns] = product * (taper * inverse_members)
+                return carry
+
+            lax.fori_loop(0, block_len // rows, one_chunk, 0)
+
+        return carry
+
+    lax.fori_loop(0, tiles * tiles, one_pair, 0)
+
+
+def apply_share(reach_tiles, class_ref, share_ref, vector, sums, out_ref):
+    tiles = class_ref.shape[0]
+    total_obs = share_ref.shape[0]
+    block_len = total_obs // tiles
+    pieces = block_len // LANES
+    rows = 64
+
+    def add_tile(a, b, first):
+        def one_chunk(chunk, carry):
+            at = pl.ds(pl.multiple_of(a * block_len + chunk * rows, rows), rows)
+            total = None if first else sums[at, :]
+            for piece in range(pieces):
+                begin = b * block_len + piece * LANES
+                term = share_ref[at, begin : begin + LANES] * vector[b * pieces + piece : b * pieces + piece + 1, :]
+                total = term if total is None else total + term
+            sums[at, :] = total
+            return carry
+
+        lax.fori_loop(0, block_len // rows, one_chunk, 0)
+
+    for a in range(tiles):
+        add_tile(a, a, True)
+        for b in range(tiles):
+            if b != a:
+                pl.when(class_ref[a, b] < reach_tiles)(functools.partial(add_tile, a, b, False))
+    ones = jnp.ones((8, LANES), jnp.float32)
+    for piece in range(total_obs // LANES):
+        folded = lax.dot_general(
+            ones,
+            sums[piece * LANES : (piece + 1) * LANES, :],
+            (((1,), (1,)), ((), ())),
+            precision=lax.Precision.HIGHEST,
+            preferred_element_type=jnp.float32,
+        )
+        out_ref[piece : piece + 1, :] = folded[0:1, :]
+
+
+def first_kernel(reach_tiles, class_ref, share_ref, vectors_ref, out_ref, vector, sums):
+    vector[...] = vectors_ref[:, :LANES]
+    apply_share(reach_tiles, class_ref, share_ref, vector, sums, out_ref)
+
+
+def total_of(x):
+    return jnp.sum(jnp.sum(x, axis=0, keepdims=True), axis=1, keepdims=True)
+
+
+def second_kernel(reach_tiles, peers, place_ref, class_ref, share_ref, vectors_ref, *refs):
+    parts, refs = refs[:peers], refs[peers:]
+    sent, refs = refs[:peers], refs[peers:]
+    state_ref, direction, residual, start, sums, product = refs
+    innovations, obs_error = vectors_ref[:, :LANES], vectors_ref[:, LANES:]
+    image = obs_error * innovations
+    for part in parts:
+        image = image + part[...]
+    norm_now = total_of(innovations * innovations)
+    alpha = norm_now / total_of(innovations * image)
+    residual_now = innovations - alpha * image
+    norm_next = total_of(residual_now * residual_now)
+    direction_now = residual_now + (norm_next / norm_now) * innovations
+    residual[...] = residual_now
+    direction[...] = direction_now
+    start[...] = alpha * innovations
+    apply_share(reach_tiles, class_ref, share_ref, direction, sums, product)
+    curvature = total_of(direction_now * product[...])
+    extra = obs_error * direction_now
+    own_curvature = total_of(direction_now * extra)
+    row_index, within, per_row = place_ref[0], place_ref[1], place_ref[2]
+    for peer in range(peers):
+        at = (row_index ^ peer) * per_row + within
+        sent[peer][0:1, :] = product[pl.ds(at, 1), :]
+        sent[peer][1:2, :] = jnp.broadcast_to(curvature, (1, LANES))
+    own = row_index * per_row + within
+    state_ref[0:1, :] = start[pl.ds(own, 1), :]
+    state_ref[1:2, :] = residual[pl.ds(own, 1), :]
+    state_ref[2:3, :] = direction[pl.ds(own, 1), :]
+    product[...] = extra
+    state_ref[3:4, :] = product[pl.ds(own, 1), :]
+    state_ref[4:5, :] = jnp.broadcast_to(norm_next, (1, LANES))
+    state_ref[5:6, :] = jnp.broadcast_to(own_curvature, (1, LANES))
+
+
+VMEM_SPEC = pl.BlockSpec(memory_space=pltpu.VMEM)
+SMEM_SPEC = pl.BlockSpec(memory_space=pltpu.SMEM)
+
+
+def swap_rows(x, mask):
+    row_count = lax.axis_size("row")
+    return lax.ppermute(x, "row", [(i, i ^ mask) for i in range(row_count)])
+
+
+def vectors_only(anomalies, innovations, obs_error, track_pos, taper_class):
+    row_count = lax.axis_size("row")
+    col_count = lax.axis_size("col")
+    sub_count = lax.axis_size("sub")
+    row_index = lax.axis_index("row")
+    within = lax.axis_index("col") * sub_count + lax.axis_index("sub")
+    local_members, total_obs = anomalies.shape
+    member_total = local_members * row_count * sub_count
+    inverse_members = 1.0 / (member_total - 1)
+    reach_tiles = max(2, row_count // 4)
+    per_row = col_count * sub_count
+    devices = row_count * per_row
+    pieces = total_obs // LANES
+    f32 = jnp.float32
+
+    packed = jnp.concatenate([innovations, obs_error]).reshape(1, 2 * LANES)
+    packed = jnp.broadcast_to(packed, (devices, 2 * LANES))
+    vectors = lax.all_to_all(packed, ("row", "col", "sub"), split_axis=0, concat_axis=0, tiled=True)
+    mate = lax.ppermute(anomalies, "sub", [(0, 1), (1, 0)])
+
+    params = pltpu.CompilerParams(vmem_limit_bytes=16 * 1024 * 1024)
+    share = pl.pallas_call(
+        functools.partial(share_kernel, reach_tiles, inverse_members),
+        out_shape=pltpu.VMEM((total_obs, total_obs), f32),
+        in_specs=[SMEM_SPEC, VMEM_SPEC, VMEM_SPEC, VMEM_SPEC],
+        out_specs=VMEM_SPEC,
+        scratch_shapes=[
+            pltpu.VMEM((2 * local_members, total_obs), anomalies.dtype),
+            pltpu.VMEM((total_obs, 2 * local_members), anomalies.dtype),
+            pltpu.VMEM((total_obs, LANES), f32),
+        ],
+        compiler_params=params,
+        cost_estimate=pl.CostEstimate(
+            flops=4 * local_members * total_obs * total_obs,
+            bytes_accessed=4 * local_members * total_obs,
+            transcendentals=total_obs * total_obs,
+        ),
+        name="share",
+    )(taper_class, track_pos.reshape(1, total_obs), anomalies, mate)
+
+    part = pl.pallas_call(
+        functools.partial(first_kernel, reach_tiles),
+        out_shape=pltpu.VMEM((pieces, LANES), f32),
+        in_specs=[SMEM_SPEC, VMEM_SPEC, VMEM_SPEC],
+        out_specs=VMEM_SPEC,
+        scratch_shapes=[pltpu.VMEM((pieces, LANES), f32), pltpu.VMEM((total_obs, LANES), f32)],
+        compiler_params=params,
+        name="first",
+    )(taper_class, share, vectors)
+    parts = [part] + [swap_rows(part, mask) for mask in range(1, row_count)]
+
+    place = jnp.stack([row_index, within, jnp.int32(per_row)]).astype(jnp.int32)
+    *sent, state = pl.pallas_call(
+        functools.partial(second_kernel, reach_tiles, row_count),
+        out_shape=[pltpu.VMEM((8, LANES), f32) for _ in range(row_count + 1)],
+        in_specs=[SMEM_SPEC, SMEM_SPEC, VMEM_SPEC, VMEM_SPEC] + [VMEM_SPEC] * row_count,
+        out_specs=[VMEM_SPEC] * (row_count + 1),
+        scratch_shapes=[pltpu.VMEM((pieces, LANES), f32)] * 3
+        + [pltpu.VMEM((total_obs, LANES), f32), pltpu.VMEM((pieces, LANES), f32)],
+        compiler_params=params,
+        name="second",
+    )(place, taper_class, share, vectors, *parts)
+    got = [sent[0]] + [swap_rows(sent[mask], mask) for mask in range(1, row_count)]
+    image, curvature = state[3], state[5]
+    for piece in got:
+        image = image + piece[0]
+        curvature = curvature + piece[1]
+    alpha = state[4] / curvature
+    return state[0] + alpha * state[2], state[1] - alpha * image
+
+
+def fits(anomalies, innovations, obs_error, track_pos, taper_class):
+    row_count = lax.axis_size("row")
+    local_members, total_obs = anomalies.shape
+    share_bytes = 4 * total_obs * total_obs
+    return (
+        ITERS == 2
+        and row_count in (2, 4)
+        and lax.axis_size("sub") == 2
+        and innovations.shape[0] == LANES
+        and total_obs % (row_count * LANES) == 0
+        and local_members % LANES == 0
+        and share_bytes <= 16 * 1024 * 1024
+    )
+
+
+def per_device(*args):
+    return vectors_only(*args) if fits(*args) else blocks(*args)
 
 
 def squares(residual):
     return lax.psum(jnp.sum(residual * residual), ("row", "col", "sub"))
 
 
-def per_device(anomalies, innovations, obs_error, track_pos, taper_class):
+def blocks(anomalies, innovations, obs_error, track_pos, taper_class):
     row_count = lax.axis_size("row")
     col_count = lax.axis_size("col")
     sub_count = lax.axis_size("sub")

time: 208 us -> 52.8 us (0.25)
  blocking collectives: 123 us -> 0 us
  between operations: 18.8 us -> 0.67 us
  Pallas kernels: 0 us -> 17.2 us
  waiting for transfers between devices: 29.8 us -> 13.4 us
  matrix products: 10.1 us -> 0 us
  starting transfers between devices: 6.32 us -> 16.3 us
  loops' own time: 7.89 us -> 0 us
  local copies, waits for them, and re-layouts: 8.07 us -> 3.04 us
    psum x3 -> x0, blocking collectives: 92.8 us -> none  [the longest x2 61.7 us: squares(): return lax.psum(jnp.sum(residual * residual), ('row', 'col', 'sub'))]
    all_gather x2 -> x0, blocking collectives: 18.2 us -> none  [per_device(): lax.all_gather(direction_vec, ('row', 'sub'), axis=0, tiled=True)]
    pallas_call x0 -> x3, Pallas kernels: none -> 17.2 us  [the longest x1 9.71 us: vectors_only(): pl.pallas_call(functools.partial(share_kernel, reach_tiles, inverse_membe...]
    all_gather x1 -> x0, waiting for transfers between devices: 15.3 us -> none  [per_device(): piece = lax.all_gather(own_quarter[None], 'row', axis=0, tiled=True)]
    unnamed x2 -> x0, blocking collectives: 12.3 us -> none
    dot_general x6 -> x0, matrix products: 10.1 us -> none  [the longest x4 7.74 us: one_tile(): jnp.einsum('mi,mq->iq', own_block, piece, preferred_element_type=jnp.floa...]
    ppermute x0 -> x7, starting transfers between devices: none -> 9.33 us  [the longest x6 8.81 us: swap_rows(): return lax.ppermute(x, 'row', [(i, i ^ mask) for i in range(row_count)])]
    all_to_all x1, waiting for transfers between devices: 14.5 us -> 6.49 us  [vectors_only(): lax.all_to_all(packed, ('row', 'col', 'sub'), split_axis=0, concat_axis=0...]
  transfers between devices with their start and end apart: 2 -> 8, of which waited for: 2 -> 5; matrix products, arithmetic and copies ran while one was open for 1% -> 3% of each run, Pallas kernels for 0% -> 0%
where the time goes in v1:
time: 52.8 us; the launch traced here: 52.5 us
  Pallas kernels  17.2 us (33%)
  starting transfers between devices  16.3 us (31%)
  waiting for transfers between devices  13.4 us (25%)
  local copies, waits for them, and re-layouts  3.04 us (6%)
  other arithmetic  1.79 us (3%)
  between operations  0.67 us (1%)
    pallas_call x1, Pallas kernels, vectors_only(): pl.pallas_call(functools.partial(share_kernel, reach_tiles, inverse_membe...  9.71 us
    ppermute x6, starting transfers between devices, swap_rows(): return lax.ppermute(x, 'row', [(i, i ^ mask) for i in range(row_count)])  8.81 us
    all_to_all x1, starting transfers between devices, vectors_only(): lax.all_to_all(packed, ('row', 'col', 'sub'), split_axis=0, concat_axis=0...  7.02 us
    ppermute x6, waiting for transfers between devices, swap_rows(): return lax.ppermute(x, 'row', [(i, i ^ mask) for i in range(row_count)])  6.95 us
    all_to_all x1, waiting for transfers between devices, vectors_only(): lax.all_to_all(packed, ('row', 'col', 'sub'), split_axis=0, concat_axis=0...  6.49 us
    pallas_call x1, Pallas kernels, vectors_only(): pl.pallas_call(functools.partial(second_kernel, reach_tiles, row_count),...  3.84 us
    pallas_call x1, Pallas kernels, vectors_only(): pl.pallas_call(functools.partial(first_kernel, reach_tiles), out_shape=pl...  3.61 us
    unnamed x7, local copies, waits for them, and re-layouts  2.42 us
  transfers between devices with their start and end apart: 8, of which 5 were waited for; matrix products, arithmetic and copies ran while one was open for 3% of the time, Pallas kernels for 0%

profile of v1, /device:TPU:0, one launch (start us, length us, event | category | flops | bytes accessed | tf_op | source)
XLA Modules:
  0.0 52.5 jit_solution(7778529931432903732)
XLA Ops:
  0.6 0.5 collective-permute-start
  1.1 0.7 %pad_maximum_fusion = f32[256]{0:T(256)S(1)} fusion(f32[128]{0:T(128)} %param.7, f32[128]{0:T(128)} %param.6), kind=kLoop, calls=%fused_computation.1 | loop fusion | flops 256 | bytes 2048 | tf_op jit(solution)/shard_map/concatenate | solution.py:163
  1.8 0.6 %broadcast_in_dim.2 = f32[16,1,256]{2,1,0:T(1,128)} broadcast(f32[256]{0:T(256)S(1)} %pad_maximum_fusion), dimensions={2} | broadcast | bytes 17408 | tf_op jit(solution)/shard_map/broadcast_in_dim | solution.py:164
  2.4 7.0 %all-to-all-start = ((f32[16,1,256]{2,1,0:T(1,128)}), f32[16,1,256]{2,1,0:T(1,128)S(1)}, u32[]{:S(2)}, u32[]{:S(2)}) async-start(f32[16,1,256]{2,1,0:T(1,128)} %broadcast_in_dim.2), calls=%async_computation | async-start | bytes 32768 | tf_op jit(solution)/shard_map/all_to_all | solution.py:165
  9.5 6.5 %all-to-all-done = f32[16,1,256]{2,1,0:T(1,128)S(1)} async-done(((f32[16,1,256]{2,1,0:T(1,128)}), f32[16,1,256]{2,1,0:T(1,128)S(1)}, u32[]{:S(2)}, u32[]{:S(2)}) %all-to-all-start) | async-done | bytes 16416 | tf_op jit(solution)/shard_map/all_to_all | solution.py:165
  16.0 1.0 %copy-done = bf16[128,2048]{1,0:T(8,128)(2,1)S(1)} copy-done((bf16[128,2048]{1,0:T(8,128)(2,1)S(1)}, bf16[128,2048]{1,0:T(8,128)(2,1)}, u32[]{:S(2)}) %copy-start) | copy-done | bytes 524312
  17.0 0.7 %copy-done.1 = s32[4,4]{1,0:T(4,128)S(1)} copy-done((s32[4,4]{1,0:T(4,128)S(1)}, s32[4,4]{1,0:T(4,128)}, u32[]{:S(2)}) %copy-start.1) | copy-done | bytes 88
  17.7 0.7 %copy-done.2 = f32[2048]{0:T(1024)S(1)} copy-done((f32[2048]{0:T(1024)S(1)}, f32[2048]{0:T(1024)}, u32[]{:S(2)}) %copy-start.2) | copy-done | bytes 8216
  18.4 9.7 %share.1.share_ref = f32[2048,2048]{1,0:T(8,128)S(1)} custom-call(s32[4,4]{1,0:T(4,128)S(1)} %copy-done.1, f32[1,2048]{1,0:T(1,128)S(1)} %bitcast.12, bf16[128,2048]{1,0:T(8,128)(2,1)S(1)} %copy-done, bf16[128,2048]{1,0:T(8,128)(2,1)S(1)} %collective-permute-done.mate_ref), custom_call_target="tpu_custom_call" | custom-call | flops 2147483648 | bytes 1048576 | tf_op jit(solution)/shard_map/share/pallas_call | solution.py:169
  28.1 3.6 %first.1.refs_0_ = f32[16,128]{1,0:T(8,128)S(1)} custom-call(s32[4,4]{1,0:T(4,128)S(1)} %copy-done.1, f32[2048,2048]{1,0:T(8,128)S(1)} %share.1.share_ref, f32[16,256]{1,0:T(8,128)S(1)} %bitcast.10), custom_call_target="tpu_custom_call" | custom-call | tf_op jit(solution)/shard_map/first/pallas_call | solution.py:188
  31.7 0.5 collective-permute-start.1
  32.2 0.6 %collective-permute-start.2 = (f32[16,128]{1,0:T(8,128)S(1)}, f32[16,128]{1,0:T(8,128)S(1)}, u32[]{:S(2)}, u32[]{:S(2)}) collective-permute-start(f32[16,128]{1,0:T(8,128)S(1)} %first.1.refs_0_), channel_id=1, source_target_pairs={{0,8},{4,12},{8,0},{12,4},{1,9},{5,13},{9,1},{13,5},{2,10},{6,14},... | collective-permute-start | bytes 24584 | tf_op jit(solution)/shard_map/ppermute | solution.py:145
  32.8 3.3 %collective-permute-start.3 = (f32[16,128]{1,0:T(8,128)S(1)}, f32[16,128]{1,0:T(8,128)S(1)}, u32[]{:S(2)}, u32[]{:S(2)}) collective-permute-start(f32[16,128]{1,0:T(8,128)S(1)} %first.1.refs_0_), channel_id=1, source_target_pairs={{0,12},{4,8},{8,4},{12,0},{1,13},{5,9},{9,5},{13,1},{2,14},{6,10},... | collective-permute-start | bytes 24584 | tf_op jit(solution)/shard_map/ppermute | solution.py:145
  36.1 0.1 pad_add_fusion.place_ref
  36.2 0.5 %collective-permute-done.2.refs_2_ = f32[16,128]{1,0:T(8,128)S(1)} collective-permute-done((f32[16,128]{1,0:T(8,128)S(1)}, f32[16,128]{1,0:T(8,128)S(1)}, u32[]{:S(2)}, u32[]{:S(2)}) %collective-permute-start.2) | collective-permute-done | bytes 8224 | tf_op jit(solution)/shard_map/ppermute | solution.py:145
  36.8 1.5 %collective-permute-done.3.refs_3_ = f32[16,128]{1,0:T(8,128)S(1)} collective-permute-done((f32[16,128]{1,0:T(8,128)S(1)}, f32[16,128]{1,0:T(8,128)S(1)}, u32[]{:S(2)}, u32[]{:S(2)}) %collective-permute-start.3) | collective-permute-done | bytes 8224 | tf_op jit(solution)/shard_map/ppermute | solution.py:145
  38.3 3.8 %second.1 = (f32[8,128]{1,0:T(8,128)S(1)}, f32[8,128]{1,0:T(8,128)S(1)}, f32[8,128]{1,0:T(8,128)S(1)}, f32[8,128]{1,0:T(8,128)S(1)}, f32[8,128]{1,0:T(8,128)S(1)}) custom-call(s32[3]{0:T(128)S(1)} %pad_add_fusion.place_ref, s32[4,4]{1,0:T(4,128)S(1)} %copy-done.1, f32[2048,2048]{1,0:T(8,128)S(1)} %share.1.share_ref, f32[16,256]{1,0:T(8,128)S(1)} %bitcast.11, ...), custom_call_target="tpu_custom_call" | custom-call | tf_op jit(solution)/shard_map/second/pallas_call | solution.py:200
  42.1 0.1 collective-permute-start.4
  42.2 3.8 %collective-permute-start.5 = (f32[8,128]{1,0:T(8,128)S(1)}, f32[8,128]{1,0:T(8,128)S(1)}, u32[]{:S(2)}, u32[]{:S(2)}) collective-permute-start(f32[8,128]{1,0:T(8,128)S(1)} %get-tuple-element.10), channel_id=1, source_target_pairs={{0,8},{4,12},{8,0},{12,4},{1,9},{5,13},{9,1},{13,5},{2,10},{6,14},... | collective-permute-start | bytes 12296 | tf_op jit(solution)/shard_map/ppermute | solution.py:145
  46.0 0.5 collective-permute-start.6
  46.5 1.1 %collective-permute-done.5 = f32[8,128]{1,0:T(8,128)S(1)} collective-permute-done((f32[8,128]{1,0:T(8,128)S(1)}, f32[8,128]{1,0:T(8,128)S(1)}, u32[]{:S(2)}, u32[]{:S(2)}) %collective-permute-start.5) | collective-permute-done | bytes 4128 | tf_op jit(solution)/shard_map/ppermute | solution.py:145
  47.6 3.8 %collective-permute-done.6 = f32[8,128]{1,0:T(8,128)S(1)} collective-permute-done((f32[8,128]{1,0:T(8,128)S(1)}, f32[8,128]{1,0:T(8,128)S(1)}, u32[]{:S(2)}, u32[]{:S(2)}) %collective-permute-start.6) | collective-permute-done | bytes 4128 | tf_op jit(solution)/shard_map/ppermute | solution.py:145
  51.4 0.5 %subtract_bitcast_fusion = (f32[128]{0:T(128)}, f32[1,128]{1,0:T(1,128)S(1)}) fusion(f32[8,128]{1,0:T(8,128)S(1)} %collective-permute-done.6, f32[8,128]{1,0:T(8,128)S(1)} %collective-permute-done.5, f32[8,128]{1,0:T(8,128)S(1)} %collective-permute-done.4, f32[8,128]{1,0:T(8,128)S(1)} %get-tuple-element.8, f32[8,128]{1,0:T(8,128)S(1)} %get-tuple-element.7), kind=kLoop, calls=%fused_computation.3 | loop fusion | flops 1408 | bytes 7168 | tf_op jit(solution)/shard_map/sub | solution.py:216
  51.9 0.5 add_bitcast_fusion
  (7 shorter events, 0.0 us)
Async XLA Ops:
  0.6 15.3 %collective-permute-start = (bf16[128,2048]{1,0:T(8,128)(2,1)}, bf16[128,2048]{1,0:T(8,128)(2,1)S(1)}, u32[]{:S(2)}, u32[]{:S(2)}) collective-permute-start(bf16[128,2048]{1,0:T(8,128)(2,1)} %own_ref.1), channel_id=1, source_target_pairs={{0,1},{1,0},{2,3},{3,2},{4,5},{5,4},{6,7},{7,6},{8,9},{9,8},{10,11... | collective-permute-start | bytes 1572872 | tf_op jit(solution)/shard_map/ppermute | solution.py:166
  2.4 13.5 %all-to-all-start = ((f32[16,1,256]{2,1,0:T(1,128)}), f32[16,1,256]{2,1,0:T(1,128)S(1)}, u32[]{:S(2)}, u32[]{:S(2)}) async-start(f32[16,1,256]{2,1,0:T(1,128)} %broadcast_in_dim.2), calls=%async_computation | async-start | bytes 32768 | tf_op jit(solution)/shard_map/all_to_all | solution.py:165
  16.0 1.0 %copy-start = (bf16[128,2048]{1,0:T(8,128)(2,1)S(1)}, bf16[128,2048]{1,0:T(8,128)(2,1)}, u32[]{:S(2)}) copy-start(bf16[128,2048]{1,0:T(8,128)(2,1)} %own_ref.1) | copy-start | bytes 1572868
  17.0 0.7 %copy-start.1 = (s32[4,4]{1,0:T(4,128)S(1)}, s32[4,4]{1,0:T(4,128)}, u32[]{:S(2)}) copy-start(s32[4,4]{1,0:T(4,128)} %class_ref.5) | copy-start | bytes 196
  17.7 0.7 %copy-start.2 = (f32[2048]{0:T(1024)S(1)}, f32[2048]{0:T(1024)}, u32[]{:S(2)}) copy-start(f32[2048]{0:T(1024)} %param.8) | copy-start | bytes 24580
  31.7 4.5 %collective-permute-start.1 = (f32[16,128]{1,0:T(8,128)S(1)}, f32[16,128]{1,0:T(8,128)S(1)}, u32[]{:S(2)}, u32[]{:S(2)}) collective-permute-start(f32[16,128]{1,0:T(8,128)S(1)} %first.1.refs_0_), channel_id=1, source_target_pairs={{0,4},{4,0},{8,12},{12,8},{1,5},{5,1},{9,13},{13,9},{2,6},{6,2},{1... | collective-permute-start | bytes 24584 | tf_op jit(solution)/shard_map/ppermute | solution.py:145
  32.2 4.5 %collective-permute-start.2 = (f32[16,128]{1,0:T(8,128)S(1)}, f32[16,128]{1,0:T(8,128)S(1)}, u32[]{:S(2)}, u32[]{:S(2)}) collective-permute-start(f32[16,128]{1,0:T(8,128)S(1)} %first.1.refs_0_), channel_id=1, source_target_pairs={{0,8},{4,12},{8,0},{12,4},{1,9},{5,13},{9,1},{13,5},{2,10},{6,14},... | collective-permute-start | bytes 24584 | tf_op jit(solution)/shard_map/ppermute | solution.py:145
  32.8 5.4 %collective-permute-start.3 = (f32[16,128]{1,0:T(8,128)S(1)}, f32[16,128]{1,0:T(8,128)S(1)}, u32[]{:S(2)}, u32[]{:S(2)}) collective-permute-start(f32[16,128]{1,0:T(8,128)S(1)} %first.1.refs_0_), channel_id=1, source_target_pairs={{0,12},{4,8},{8,4},{12,0},{1,13},{5,9},{9,5},{13,1},{2,14},{6,10},... | collective-permute-start | bytes 24584 | tf_op jit(solution)/shard_map/ppermute | solution.py:145
  42.1 4.4 %collective-permute-start.4 = (f32[8,128]{1,0:T(8,128)S(1)}, f32[8,128]{1,0:T(8,128)S(1)}, u32[]{:S(2)}, u32[]{:S(2)}) collective-permute-start(f32[8,128]{1,0:T(8,128)S(1)} %get-tuple-element.9), channel_id=1, source_target_pairs={{0,4},{4,0},{8,12},{12,8},{1,5},{5,1},{9,13},{13,9},{2,6},{6,2},{1... | collective-permute-start | bytes 12296 | tf_op jit(solution)/shard_map/ppermute | solution.py:145
  42.2 5.4 %collective-permute-start.5 = (f32[8,128]{1,0:T(8,128)S(1)}, f32[8,128]{1,0:T(8,128)S(1)}, u32[]{:S(2)}, u32[]{:S(2)}) collective-permute-start(f32[8,128]{1,0:T(8,128)S(1)} %get-tuple-element.10), channel_id=1, source_target_pairs={{0,8},{4,12},{8,0},{12,4},{1,9},{5,13},{9,1},{13,5},{2,10},{6,14},... | collective-permute-start | bytes 12296 | tf_op jit(solution)/shard_map/ppermute | solution.py:145
  46.0 5.4 %collective-permute-start.6 = (f32[8,128]{1,0:T(8,128)S(1)}, f32[8,128]{1,0:T(8,128)S(1)}, u32[]{:S(2)}, u32[]{:S(2)}) collective-permute-start(f32[8,128]{1,0:T(8,128)S(1)} %get-tuple-element.11), channel_id=1, source_target_pairs={{0,12},{4,8},{8,4},{12,0},{1,13},{5,9},{9,5},{13,1},{2,14},{6,10},... | collective-permute-start | bytes 12296 | tf_op jit(solution)/shard_map/ppermute | solution.py:145

commit v2 on v1

--- a/solution.py
+++ b/solution.py
@@ -1,4 +1,5 @@
 import functools
+import math
 
 import jax
 import jax.numpy as jnp
@@ -12,100 +13,137 @@
 
 
 track_width = 0.0001
-
-
-def share_kernel(reach_tiles, inverse_members, class_ref, pos_ref, own_ref, mate_ref, share_ref, both, turned, column):
+exp2_rate = -math.log2(math.e) / track_width
+
+
+def for_each_pair(reach_tiles, class_ref, action):
     tiles = class_ref.shape[0]
-    members, total_obs = own_ref.shape
-    block_len = total_obs // tiles
-    both[:members, :] = own_ref[...]
-    both[members:, :] = mate_ref[...]
-    turned[:, :members] = own_ref[...].T
-    turned[:, members:] = mate_ref[...].T
-    for piece in range(total_obs // LANES):
-        at = piece * LANES
-        row = jnp.broadcast_to(pos_ref[:, at : at + LANES], (LANES, LANES))
-        column[at : at + LANES, :] = row.T
-    rows = 128
 
     def one_pair(pair, carry):
         a, b = pair // tiles, pair % tiles
-        klass = class_ref[a, b]
-
-        @pl.when(klass < reach_tiles)
-        def _():
-            weight = jnp.maximum(0.0, 1.0 - klass.astype(jnp.float32) / reach_tiles)
-            columns = pl.ds(pl.multiple_of(b * block_len, LANES), block_len)
-            right = both[:, columns]
-            right_pos = pos_ref[:, columns]
-
-            def one_chunk(chunk, carry):
-                at = pl.ds(pl.multiple_of(a * block_len + chunk * rows, rows), rows)
-                product = jnp.dot(turned[at, :], right, preferred_element_type=jnp.float32)
-                left_pos = jnp.concatenate([column[at, :]] * (block_len // LANES), axis=1)
-                distance = left_pos - right_pos
-                taper = weight * jnp.exp(-(distance * distance) * (1.0 / track_width))
-                share_ref[at, columns] = product * (taper * inverse_members)
-                return carry
-
-            lax.fori_loop(0, block_len // rows, one_chunk, 0)
-
+        pl.when(class_ref[a, b] < reach_tiles)(lambda: action(pair, a, b))
         return carry
 
     lax.fori_loop(0, tiles * tiles, one_pair, 0)
 
 
-def apply_share(reach_tiles, class_ref, share_ref, vector, sums, out_ref):
-    tiles = class_ref.shape[0]
+def tile_at(a, b, block_len):
+    top = pl.multiple_of(a * block_len, LANES)
+    left = pl.multiple_of(b * block_len, LANES)
+    return pl.ds(top, block_len), pl.ds(left, block_len)
+
+
+def pack_kernel(innovations_ref, obs_error_ref, packed_ref, row, arrived):
+    copies = [
+        pltpu.make_async_copy(ref, row.at[:, pl.ds(at * LANES, LANES)], arrived.at[at])
+        for at, ref in enumerate((innovations_ref, obs_error_ref))
+    ]
+    for copy in copies:
+        copy.start()
+    for copy in copies:
+        copy.wait()
+    packed_ref[...] = jnp.broadcast_to(row[...], packed_ref.shape)
+
+
+def share_kernel(reach_tiles, class_hbm, pos_hbm, own_ref, mate_ref, share_ref, *scratch):
+    class_ref, pos_ref, both, turned, column, tiles_here, arrived, left = scratch
+    members, total_obs = own_ref.shape
+    block_len = total_obs // class_ref.shape[0]
+    pos_copy = pltpu.make_async_copy(pos_hbm, pos_ref, arrived.at[0])
+    own_copy = pltpu.make_async_copy(own_ref, both.at[pl.ds(0, members), :], arrived.at[1])
+    class_copy = pltpu.make_async_copy(class_hbm, class_ref, arrived.at[2])
+    for copy in (pos_copy, own_copy, class_copy):
+        copy.start()
+    both[members:, :] = mate_ref[...]
+    turned[:, members:] = mate_ref[...].T
+    pos_copy.wait()
+    spread_columns(pos_ref[...], column)
+    own_copy.wait()
+    turned[:, :members] = both[:members, :].T
+    class_copy.wait()
+    rows = 128
+
+    def out_copy(pair, a, b):
+        at = tile_at(a, b, block_len)
+        return pltpu.make_async_copy(tiles_here.at[at], share_ref.at[at], left.at[pair])
+
+    def make_tile(pair, a, b):
+        at = tile_at(a, b, block_len)
+        right = both[:, at[1]]
+        right_pos = pos_ref[:, at[1]]
+        left_turned, left_column, tile = turned.at[at[0], :], column.at[at[0], :], tiles_here.at[at]
+        for begin in range(0, block_len, rows):
+            part = slice(begin, begin + rows)
+            product = jnp.dot(left_turned[part, :], right, preferred_element_type=jnp.float32)
+            left_pos = jnp.concatenate([left_column[part, :]] * (block_len // LANES), axis=1)
+            distance = left_pos - right_pos
+            tile[part, :] = product * jnp.exp2(distance * distance * exp2_rate)
+        out_copy(pair, a, b).start()
+
+    for_each_pair(reach_tiles, class_ref, make_tile)
+    for_each_pair(reach_tiles, class_ref, lambda *at: out_copy(*at).wait())
+
+
+def spread_columns(row, column):
+    for begin in range(0, column.shape[0], LANES):
+        square = jnp.broadcast_to(row[:, begin : begin + LANES], (LANES, LANES))
+        column[begin : begin + LANES, :] = square.T
+
+
+def apply_share(reach_tiles, inverse_members, class_ref, share_ref, vector, column, sums, out_ref, ready=None):
     total_obs = share_ref.shape[0]
-    block_len = total_obs // tiles
-    pieces = block_len // LANES
-    rows = 64
-
-    def add_tile(a, b, first):
-        def one_chunk(chunk, carry):
-            at = pl.ds(pl.multiple_of(a * block_len + chunk * rows, rows), rows)
-            total = None if first else sums[at, :]
-            for piece in range(pieces):
-                begin = b * block_len + piece * LANES
-                term = share_ref[at, begin : begin + LANES] * vector[b * pieces + piece : b * pieces + piece + 1, :]
-                total = term if total is None else total + term
-            sums[at, :] = total
-            return carry
-
-        lax.fori_loop(0, block_len // rows, one_chunk, 0)
-
-    for a in range(tiles):
-        add_tile(a, a, True)
-        for b in range(tiles):
-            if b != a:
-                pl.when(class_ref[a, b] < reach_tiles)(functools.partial(add_tile, a, b, False))
-    ones = jnp.ones((8, LANES), jnp.float32)
+    block_len = total_obs // class_ref.shape[0]
+    lanes = block_len // LANES
     for piece in range(total_obs // LANES):
-        folded = lax.dot_general(
-            ones,
-            sums[piece * LANES : (piece + 1) * LANES, :],
-            (((1,), (1,)), ((), ())),
-            precision=lax.Precision.HIGHEST,
-            preferred_element_type=jnp.float32,
-        )
-        out_ref[piece : piece + 1, :] = folded[0:1, :]
-
-
-def first_kernel(reach_tiles, class_ref, share_ref, vectors_ref, out_ref, vector, sums):
-    vector[...] = vectors_ref[:, :LANES]
-    apply_share(reach_tiles, class_ref, share_ref, vector, sums, out_ref)
+        square = jnp.broadcast_to(vector[piece : piece + 1, :], (LANES, LANES))
+        column[piece * LANES : (piece + 1) * LANES, :] = square.T
+    sums[...] = jnp.zeros_like(sums)
+
+    def add_tile(pair, a, b):
+        if ready is not None:
+            ready(pair, a, b)
+        weight = jnp.maximum(0.0, 1.0 - class_ref[a, b].astype(jnp.float32) / reach_tiles) * inverse_members
+        at = tile_at(a, b, block_len)
+        tile, factor = share_ref.at[at], column.at[at[0], :]
+        totals = [None] * lanes
+        for begin in range(0, block_len, 8):
+            part = slice(begin, begin + 8)
+            for lane in range(lanes):
+                term = tile[part, lane * LANES : (lane + 1) * LANES] * factor[part, :]
+                totals[lane] = term if totals[lane] is None else totals[lane] + term
+        into = sums.at[:, at[1]]
+        for lane in range(lanes):
+            into[:, lane * LANES : (lane + 1) * LANES] += weight * totals[lane]
+
+    for_each_pair(reach_tiles, class_ref, add_tile)
+    for piece in range(total_obs // LANES):
+        out_ref[piece : piece + 1, :] = jnp.sum(sums[:, piece * LANES : (piece + 1) * LANES], axis=0, keepdims=True)
+
+
+def first_kernel(
+    reach_tiles, inverse_members, class_ref, stored_ref, vectors_ref, share_ref, out_ref, vector, column, sums, arrived
+):
+    block_len = stored_ref.shape[0] // class_ref.shape[0]
+
+    def in_copy(pair, a, b):
+        at = tile_at(a, b, block_len)
+        return pltpu.make_async_copy(stored_ref.at[at], share_ref.at[at], arrived.at[pair])
+
+    for_each_pair(reach_tiles, class_ref, lambda *at: in_copy(*at).start())
+    vector[...] = vectors_ref[:, 0, :LANES]
+    ready = lambda *at: in_copy(*at).wait()
+    apply_share(reach_tiles, inverse_members, class_ref, share_ref, vector, column, sums, out_ref, ready)
 
 
 def total_of(x):
     return jnp.sum(jnp.sum(x, axis=0, keepdims=True), axis=1, keepdims=True)
 
 
-def second_kernel(reach_tiles, peers, place_ref, class_ref, share_ref, vectors_ref, *refs):
+def second_kernel(reach_tiles, inverse_members, peers, place_ref, class_ref, share_ref, vectors_ref, *refs):
     parts, refs = refs[:peers], refs[peers:]
     sent, refs = refs[:peers], refs[peers:]
-    state_ref, direction, residual, start, sums, product = refs
-    innovations, obs_error = vectors_ref[:, :LANES], vectors_ref[:, LANES:]
+    state_ref, direction, residual, start, column, sums, product = refs
+    innovations, obs_error = vectors_ref[:, 0, :LANES], vectors_ref[:, 0, LANES:]
     image = obs_error * innovations
     for part in parts:
         image = image + part[...]
@@ -117,7 +155,7 @@
     residual[...] = residual_now
     direction[...] = direction_now
     start[...] = alpha * innovations
-    apply_share(reach_tiles, class_ref, share_ref, direction, sums, product)
+    apply_share(reach_tiles, inverse_members, class_ref, share_ref, direction, column, sums, product)
     curvature = total_of(direction_now * product[...])
     extra = obs_error * direction_now
     own_curvature = total_of(direction_now * extra)
@@ -136,8 +174,24 @@
     state_ref[5:6, :] = jnp.broadcast_to(own_curvature, (1, LANES))
 
 
+def last_kernel(state_ref, *refs):
+    parts, (solution_ref, residual_ref) = refs[:-2], refs[-2:]
+    image, curvature = state_ref[3:4, :], state_ref[5:6, :]
+    for part in parts:
+        image = image + part[0:1, :]
+        curvature = curvature + part[1:2, :]
+    alpha = state_ref[4:5, :] / curvature
+    solution_ref[...] = state_ref[0:1, :] + alpha * state_ref[2:3, :]
+    residual_ref[...] = state_ref[1:2, :] - alpha * image
+
+
 VMEM_SPEC = pl.BlockSpec(memory_space=pltpu.VMEM)
 SMEM_SPEC = pl.BlockSpec(memory_space=pltpu.SMEM)
+HBM_SPEC = pl.BlockSpec(memory_space=pltpu.HBM)
+
+
+def in_hbm(x):
+    return pltpu.with_memory_space_constraint(x, pltpu.HBM)
 
 
 def swap_rows(x, mask):
@@ -160,60 +214,85 @@
     pieces = total_obs // LANES
     f32 = jnp.float32
 
-    packed = jnp.concatenate([innovations, obs_error]).reshape(1, 2 * LANES)
-    packed = jnp.broadcast_to(packed, (devices, 2 * LANES))
-    vectors = lax.all_to_all(packed, ("row", "col", "sub"), split_axis=0, concat_axis=0, tiled=True)
+    packed = pl.pallas_call(
+        pack_kernel,
+        out_shape=pltpu.VMEM((devices, 1, 2 * LANES), f32),
+        in_specs=[HBM_SPEC, HBM_SPEC],
+        out_specs=VMEM_SPEC,
+        scratch_shapes=[pltpu.VMEM((1, 2 * LANES), f32), pltpu.SemaphoreType.DMA((2,))],
+        compiler_params=pltpu.CompilerParams(vmem_limit_bytes=1024 * 1024),
+        name="pack",
+    )(in_hbm(innovations.reshape(1, LANES)), in_hbm(obs_error.reshape(1, LANES)))
     mate = lax.ppermute(anomalies, "sub", [(0, 1), (1, 0)])
 
-    params = pltpu.CompilerParams(vmem_limit_bytes=16 * 1024 * 1024)
+    pairs = row_count * row_count
     share = pl.pallas_call(
-        functools.partial(share_kernel, reach_tiles, inverse_members),
-        out_shape=pltpu.VMEM((total_obs, total_obs), f32),
-        in_specs=[SMEM_SPEC, VMEM_SPEC, VMEM_SPEC, VMEM_SPEC],
-        out_specs=VMEM_SPEC,
+        functools.partial(share_kernel, reach_tiles),
+        out_shape=jax.ShapeDtypeStruct((total_obs, total_obs), f32),
+        in_specs=[HBM_SPEC, HBM_SPEC, HBM_SPEC, VMEM_SPEC],
+        out_specs=HBM_SPEC,
         scratch_shapes=[
+            pltpu.SMEM(taper_class.shape, jnp.int32),
+            pltpu.VMEM((1, total_obs), f32),
             pltpu.VMEM((2 * local_members, total_obs), anomalies.dtype),
             pltpu.VMEM((total_obs, 2 * local_members), anomalies.dtype),
             pltpu.VMEM((total_obs, LANES), f32),
+            pltpu.VMEM((total_obs, total_obs), f32),
+            pltpu.SemaphoreType.DMA((3,)),
+            pltpu.SemaphoreType.DMA((pairs,)),
         ],
-        compiler_params=params,
+        compiler_params=pltpu.CompilerParams(vmem_limit_bytes=40 * 1024 * 1024),
         cost_estimate=pl.CostEstimate(
             flops=4 * local_members * total_obs * total_obs,
-            bytes_accessed=4 * local_members * total_obs,
+            bytes_accessed=4 * total_obs * total_obs,
             transcendentals=total_obs * total_obs,
         ),
         name="share",
-    )(taper_class, track_pos.reshape(1, total_obs), anomalies, mate)
-
-    part = pl.pallas_call(
-        functools.partial(first_kernel, reach_tiles),
-        out_shape=pltpu.VMEM((pieces, LANES), f32),
-        in_specs=[SMEM_SPEC, VMEM_SPEC, VMEM_SPEC],
-        out_specs=VMEM_SPEC,
-        scratch_shapes=[pltpu.VMEM((pieces, LANES), f32), pltpu.VMEM((total_obs, LANES), f32)],
+    )(in_hbm(taper_class), in_hbm(track_pos.reshape(1, total_obs)), in_hbm(anomalies), mate)
+    vectors = lax.all_to_all(packed, ("row", "col", "sub"), split_axis=0, concat_axis=0, tiled=True)
+
+    params = pltpu.CompilerParams(vmem_limit_bytes=8 * 1024 * 1024)
+    share, part = pl.pallas_call(
+        functools.partial(first_kernel, reach_tiles, inverse_members),
+        out_shape=[pltpu.VMEM((total_obs, total_obs), f32), pltpu.VMEM((pieces, LANES), f32)],
+        in_specs=[SMEM_SPEC, HBM_SPEC, VMEM_SPEC],
+        out_specs=[VMEM_SPEC, VMEM_SPEC],
+        scratch_shapes=[
+            pltpu.VMEM((pieces, LANES), f32),
+            pltpu.VMEM((total_obs, LANES), f32),
+            pltpu.VMEM((8, total_obs), f32),
+            pltpu.SemaphoreType.DMA((pairs,)),
+        ],
         compiler_params=params,
         name="first",
-    )(taper_class, share, vectors)
+    )(taper_class, in_hbm(share), vectors)
     parts = [part] + [swap_rows(part, mask) for mask in range(1, row_count)]
 
     place = jnp.stack([row_index, within, jnp.int32(per_row)]).astype(jnp.int32)
     *sent, state = pl.pallas_call(
-        functools.partial(second_kernel, reach_tiles, row_count),
+        functools.partial(second_kernel, reach_tiles, inverse_members, row_count),
         out_shape=[pltpu.VMEM((8, LANES), f32) for _ in range(row_count + 1)],
         in_specs=[SMEM_SPEC, SMEM_SPEC, VMEM_SPEC, VMEM_SPEC] + [VMEM_SPEC] * row_count,
         out_specs=[VMEM_SPEC] * (row_count + 1),
         scratch_shapes=[pltpu.VMEM((pieces, LANES), f32)] * 3
-        + [pltpu.VMEM((total_obs, LANES), f32), pltpu.VMEM((pieces, LANES), f32)],
+        + [
+            pltpu.VMEM((total_obs, LANES), f32),
+            pltpu.VMEM((8, total_obs), f32),
+            pltpu.VMEM((pieces, LANES), f32),
+        ],
         compiler_params=params,
         name="second",
     )(place, taper_class, share, vectors, *parts)
     got = [sent[0]] + [swap_rows(sent[mask], mask) for mask in range(1, row_count)]
-    image, curvature = state[3], state[5]
-    for piece in got:
-        image = image + piece[0]
-        curvature = curvature + piece[1]
-    alpha = state[4] / curvature
-    return state[0] + alpha * state[2], state[1] - alpha * image
+    solution_part, residual_part = pl.pallas_call(
+        last_kernel,
+        out_shape=[jax.ShapeDtypeStruct((1, LANES), f32)] * 2,
+        in_specs=[VMEM_SPEC] * (row_count + 1),
+        out_specs=[VMEM_SPEC] * 2,
+        compiler_params=pltpu.CompilerParams(vmem_limit_bytes=1024 * 1024),
+        name="last",
+    )(state, *got)
+    return solution_part.reshape(LANES), residual_part.reshape(LANES)
 
 
 def fits(anomalies, innovations, obs_error, track_pos, taper_class):

time: 52.8 us -> 40 us (0.76)
  waiting for transfers between devices: 13.4 us -> 6.94 us
  local copies, waits for them, and re-layouts: 3.04 us -> 0.01 us
  other arithmetic: 1.79 us -> 0.08 us
  Pallas kernels: 17.2 us -> 15.6 us
    all_to_all x1, waiting for transfers between devices: 6.49 us -> 0.46 us  [vectors_only(): lax.all_to_all(packed, ('row', 'col', 'sub'), split_axis=0, concat_axis=0...]
    unnamed x7 -> x2, local copies, waits for them, and re-layouts: 2.42 us -> 0.01 us
    pallas_call x3 -> x5, Pallas kernels: 17.2 us -> 15.6 us  [the longest x1 6.01 us: vectors_only(): pl.pallas_call(functools.partial(share_kernel, reach_tiles), out_shape=ja...]
    concatenate x1 -> x0, other arithmetic: 0.68 us -> none  [vectors_only(): packed = jnp.concatenate([innovations, obs_error]).reshape(1, 2 * LANES)]
    broadcast_in_dim x1 -> x0, local copies, waits for them, and re-layouts: 0.62 us -> none  [vectors_only(): packed = jnp.broadcast_to(packed, (devices, 2 * LANES))]
  transfers between devices with their start and end apart: 8 -> 8, of which waited for: 5 -> 5; matrix products, arithmetic and copies ran while one was open for 3% -> 0% of each run, Pallas kernels for 0% -> 18%
where the time goes in v2:
time: 40 us; the launch traced here: 39.8 us
  starting transfers between devices  16.4 us (41%)
  Pallas kernels  15.6 us (39%)
  waiting for transfers between devices  6.94 us (17%)
  between operations  0.69 us (2%)
    ppermute x6, starting transfers between devices, swap_rows(): return lax.ppermute(x, 'row', [(i, i ^ mask) for i in range(row_count)])  8.84 us
    all_to_all x1, starting transfers between devices, vectors_only(): lax.all_to_all(packed, ('row', 'col', 'sub'), split_axis=0, concat_axis=0...  7.03 us
    ppermute x6, waiting for transfers between devices, swap_rows(): return lax.ppermute(x, 'row', [(i, i ^ mask) for i in range(row_count)])  6.48 us
    pallas_call x1, Pallas kernels, vectors_only(): pl.pallas_call(functools.partial(share_kernel, reach_tiles), out_shape=ja...  6.01 us
    pallas_call x1, Pallas kernels, vectors_only(): pl.pallas_call(functools.partial(first_kernel, reach_tiles, inverse_membe...  4.97 us
    pallas_call x1, Pallas kernels, vectors_only(): pl.pallas_call(functools.partial(second_kernel, reach_tiles, inverse_memb...  2.85 us
    pallas_call x1, Pallas kernels, vectors_only(): pl.pallas_call(pack_kernel, out_shape=pltpu.VMEM((devices, 1, 2 * LANES),...  1.29 us
  transfers between devices with their start and end apart: 8, of which 5 were waited for; matrix products, arithmetic and copies ran while one was open for 0% of the time, Pallas kernels for 18%

profile of v2, /device:TPU:0, one launch (start us, length us, event | category | flops | bytes accessed | tf_op | source)
XLA Modules:
  0.0 39.8 jit_solution(4458381262951076608)
XLA Ops:
  0.6 0.0 copy-start
  0.6 0.5 %collective-permute-start = (bf16[128,2048]{1,0:T(8,128)(2,1)}, bf16[128,2048]{1,0:T(8,128)(2,1)S(1)}, u32[]{:S(2)}, u32[]{:S(2)}) collective-permute-start(bf16[128,2048]{1,0:T(8,128)(2,1)} %own_ref.1), channel_id=1, source_target_pairs={{0,1},{1,0},{2,3},{3,2},{4,5},{5,4},{6,7},{7,6},{8,9},{9,8},{10,11... | collective-permute-start | bytes 1572872 | tf_op jit(solution)/shard_map/ppermute | solution.py:226
  1.2 1.3 %pack.1 = f32[16,1,256]{2,1,0:T(1,128)} custom-call(f32[1,128]{1,0:T(1,128)} %bitcast.8, f32[1,128]{1,0:T(1,128)} %bitcast.9), custom_call_target="tpu_custom_call" | custom-call | tf_op jit(solution)/shard_map/pack/pallas_call | solution.py:217
  2.5 7.0 %all-to-all-start = ((f32[16,1,256]{2,1,0:T(1,128)}), f32[16,1,256]{2,1,0:T(1,128)S(1)}, u32[]{:S(2)}, u32[]{:S(2)}) async-start(f32[16,1,256]{2,1,0:T(1,128)} %pack.1), calls=%async_computation | async-start | bytes 32768 | tf_op jit(solution)/shard_map/all_to_all | solution.py:252
  9.5 0.0 collective-permute-done.mate_ref
  9.5 6.0 %share.1.stored_ref = f32[2048,2048]{1,0:T(8,128)} custom-call(s32[4,4]{1,0:T(4,128)} %class_ref.3, f32[1,2048]{1,0:T(1,128)} %bitcast.7, bf16[128,2048]{1,0:T(8,128)(2,1)} %own_ref.1, bf16[128,2048]{1,0:T(8,128)(2,1)S(1)} %collective-permute-done.mate_ref), custom_call_target="tpu_custom_call" | custom-call | flops 2147483648 | bytes 16777216 | tf_op jit(solution)/shard_map/share/pallas_call | solution.py:229
  15.5 0.5 %all-to-all-done.vectors_ref = f32[16,1,256]{2,1,0:T(1,128)S(1)} async-done(((f32[16,1,256]{2,1,0:T(1,128)}), f32[16,1,256]{2,1,0:T(1,128)S(1)}, u32[]{:S(2)}, u32[]{:S(2)}) %all-to-all-start) | async-done | bytes 16416 | tf_op jit(solution)/shard_map/all_to_all | solution.py:252
  16.0 0.0 copy-done
  16.0 5.0 %first.1 = (f32[2048,2048]{1,0:T(8,128)S(1)}, f32[16,128]{1,0:T(8,128)S(1)}) custom-call(s32[4,4]{1,0:T(4,128)S(1)} %copy-done, f32[2048,2048]{1,0:T(8,128)} %share.1.stored_ref, f32[16,1,256]{2,1,0:T(1,128)S(1)} %all-to-all-done.vectors_ref), custom_call_target="tpu_custom_call" | custom-call | tf_op jit(solution)/shard_map/first/pallas_call | solution.py:255
  21.0 3.3 %collective-permute-start.3 = (f32[16,128]{1,0:T(8,128)S(1)}, f32[16,128]{1,0:T(8,128)S(1)}, u32[]{:S(2)}, u32[]{:S(2)}) collective-permute-start(f32[16,128]{1,0:T(8,128)S(1)} %get-tuple-element.12.refs_0_), channel_id=1, source_target_pairs={{0,12},{4,8},{8,4},{12,0},{1,13},{5,9},{9,5},{13,1},{2,14},{6,10},... | collective-permute-start | bytes 24584 | tf_op jit(solution)/shard_map/ppermute | solution.py:199
  24.3 0.0 collective-permute-start.2
  24.3 1.1 %collective-permute-start.1 = (f32[16,128]{1,0:T(8,128)S(1)}, f32[16,128]{1,0:T(8,128)S(1)}, u32[]{:S(2)}, u32[]{:S(2)}) collective-permute-start(f32[16,128]{1,0:T(8,128)S(1)} %get-tuple-element.12.refs_0_), channel_id=1, source_target_pairs={{0,4},{4,0},{8,12},{12,8},{1,5},{5,1},{9,13},{13,9},{2,6},{6,2},{1... | collective-permute-start | bytes 24584 | tf_op jit(solution)/shard_map/ppermute | solution.py:199
  25.4 0.1 pad_add_fusion.place_ref
  25.5 1.0 %collective-permute-done.3.refs_3_ = f32[16,128]{1,0:T(8,128)S(1)} collective-permute-done((f32[16,128]{1,0:T(8,128)S(1)}, f32[16,128]{1,0:T(8,128)S(1)}, u32[]{:S(2)}, u32[]{:S(2)}) %collective-permute-start.3) | collective-permute-done | bytes 8224 | tf_op jit(solution)/shard_map/ppermute | solution.py:199
  26.5 2.4 %collective-permute-done.2.refs_2_ = f32[16,128]{1,0:T(8,128)S(1)} collective-permute-done((f32[16,128]{1,0:T(8,128)S(1)}, f32[16,128]{1,0:T(8,128)S(1)}, u32[]{:S(2)}, u32[]{:S(2)}) %collective-permute-start.2) | collective-permute-done | bytes 8224 | tf_op jit(solution)/shard_map/ppermute | solution.py:199
  28.9 0.0 collective-permute-done.1.refs_1_
  28.9 2.9 %second.1 = (f32[8,128]{1,0:T(8,128)S(1)}, f32[8,128]{1,0:T(8,128)S(1)}, f32[8,128]{1,0:T(8,128)S(1)}, f32[8,128]{1,0:T(8,128)S(1)}, f32[8,128]{1,0:T(8,128)S(1)}) custom-call(s32[3]{0:T(128)S(1)} %pad_add_fusion.place_ref, s32[4,4]{1,0:T(4,128)S(1)} %copy-done, f32[2048,2048]{1,0:T(8,128)S(1)} %get-tuple-element.11.share_ref, ...), custom_call_target="tpu_custom_call" | custom-call | tf_op jit(solution)/shard_map/second/pallas_call | solution.py:272
  31.7 0.2 collective-permute-start.4
  31.9 1.9 %collective-permute-start.5 = (f32[8,128]{1,0:T(8,128)S(1)}, f32[8,128]{1,0:T(8,128)S(1)}, u32[]{:S(2)}, u32[]{:S(2)}) collective-permute-start(f32[8,128]{1,0:T(8,128)S(1)} %get-tuple-element.16), channel_id=1, source_target_pairs={{0,8},{4,12},{8,0},{12,4},{1,9},{5,13},{9,1},{13,5},{2,10},{6,14},... | collective-permute-start | bytes 12296 | tf_op jit(solution)/shard_map/ppermute | solution.py:199
  33.8 2.3 %collective-permute-start.6 = (f32[8,128]{1,0:T(8,128)S(1)}, f32[8,128]{1,0:T(8,128)S(1)}, u32[]{:S(2)}, u32[]{:S(2)}) collective-permute-start(f32[8,128]{1,0:T(8,128)S(1)} %get-tuple-element.17), channel_id=1, source_target_pairs={{0,12},{4,8},{8,4},{12,0},{1,13},{5,9},{9,5},{13,1},{2,14},{6,10},... | collective-permute-start | bytes 12296 | tf_op jit(solution)/shard_map/ppermute | solution.py:199
  36.1 0.0 collective-permute-done.4.refs_1_
  36.1 0.3 collective-permute-done.5.refs_2_
  36.4 2.8 %collective-permute-done.6.refs_3_ = f32[8,128]{1,0:T(8,128)S(1)} collective-permute-done((f32[8,128]{1,0:T(8,128)S(1)}, f32[8,128]{1,0:T(8,128)S(1)}, u32[]{:S(2)}, u32[]{:S(2)}) %collective-permute-start.6) | collective-permute-done | bytes 4128 | tf_op jit(solution)/shard_map/ppermute | solution.py:199
  39.2 0.5 %last.1 = (f32[1,128]{1,0:T(1,128)}, f32[1,128]{1,0:T(1,128)}) custom-call(f32[8,128]{1,0:T(8,128)S(1)} %get-tuple-element.13.state_ref, f32[8,128]{1,0:T(8,128)S(1)} %get-tuple-element.14.refs_0_, f32[8,128]{1,0:T(8,128)S(1)} %collective-permute-done.4.refs_1_, f32[8,128]{1,0:T(8,128)S(1)} %collective-permute-done.5.refs_2_, ...), custom_call_target="tpu_custom_call" | custom-call | tf_op jit(solution)/shard_map/last/pallas_call | solution.py:287
Async XLA Ops:
  0.6 15.4 %copy-start = (s32[4,4]{1,0:T(4,128)S(1)}, s32[4,4]{1,0:T(4,128)}, u32[]{:S(2)}) copy-start(s32[4,4]{1,0:T(4,128)} %class_ref.3) | copy-start | bytes 196
  0.6 8.9 %collective-permute-start = (bf16[128,2048]{1,0:T(8,128)(2,1)}, bf16[128,2048]{1,0:T(8,128)(2,1)S(1)}, u32[]{:S(2)}, u32[]{:S(2)}) collective-permute-start(bf16[128,2048]{1,0:T(8,128)(2,1)} %own_ref.1), channel_id=1, source_target_pairs={{0,1},{1,0},{2,3},{3,2},{4,5},{5,4},{6,7},{7,6},{8,9},{9,8},{10,11... | collective-permute-start | bytes 1572872 | tf_op jit(solution)/shard_map/ppermute | solution.py:226
  2.5 13.5 %all-to-all-start = ((f32[16,1,256]{2,1,0:T(1,128)}), f32[16,1,256]{2,1,0:T(1,128)S(1)}, u32[]{:S(2)}, u32[]{:S(2)}) async-start(f32[16,1,256]{2,1,0:T(1,128)} %pack.1), calls=%async_computation | async-start | bytes 32768 | tf_op jit(solution)/shard_map/all_to_all | solution.py:252
  21.0 5.5 %collective-permute-start.3 = (f32[16,128]{1,0:T(8,128)S(1)}, f32[16,128]{1,0:T(8,128)S(1)}, u32[]{:S(2)}, u32[]{:S(2)}) collective-permute-start(f32[16,128]{1,0:T(8,128)S(1)} %get-tuple-element.12.refs_0_), channel_id=1, source_target_pairs={{0,12},{4,8},{8,4},{12,0},{1,13},{5,9},{9,5},{13,1},{2,14},{6,10},... | collective-permute-start | bytes 24584 | tf_op jit(solution)/shard_map/ppermute | solution.py:199
  24.3 4.5 %collective-permute-start.2 = (f32[16,128]{1,0:T(8,128)S(1)}, f32[16,128]{1,0:T(8,128)S(1)}, u32[]{:S(2)}, u32[]{:S(2)}) collective-permute-start(f32[16,128]{1,0:T(8,128)S(1)} %get-tuple-element.12.refs_0_), channel_id=1, source_target_pairs={{0,8},{4,12},{8,0},{12,4},{1,9},{5,13},{9,1},{13,5},{2,10},{6,14},... | collective-permute-start | bytes 24584 | tf_op jit(solution)/shard_map/ppermute | solution.py:199
  24.3 4.5 %collective-permute-start.1 = (f32[16,128]{1,0:T(8,128)S(1)}, f32[16,128]{1,0:T(8,128)S(1)}, u32[]{:S(2)}, u32[]{:S(2)}) collective-permute-start(f32[16,128]{1,0:T(8,128)S(1)} %get-tuple-element.12.refs_0_), channel_id=1, source_target_pairs={{0,4},{4,0},{8,12},{12,8},{1,5},{5,1},{9,13},{13,9},{2,6},{6,2},{1... | collective-permute-start | bytes 24584 | tf_op jit(solution)/shard_map/ppermute | solution.py:199
  31.7 4.4 %collective-permute-start.4 = (f32[8,128]{1,0:T(8,128)S(1)}, f32[8,128]{1,0:T(8,128)S(1)}, u32[]{:S(2)}, u32[]{:S(2)}) collective-permute-start(f32[8,128]{1,0:T(8,128)S(1)} %get-tuple-element.15), channel_id=1, source_target_pairs={{0,4},{4,0},{8,12},{12,8},{1,5},{5,1},{9,13},{13,9},{2,6},{6,2},{1... | collective-permute-start | bytes 12296 | tf_op jit(solution)/shard_map/ppermute | solution.py:199
  31.9 4.5 %collective-permute-start.5 = (f32[8,128]{1,0:T(8,128)S(1)}, f32[8,128]{1,0:T(8,128)S(1)}, u32[]{:S(2)}, u32[]{:S(2)}) collective-permute-start(f32[8,128]{1,0:T(8,128)S(1)} %get-tuple-element.16), channel_id=1, source_target_pairs={{0,8},{4,12},{8,0},{12,4},{1,9},{5,13},{9,1},{13,5},{2,10},{6,14},... | collective-permute-start | bytes 12296 | tf_op jit(solution)/shard_map/ppermute | solution.py:199
  33.8 5.4 %collective-permute-start.6 = (f32[8,128]{1,0:T(8,128)S(1)}, f32[8,128]{1,0:T(8,128)S(1)}, u32[]{:S(2)}, u32[]{:S(2)}) collective-permute-start(f32[8,128]{1,0:T(8,128)S(1)} %get-tuple-element.17), channel_id=1, source_target_pairs={{0,12},{4,8},{8,4},{12,0},{1,13},{5,9},{9,5},{13,1},{2,14},{6,10},... | collective-permute-start | bytes 12296 | tf_op jit(solution)/shard_map/ppermute | solution.py:199

commit v3 on v2

--- a/solution.py
+++ b/solution.py
@@ -10,27 +10,31 @@
 
 ITERS = 2
 LANES = 128
+KEPT_BYTES = 3 * 1024 * 1024
 
 
 track_width = 0.0001
 exp2_rate = -math.log2(math.e) / track_width
 
 
+def off_diagonal(tiles):
+    return tiles * (tiles - 1) // 2
+
+
 def for_each_pair(reach_tiles, class_ref, action):
     tiles = class_ref.shape[0]
 
     def one_pair(pair, carry):
         a, b = pair // tiles, pair % tiles
-        pl.when(class_ref[a, b] < reach_tiles)(lambda: action(pair, a, b))
+        slot = a * tiles - (a * (a + 1)) // 2 + b - a - 1
+        pl.when(jnp.logical_and(a < b, class_ref[a, b] < reach_tiles))(lambda: action(slot, a, b))
         return carry
 
     lax.fori_loop(0, tiles * tiles, one_pair, 0)
 
 
-def tile_at(a, b, block_len):
-    top = pl.multiple_of(a * block_len, LANES)
-    left = pl.multiple_of(b * block_len, LANES)
-    return pl.ds(top, block_len), pl.ds(left, block_len)
+def block_at(a, block_len):
+    return pl.ds(pl.multiple_of(a * block_len, LANES), block_len)
 
 
 def pack_kernel(innovations_ref, obs_error_ref, packed_ref, row, arrived):
@@ -45,43 +49,62 @@
     packed_ref[...] = jnp.broadcast_to(row[...], packed_ref.shape)
 
 
-def share_kernel(reach_tiles, class_hbm, pos_hbm, own_ref, mate_ref, share_ref, *scratch):
-    class_ref, pos_ref, both, turned, column, tiles_here, arrived, left = scratch
+def share_kernel(reach_tiles, class_hbm, pos_hbm, own_ref, mate_ref, kept_ref, stored_ref, *scratch):
+    class_ref, pos_ref, both, turned, column, made, arrived, left = scratch
     members, total_obs = own_ref.shape
-    block_len = total_obs // class_ref.shape[0]
+    tiles = class_ref.shape[0]
+    block_len = total_obs // tiles
+    kept = kept_ref.shape[0]
     pos_copy = pltpu.make_async_copy(pos_hbm, pos_ref, arrived.at[0])
     own_copy = pltpu.make_async_copy(own_ref, both.at[pl.ds(0, members), :], arrived.at[1])
     class_copy = pltpu.make_async_copy(class_hbm, class_ref, arrived.at[2])
-    for copy in (pos_copy, own_copy, class_copy):
+    mate_copy = pltpu.make_async_copy(mate_ref, both.at[pl.ds(members, members), :], arrived.at[3])
+    for copy in (pos_copy, own_copy, mate_copy, class_copy):
         copy.start()
-    both[members:, :] = mate_ref[...]
-    turned[:, members:] = mate_ref[...].T
     pos_copy.wait()
     spread_columns(pos_ref[...], column)
     own_copy.wait()
     turned[:, :members] = both[:members, :].T
+    mate_copy.wait()
+    turned[:, members:] = both[members:, :].T
     class_copy.wait()
     rows = 128
 
-    def out_copy(pair, a, b):
-        at = tile_at(a, b, block_len)
-        return pltpu.make_async_copy(tiles_here.at[at], share_ref.at[at], left.at[pair])
-
-    def make_tile(pair, a, b):
-        at = tile_at(a, b, block_len)
-        right = both[:, at[1]]
-        right_pos = pos_ref[:, at[1]]
-        left_turned, left_column, tile = turned.at[at[0], :], column.at[at[0], :], tiles_here.at[at]
+    def out_copy(slot):
+        return pltpu.make_async_copy(made.at[slot], stored_ref.at[slot], left.at[slot])
+
+    def make_tile(tile, a, b):
+        rows_at, columns_at = block_at(a, block_len), block_at(b, block_len)
+        right = both[:, columns_at]
+        right_pos = pos_ref[:, columns_at]
+        left_turned, left_column = turned.at[rows_at, :], column.at[rows_at, :]
         for begin in range(0, block_len, rows):
             part = slice(begin, begin + rows)
             product = jnp.dot(left_turned[part, :], right, preferred_element_type=jnp.float32)
             left_pos = jnp.concatenate([left_column[part, :]] * (block_len // LANES), axis=1)
             distance = left_pos - right_pos
             tile[part, :] = product * jnp.exp2(distance * distance * exp2_rate)
-        out_copy(pair, a, b).start()
-
-    for_each_pair(reach_tiles, class_ref, make_tile)
-    for_each_pair(reach_tiles, class_ref, lambda *at: out_copy(*at).wait())
+
+    def make_pair(slot, a, b):
+        slot = slot + tiles - kept
+        make_tile(made.at[slot], a, b)
+        out_copy(slot).start()
+
+    def make_stored(slot, carry):
+        make_tile(made.at[slot], slot + kept, slot + kept)
+        out_copy(slot).start()
+        return carry
+
+    def make_kept(slot, carry):
+        make_tile(kept_ref.at[slot], slot, slot)
+        return carry
+
+    for_each_pair(reach_tiles, class_ref, make_pair)
+    lax.fori_loop(0, tiles - kept, make_stored, 0)
+    lax.fori_loop(0, kept, make_kept, 0)
+    for_each_pair(reach_tiles, class_ref, lambda slot, a, b: out_copy(slot + tiles - kept).wait())
+    for slot in range(tiles - kept):
+        out_copy(slot).wait()
 
 
 def spread_columns(row, column):
@@ -90,59 +113,105 @@
         column[begin : begin + LANES, :] = square.T
 
 
-def apply_share(reach_tiles, inverse_members, class_ref, share_ref, vector, column, sums, out_ref, ready=None):
-    total_obs = share_ref.shape[0]
-    block_len = total_obs // class_ref.shape[0]
+def apply_share(
+    reach_tiles, inverse_members, class_ref, kept_ref, stored_ref, vector, column, across, sums, out_ref, ready=None
+):
+    tiles = class_ref.shape[0]
+    kept = kept_ref.shape[0]
+    block_len = kept_ref.shape[1]
     lanes = block_len // LANES
-    for piece in range(total_obs // LANES):
+    for piece in range(tiles * lanes):
         square = jnp.broadcast_to(vector[piece : piece + 1, :], (LANES, LANES))
         column[piece * LANES : (piece + 1) * LANES, :] = square.T
     sums[...] = jnp.zeros_like(sums)
 
-    def add_tile(pair, a, b):
-        if ready is not None:
-            ready(pair, a, b)
-        weight = jnp.maximum(0.0, 1.0 - class_ref[a, b].astype(jnp.float32) / reach_tiles) * inverse_members
-        at = tile_at(a, b, block_len)
-        tile, factor = share_ref.at[at], column.at[at[0], :]
+    def add_diagonal(tile, a):
+        at = block_at(a, block_len)
+        factor = column.at[at, :]
         totals = [None] * lanes
         for begin in range(0, block_len, 8):
             part = slice(begin, begin + 8)
             for lane in range(lanes):
                 term = tile[part, lane * LANES : (lane + 1) * LANES] * factor[part, :]
                 totals[lane] = term if totals[lane] is None else totals[lane] + term
-        into = sums.at[:, at[1]]
+        into = sums.at[:, at]
         for lane in range(lanes):
-            into[:, lane * LANES : (lane + 1) * LANES] += weight * totals[lane]
-
-    for_each_pair(reach_tiles, class_ref, add_tile)
-    for piece in range(total_obs // LANES):
+            into[:, lane * LANES : (lane + 1) * LANES] += tile_weight(class_ref[a, a]) * totals[lane]
+
+    def tile_weight(klass):
+        return jnp.maximum(0.0, 1.0 - klass.astype(jnp.float32) / reach_tiles) * inverse_members
+
+    def add_pair(slot, a, b):
+        slot = slot + tiles - kept
+        if ready is not None:
+            ready(slot)
+        weight = tile_weight(class_ref[a, b])
+        at_a, at_b = block_at(a, block_len), block_at(b, block_len)
+        tile, factor = stored_ref.at[slot], column.at[at_a, :]
+        rows_b = [jnp.broadcast_to(vector[pl.ds(b * lanes + lane, 1), :], (8, LANES)) for lane in range(lanes)]
+        totals = [None] * lanes
+        for begin in range(0, block_len, 8):
+            part = slice(begin, begin + 8)
+            line = None
+            for lane in range(lanes):
+                here = tile[part, lane * LANES : (lane + 1) * LANES]
+                term = here * factor[part, :]
+                totals[lane] = term if totals[lane] is None else totals[lane] + term
+                term = here * rows_b[lane]
+                line = term if line is None else line + term
+            across[part, :] = line
+        into_a, into_b = sums.at[:, at_a], sums.at[:, at_b]
+        for lane in range(lanes):
+            where = slice(lane * LANES, (lane + 1) * LANES)
+            into_b[:, where] += weight * totals[lane]
+            turned = across[where, :].T
+            folded = turned[:8, :]
+            for begin in range(8, LANES, 8):
+                folded = folded + turned[begin : begin + 8, :]
+            into_a[:, where] += weight * folded
+
+    def one_kept(slot, carry):
+        add_diagonal(kept_ref.at[slot], slot)
+        return carry
+
+    def one_stored(slot, carry):
+        if ready is not None:
+            ready(slot)
+        add_diagonal(stored_ref.at[slot], slot + kept)
+        return carry
+
+    lax.fori_loop(0, kept, one_kept, 0)
+    lax.fori_loop(0, tiles - kept, one_stored, 0)
+    for_each_pair(reach_tiles, class_ref, add_pair)
+    for piece in range(tiles * lanes):
         out_ref[piece : piece + 1, :] = jnp.sum(sums[:, piece * LANES : (piece + 1) * LANES], axis=0, keepdims=True)
 
 
-def first_kernel(
-    reach_tiles, inverse_members, class_ref, stored_ref, vectors_ref, share_ref, out_ref, vector, column, sums, arrived
-):
-    block_len = stored_ref.shape[0] // class_ref.shape[0]
-
-    def in_copy(pair, a, b):
-        at = tile_at(a, b, block_len)
-        return pltpu.make_async_copy(stored_ref.at[at], share_ref.at[at], arrived.at[pair])
-
-    for_each_pair(reach_tiles, class_ref, lambda *at: in_copy(*at).start())
+def first_kernel(reach_tiles, inverse_members, class_ref, kept_ref, hbm_ref, vectors_ref, stored_ref, out_ref, *scratch):
+    vector, column, across, sums, arrived = scratch
+    tiles = class_ref.shape[0]
+    kept = kept_ref.shape[0]
+
+    def in_copy(slot):
+        return pltpu.make_async_copy(hbm_ref.at[slot], stored_ref.at[slot], arrived.at[slot])
+
+    for slot in range(tiles - kept):
+        in_copy(slot).start()
+    for_each_pair(reach_tiles, class_ref, lambda slot, a, b: in_copy(slot + tiles - kept).start())
     vector[...] = vectors_ref[:, 0, :LANES]
-    ready = lambda *at: in_copy(*at).wait()
-    apply_share(reach_tiles, inverse_members, class_ref, share_ref, vector, column, sums, out_ref, ready)
+    ready = lambda slot: in_copy(slot).wait()
+    refs = (class_ref, kept_ref, stored_ref, vector, column, across, sums, out_ref)
+    apply_share(reach_tiles, inverse_members, *refs, ready)
 
 
 def total_of(x):
     return jnp.sum(jnp.sum(x, axis=0, keepdims=True), axis=1, keepdims=True)
 
 
-def second_kernel(reach_tiles, inverse_members, peers, place_ref, class_ref, share_ref, vectors_ref, *refs):
-    parts, refs = refs[:peers], refs[peers:]
+def second_kernel(reach_tiles, inverse_members, peers, place_ref, class_ref, kept_ref, stored_ref, *refs):
+    vectors_ref, parts, refs = refs[0], refs[1 : peers + 1], refs[peers + 1 :]
     sent, refs = refs[:peers], refs[peers:]
-    state_ref, direction, residual, start, column, sums, product = refs
+    state_ref, direction, residual, start, column, across, sums, product = refs
     innovations, obs_error = vectors_ref[:, 0, :LANES], vectors_ref[:, 0, LANES:]
     image = obs_error * innovations
     for part in parts:
@@ -155,7 +224,8 @@
     residual[...] = residual_now
     direction[...] = direction_now
     start[...] = alpha * innovations
-    apply_share(reach_tiles, inverse_members, class_ref, share_ref, direction, column, sums, product)
+    shared = (class_ref, kept_ref, stored_ref, direction, column, across, sums, product)
+    apply_share(reach_tiles, inverse_members, *shared)
     curvature = total_of(direction_now * product[...])
     extra = obs_error * direction_now
     own_curvature = total_of(direction_now * extra)
@@ -225,65 +295,59 @@
     )(in_hbm(innovations.reshape(1, LANES)), in_hbm(obs_error.reshape(1, LANES)))
     mate = lax.ppermute(anomalies, "sub", [(0, 1), (1, 0)])
 
-    pairs = row_count * row_count
-    share = pl.pallas_call(
+    block_len = total_obs // row_count
+    kept_count = min(row_count, KEPT_BYTES // (4 * block_len * block_len))
+    stored_count = row_count - kept_count + off_diagonal(row_count)
+    kept_shape, stored_shape = (kept_count, block_len, block_len), (stored_count, block_len, block_len)
+    work = [pltpu.VMEM((total_obs, LANES), f32), pltpu.VMEM((block_len, LANES), f32), pltpu.VMEM((8, total_obs), f32)]
+    kept, stored = pl.pallas_call(
         functools.partial(share_kernel, reach_tiles),
-        out_shape=jax.ShapeDtypeStruct((total_obs, total_obs), f32),
-        in_specs=[HBM_SPEC, HBM_SPEC, HBM_SPEC, VMEM_SPEC],
-        out_specs=HBM_SPEC,
+        out_shape=[pltpu.VMEM(kept_shape, f32), pltpu.HBM(stored_shape, f32)],
+        in_specs=[HBM_SPEC] * 4,
+        out_specs=[VMEM_SPEC, HBM_SPEC],
         scratch_shapes=[
             pltpu.SMEM(taper_class.shape, jnp.int32),
             pltpu.VMEM((1, total_obs), f32),
             pltpu.VMEM((2 * local_members, total_obs), anomalies.dtype),
             pltpu.VMEM((total_obs, 2 * local_members), anomalies.dtype),
             pltpu.VMEM((total_obs, LANES), f32),
-            pltpu.VMEM((total_obs, total_obs), f32),
-            pltpu.SemaphoreType.DMA((3,)),
-            pltpu.SemaphoreType.DMA((pairs,)),
+            pltpu.VMEM(stored_shape, f32),
+            pltpu.SemaphoreType.DMA((4,)),
+            pltpu.SemaphoreType.DMA((stored_count,)),
         ],
-        compiler_params=pltpu.CompilerParams(vmem_limit_bytes=40 * 1024 * 1024),
+        compiler_params=pltpu.CompilerParams(vmem_limit_bytes=24 * 1024 * 1024),
         cost_estimate=pl.CostEstimate(
             flops=4 * local_members * total_obs * total_obs,
             bytes_accessed=4 * total_obs * total_obs,
             transcendentals=total_obs * total_obs,
         ),
         name="share",
-    )(in_hbm(taper_class), in_hbm(track_pos.reshape(1, total_obs)), in_hbm(anomalies), mate)
+    )(in_hbm(taper_class), in_hbm(track_pos.reshape(1, total_obs)), in_hbm(anomalies), in_hbm(mate))
     vectors = lax.all_to_all(packed, ("row", "col", "sub"), split_axis=0, concat_axis=0, tiled=True)
 
     params = pltpu.CompilerParams(vmem_limit_bytes=8 * 1024 * 1024)
-    share, part = pl.pallas_call(
+    stored, part = pl.pallas_call(
         functools.partial(first_kernel, reach_tiles, inverse_members),
-        out_shape=[pltpu.VMEM((total_obs, total_obs), f32), pltpu.VMEM((pieces, LANES), f32)],
-        in_specs=[SMEM_SPEC, HBM_SPEC, VMEM_SPEC],
+        out_shape=[pltpu.VMEM(stored_shape, f32), pltpu.VMEM((pieces, LANES), f32)],
+        in_specs=[SMEM_SPEC, VMEM_SPEC, HBM_SPEC, VMEM_SPEC],
         out_specs=[VMEM_SPEC, VMEM_SPEC],
-        scratch_shapes=[
-            pltpu.VMEM((pieces, LANES), f32),
-            pltpu.VMEM((total_obs, LANES), f32),
-            pltpu.VMEM((8, total_obs), f32),
-            pltpu.SemaphoreType.DMA((pairs,)),
-        ],
+        scratch_shapes=[pltpu.VMEM((pieces, LANES), f32)] + work + [pltpu.SemaphoreType.DMA((stored_count,))],
         compiler_params=params,
         name="first",
-    )(taper_class, in_hbm(share), vectors)
-    parts = [part] + [swap_rows(part, mask) for mask in range(1, row_count)]
+    )(taper_class, kept, in_hbm(stored), vectors)
+    parts = [part] + [swap_rows(part, mask) for mask in reversed(range(1, row_count))]
 
     place = jnp.stack([row_index, within, jnp.int32(per_row)]).astype(jnp.int32)
     *sent, state = pl.pallas_call(
         functools.partial(second_kernel, reach_tiles, inverse_members, row_count),
         out_shape=[pltpu.VMEM((8, LANES), f32) for _ in range(row_count + 1)],
-        in_specs=[SMEM_SPEC, SMEM_SPEC, VMEM_SPEC, VMEM_SPEC] + [VMEM_SPEC] * row_count,
+        in_specs=[SMEM_SPEC, SMEM_SPEC] + [VMEM_SPEC] * (row_count + 3),
         out_specs=[VMEM_SPEC] * (row_count + 1),
-        scratch_shapes=[pltpu.VMEM((pieces, LANES), f32)] * 3
-        + [
-            pltpu.VMEM((total_obs, LANES), f32),
-            pltpu.VMEM((8, total_obs), f32),
-            pltpu.VMEM((pieces, LANES), f32),
-        ],
+        scratch_shapes=[pltpu.VMEM((pieces, LANES), f32)] * 3 + work + [pltpu.VMEM((pieces, LANES), f32)],
         compiler_params=params,
         name="second",
-    )(place, taper_class, share, vectors, *parts)
-    got = [sent[0]] + [swap_rows(sent[mask], mask) for mask in range(1, row_count)]
+    )(place, taper_class, kept, stored, vectors, *parts)
+    got = [sent[0]] + [swap_rows(sent[mask], mask) for mask in reversed(range(1, row_count))]
     solution_part, residual_part = pl.pallas_call(
         last_kernel,
         out_shape=[jax.ShapeDtypeStruct((1, LANES), f32)] * 2,

time: 40 us -> 36.1 us (0.903)
  Pallas kernels: 15.6 us -> 12.4 us
  waiting for transfers between devices: 6.94 us -> 5.45 us
  local copies, waits for them, and re-layouts: 0.01 us -> 0.8 us
    ppermute x6, waiting for transfers between devices: 6.48 us -> 4.34 us  [swap_rows(): return lax.ppermute(x, 'row', [(i, i ^ mask) for i in range(row_count)])]
    pallas_call x1, Pallas kernels: 4.97 us -> 3.25 us  [vectors_only(): pl.pallas_call(functools.partial(first_kernel, reach_tiles, inverse_membe...]
    pallas_call x1, Pallas kernels: 6.01 us -> 4.55 us  [vectors_only(): pl.pallas_call(functools.partial(share_kernel, reach_tiles), out_shape=[p...]
    unnamed x2 -> x4, local copies, waits for them, and re-layouts: 0.01 us -> 0.8 us
    all_to_all x1, waiting for transfers between devices: 0.46 us -> 1.11 us  [vectors_only(): lax.all_to_all(packed, ('row', 'col', 'sub'), split_axis=0, concat_axis=0...]
  transfers between devices with their start and end apart: 8 -> 8, of which waited for: 5 -> 5; matrix products, arithmetic and copies ran while one was open for 0% -> 0% of each run, Pallas kernels for 18% -> 16%
where the time goes in v3:
time: 36.1 us; the launch traced here: 35.8 us
  starting transfers between devices  16.4 us (45%)
  Pallas kernels  12.4 us (34%)
  waiting for transfers between devices  5.45 us (15%)
  local copies, waits for them, and re-layouts  0.8 us (2%)
  between operations  0.7 us (2%)
    ppermute x6, starting transfers between devices, swap_rows(): return lax.ppermute(x, 'row', [(i, i ^ mask) for i in range(row_count)])  8.84 us
    all_to_all x1, starting transfers between devices, vectors_only(): lax.all_to_all(packed, ('row', 'col', 'sub'), split_axis=0, concat_axis=0...  7.03 us
    pallas_call x1, Pallas kernels, vectors_only(): pl.pallas_call(functools.partial(share_kernel, reach_tiles), out_shape=[p...  4.55 us
    ppermute x6, waiting for transfers between devices, swap_rows(): return lax.ppermute(x, 'row', [(i, i ^ mask) for i in range(row_count)])  4.34 us
    pallas_call x1, Pallas kernels, vectors_only(): pl.pallas_call(functools.partial(first_kernel, reach_tiles, inverse_membe...  3.25 us
    pallas_call x1, Pallas kernels, vectors_only(): pl.pallas_call(functools.partial(second_kernel, reach_tiles, inverse_memb...  2.76 us
    pallas_call x1, Pallas kernels, vectors_only(): pl.pallas_call(pack_kernel, out_shape=pltpu.VMEM((devices, 1, 2 * LANES),...  1.29 us
    all_to_all x1, waiting for transfers between devices, vectors_only(): lax.all_to_all(packed, ('row', 'col', 'sub'), split_axis=0, concat_axis=0...  1.11 us
  transfers between devices with their start and end apart: 8, of which 5 were waited for; matrix products, arithmetic and copies ran while one was open for 0% of the time, Pallas kernels for 16%

profile of v3, /device:TPU:0, one launch (start us, length us, event | category | flops | bytes accessed | tf_op | source)
XLA Modules:
  0.0 35.8 jit_solution(15639096271180996818)
XLA Ops:
  0.6 0.0 copy-start
  0.6 0.5 %collective-permute-start = (bf16[128,2048]{1,0:T(8,128)(2,1)}, bf16[128,2048]{1,0:T(8,128)(2,1)S(1)}, u32[]{:S(2)}, u32[]{:S(2)}) collective-permute-start(bf16[128,2048]{1,0:T(8,128)(2,1)} %own_ref.1), channel_id=1, source_target_pairs={{0,1},{1,0},{2,3},{3,2},{4,5},{5,4},{6,7},{7,6},{8,9},{9,8},{10,11... | collective-permute-start | bytes 1572872 | tf_op jit(solution)/shard_map/ppermute | solution.py:296
  1.2 1.3 %pack.1 = f32[16,1,256]{2,1,0:T(1,128)} custom-call(f32[1,128]{1,0:T(1,128)} %bitcast.7, f32[1,128]{1,0:T(1,128)} %bitcast.8), custom_call_target="tpu_custom_call" | custom-call | tf_op jit(solution)/shard_map/pack/pallas_call | solution.py:287
  2.5 7.0 %all-to-all-start = ((f32[16,1,256]{2,1,0:T(1,128)}), f32[16,1,256]{2,1,0:T(1,128)S(1)}, u32[]{:S(2)}, u32[]{:S(2)}) async-start(f32[16,1,256]{2,1,0:T(1,128)} %pack.1), calls=%async_computation | async-start | bytes 32768 | tf_op jit(solution)/shard_map/all_to_all | solution.py:326
  9.5 0.0 collective-permute-done.mate_ref
  9.5 0.8 %copy-done.1 = bf16[128,2048]{1,0:T(8,128)(2,1)} copy-done((bf16[128,2048]{1,0:T(8,128)(2,1)}, bf16[128,2048]{1,0:T(8,128)(2,1)S(1)}, u32[]{:S(2)}) %copy-start.1) | copy-done | bytes 524312
  10.3 4.6 %share.1 = (f32[3,512,512]{2,1,0:T(8,128)S(1)}, f32[7,512,512]{2,1,0:T(8,128)}) custom-call(s32[4,4]{1,0:T(4,128)} %class_ref.3, f32[1,2048]{1,0:T(1,128)} %bitcast.9, bf16[128,2048]{1,0:T(8,128)(2,1)} %own_ref.1, bf16[128,2048]{1,0:T(8,128)(2,1)} %copy-done.1), custom_call_target="tpu_custom_call" | custom-call | flops 2147483648 | bytes 16777216 | tf_op jit(solution)/shard_map/share/pallas_call | solution.py:303
  14.9 1.1 %all-to-all-done.vectors_ref.refs_0_ = f32[16,1,256]{2,1,0:T(1,128)S(1)} async-done(((f32[16,1,256]{2,1,0:T(1,128)}), f32[16,1,256]{2,1,0:T(1,128)S(1)}, u32[]{:S(2)}, u32[]{:S(2)}) %all-to-all-start) | async-done | bytes 16416 | tf_op jit(solution)/shard_map/all_to_all | solution.py:326
  16.0 3.3 %first.1 = (f32[7,512,512]{2,1,0:T(8,128)S(1)}, f32[16,128]{1,0:T(8,128)S(1)}) custom-call(s32[4,4]{1,0:T(4,128)S(1)} %copy-done, f32[3,512,512]{2,1,0:T(8,128)S(1)} %get-tuple-element.13.kept_ref, f32[7,512,512]{2,1,0:T(8,128)} %get-tuple-element.14.hbm_ref, f32[16,1,256]{2,1,0:T(1,128)S(1)} %all-to-all-done.vectors_ref.refs_0_), custom_call_target="tpu_custom_call" | custom-call | tf_op jit(solution)/shard_map/first/pallas_call | solution.py:329
  19.3 2.7 %collective-permute-start.1 = (f32[16,128]{1,0:T(8,128)S(1)}, f32[16,128]{1,0:T(8,128)S(1)}, u32[]{:S(2)}, u32[]{:S(2)}) collective-permute-start(f32[16,128]{1,0:T(8,128)S(1)} %get-tuple-element.16.refs_1_), channel_id=1, source_target_pairs={{0,12},{4,8},{8,4},{12,0},{1,13},{5,9},{9,5},{13,1},{2,14},{6,10},... | collective-permute-start | bytes 24584 | tf_op jit(solution)/shard_map/ppermute | solution.py:269
  21.9 0.0 collective-permute-start.2
  22.0 1.8 %collective-permute-start.3 = (f32[16,128]{1,0:T(8,128)S(1)}, f32[16,128]{1,0:T(8,128)S(1)}, u32[]{:S(2)}, u32[]{:S(2)}) collective-permute-start(f32[16,128]{1,0:T(8,128)S(1)} %get-tuple-element.16.refs_1_), channel_id=1, source_target_pairs={{0,4},{4,0},{8,12},{12,8},{1,5},{5,1},{9,13},{13,9},{2,6},{6,2},{1... | collective-permute-start | bytes 24584 | tf_op jit(solution)/shard_map/ppermute | solution.py:269
  23.7 0.1 pad_add_fusion.place_ref
  23.8 1.0 %collective-permute-done.1.refs_2_ = f32[16,128]{1,0:T(8,128)S(1)} collective-permute-done((f32[16,128]{1,0:T(8,128)S(1)}, f32[16,128]{1,0:T(8,128)S(1)}, u32[]{:S(2)}, u32[]{:S(2)}) %collective-permute-start.1) | collective-permute-done | bytes 8224 | tf_op jit(solution)/shard_map/ppermute | solution.py:269
  24.8 1.7 %collective-permute-done.2.refs_3_ = f32[16,128]{1,0:T(8,128)S(1)} collective-permute-done((f32[16,128]{1,0:T(8,128)S(1)}, f32[16,128]{1,0:T(8,128)S(1)}, u32[]{:S(2)}, u32[]{:S(2)}) %collective-permute-start.2) | collective-permute-done | bytes 8224 | tf_op jit(solution)/shard_map/ppermute | solution.py:269
  26.5 0.0 collective-permute-done.3.refs_4_
  26.5 2.8 %second.1 = (f32[8,128]{1,0:T(8,128)S(1)}, f32[8,128]{1,0:T(8,128)S(1)}, f32[8,128]{1,0:T(8,128)S(1)}, f32[8,128]{1,0:T(8,128)S(1)}, f32[8,128]{1,0:T(8,128)S(1)}) custom-call(s32[3]{0:T(128)S(1)} %pad_add_fusion.place_ref, s32[4,4]{1,0:T(4,128)S(1)} %copy-done, f32[3,512,512]{2,1,0:T(8,128)S(1)} %get-tuple-element.13.kept_ref, ...), custom_call_target="tpu_custom_call" | custom-call | tf_op jit(solution)/shard_map/second/pallas_call | solution.py:341
  29.3 1.5 %collective-permute-start.4 = (f32[8,128]{1,0:T(8,128)S(1)}, f32[8,128]{1,0:T(8,128)S(1)}, u32[]{:S(2)}, u32[]{:S(2)}) collective-permute-start(f32[8,128]{1,0:T(8,128)S(1)} %get-tuple-element.19), channel_id=1, source_target_pairs={{0,12},{4,8},{8,4},{12,0},{1,13},{5,9},{9,5},{13,1},{2,14},{6,10},... | collective-permute-start | bytes 12296 | tf_op jit(solution)/shard_map/ppermute | solution.py:269
  30.7 0.9 %collective-permute-start.5 = (f32[8,128]{1,0:T(8,128)S(1)}, f32[8,128]{1,0:T(8,128)S(1)}, u32[]{:S(2)}, u32[]{:S(2)}) collective-permute-start(f32[8,128]{1,0:T(8,128)S(1)} %get-tuple-element.20), channel_id=1, source_target_pairs={{0,8},{4,12},{8,0},{12,4},{1,9},{5,13},{9,1},{13,5},{2,10},{6,14},... | collective-permute-start | bytes 12296 | tf_op jit(solution)/shard_map/ppermute | solution.py:269
  31.6 2.1 %collective-permute-start.6 = (f32[8,128]{1,0:T(8,128)S(1)}, f32[8,128]{1,0:T(8,128)S(1)}, u32[]{:S(2)}, u32[]{:S(2)}) collective-permute-start(f32[8,128]{1,0:T(8,128)S(1)} %get-tuple-element.21), channel_id=1, source_target_pairs={{0,4},{4,0},{8,12},{12,8},{1,5},{5,1},{9,13},{13,9},{2,6},{6,2},{1... | collective-permute-start | bytes 12296 | tf_op jit(solution)/shard_map/ppermute | solution.py:269
  33.7 1.0 %collective-permute-done.4.refs_1_ = f32[8,128]{1,0:T(8,128)S(1)} collective-permute-done((f32[8,128]{1,0:T(8,128)S(1)}, f32[8,128]{1,0:T(8,128)S(1)}, u32[]{:S(2)}, u32[]{:S(2)}) %collective-permute-start.4) | collective-permute-done | bytes 4128 | tf_op jit(solution)/shard_map/ppermute | solution.py:269
  34.7 0.6 %collective-permute-done.5.refs_2_ = f32[8,128]{1,0:T(8,128)S(1)} collective-permute-done((f32[8,128]{1,0:T(8,128)S(1)}, f32[8,128]{1,0:T(8,128)S(1)}, u32[]{:S(2)}, u32[]{:S(2)}) %collective-permute-start.5) | collective-permute-done | bytes 4128 | tf_op jit(solution)/shard_map/ppermute | solution.py:269
  35.2 0.0 collective-permute-done.6.refs_3_
  35.3 0.5 %last.1 = (f32[1,128]{1,0:T(1,128)}, f32[1,128]{1,0:T(1,128)}) custom-call(f32[8,128]{1,0:T(8,128)S(1)} %get-tuple-element.17.state_ref, f32[8,128]{1,0:T(8,128)S(1)} %get-tuple-element.18.refs_0_, f32[8,128]{1,0:T(8,128)S(1)} %collective-permute-done.4.refs_1_, f32[8,128]{1,0:T(8,128)S(1)} %collective-permute-done.5.refs_2_, ...), custom_call_target="tpu_custom_call" | custom-call | tf_op jit(solution)/shard_map/last/pallas_call | solution.py:351
  (2 shorter events, 0.0 us)
Async XLA Ops:
  0.6 15.4 %copy-start = (s32[4,4]{1,0:T(4,128)S(1)}, s32[4,4]{1,0:T(4,128)}, u32[]{:S(2)}) copy-start(s32[4,4]{1,0:T(4,128)} %class_ref.3) | copy-start | bytes 196
  0.6 8.9 %collective-permute-start = (bf16[128,2048]{1,0:T(8,128)(2,1)}, bf16[128,2048]{1,0:T(8,128)(2,1)S(1)}, u32[]{:S(2)}, u32[]{:S(2)}) collective-permute-start(bf16[128,2048]{1,0:T(8,128)(2,1)} %own_ref.1), channel_id=1, source_target_pairs={{0,1},{1,0},{2,3},{3,2},{4,5},{5,4},{6,7},{7,6},{8,9},{9,8},{10,11... | collective-permute-start | bytes 1572872 | tf_op jit(solution)/shard_map/ppermute | solution.py:296
  2.5 13.5 %all-to-all-start = ((f32[16,1,256]{2,1,0:T(1,128)}), f32[16,1,256]{2,1,0:T(1,128)S(1)}, u32[]{:S(2)}, u32[]{:S(2)}) async-start(f32[16,1,256]{2,1,0:T(1,128)} %pack.1), calls=%async_computation | async-start | bytes 32768 | tf_op jit(solution)/shard_map/all_to_all | solution.py:326
  9.5 0.8 %copy-start.1 = (bf16[128,2048]{1,0:T(8,128)(2,1)}, bf16[128,2048]{1,0:T(8,128)(2,1)S(1)}, u32[]{:S(2)}) copy-start(bf16[128,2048]{1,0:T(8,128)(2,1)S(1)} %collective-permute-done.mate_ref) | copy-start | bytes 1572868
  19.3 5.5 %collective-permute-start.1 = (f32[16,128]{1,0:T(8,128)S(1)}, f32[16,128]{1,0:T(8,128)S(1)}, u32[]{:S(2)}, u32[]{:S(2)}) collective-permute-start(f32[16,128]{1,0:T(8,128)S(1)} %get-tuple-element.16.refs_1_), channel_id=1, source_target_pairs={{0,12},{4,8},{8,4},{12,0},{1,13},{5,9},{9,5},{13,1},{2,14},{6,10},... | collective-permute-start | bytes 24584 | tf_op jit(solution)/shard_map/ppermute | solution.py:269
  21.9 4.5 %collective-permute-start.2 = (f32[16,128]{1,0:T(8,128)S(1)}, f32[16,128]{1,0:T(8,128)S(1)}, u32[]{:S(2)}, u32[]{:S(2)}) collective-permute-start(f32[16,128]{1,0:T(8,128)S(1)} %get-tuple-element.16.refs_1_), channel_id=1, source_target_pairs={{0,8},{4,12},{8,0},{12,4},{1,9},{5,13},{9,1},{13,5},{2,10},{6,14},... | collective-permute-start | bytes 24584 | tf_op jit(solution)/shard_map/ppermute | solution.py:269
  22.0 4.5 %collective-permute-start.3 = (f32[16,128]{1,0:T(8,128)S(1)}, f32[16,128]{1,0:T(8,128)S(1)}, u32[]{:S(2)}, u32[]{:S(2)}) collective-permute-start(f32[16,128]{1,0:T(8,128)S(1)} %get-tuple-element.16.refs_1_), channel_id=1, source_target_pairs={{0,4},{4,0},{8,12},{12,8},{1,5},{5,1},{9,13},{13,9},{2,6},{6,2},{1... | collective-permute-start | bytes 24584 | tf_op jit(solution)/shard_map/ppermute | solution.py:269
  29.3 5.4 %collective-permute-start.4 = (f32[8,128]{1,0:T(8,128)S(1)}, f32[8,128]{1,0:T(8,128)S(1)}, u32[]{:S(2)}, u32[]{:S(2)}) collective-permute-start(f32[8,128]{1,0:T(8,128)S(1)} %get-tuple-element.19), channel_id=1, source_target_pairs={{0,12},{4,8},{8,4},{12,0},{1,13},{5,9},{9,5},{13,1},{2,14},{6,10},... | collective-permute-start | bytes 12296 | tf_op jit(solution)/shard_map/ppermute | solution.py:269
  30.7 4.5 %collective-permute-start.5 = (f32[8,128]{1,0:T(8,128)S(1)}, f32[8,128]{1,0:T(8,128)S(1)}, u32[]{:S(2)}, u32[]{:S(2)}) collective-permute-start(f32[8,128]{1,0:T(8,128)S(1)} %get-tuple-element.20), channel_id=1, source_target_pairs={{0,8},{4,12},{8,0},{12,4},{1,9},{5,13},{9,1},{13,5},{2,10},{6,14},... | collective-permute-start | bytes 12296 | tf_op jit(solution)/shard_map/ppermute | solution.py:269
  31.6 3.7 %collective-permute-start.6 = (f32[8,128]{1,0:T(8,128)S(1)}, f32[8,128]{1,0:T(8,128)S(1)}, u32[]{:S(2)}, u32[]{:S(2)}) collective-permute-start(f32[8,128]{1,0:T(8,128)S(1)} %get-tuple-element.21), channel_id=1, source_target_pairs={{0,4},{4,0},{8,12},{12,8},{1,5},{5,1},{9,13},{13,9},{2,6},{6,2},{1... | collective-permute-start | bytes 12296 | tf_op jit(solution)/shard_map/ppermute | solution.py:269

commit v4 on v3

--- a/solution.py
+++ b/solution.py
@@ -21,32 +21,38 @@
     return tiles * (tiles - 1) // 2
 
 
+def first_slot(a, tiles):
+    return a * tiles - (a * (a + 1)) // 2
+
+
 def for_each_pair(reach_tiles, class_ref, action):
     tiles = class_ref.shape[0]
 
-    def one_pair(pair, carry):
-        a, b = pair // tiles, pair % tiles
-        slot = a * tiles - (a * (a + 1)) // 2 + b - a - 1
-        pl.when(jnp.logical_and(a < b, class_ref[a, b] < reach_tiles))(lambda: action(slot, a, b))
+    def one_pair(slot, carry):
+        a = jnp.int32(0)
+        for row in range(1, tiles - 1):
+            a = a + (slot >= first_slot(row, tiles)).astype(jnp.int32)
+        b = slot - first_slot(a, tiles) + a + 1
+        pl.when(class_ref[a, b] < reach_tiles)(lambda: action(slot, a, b))
         return carry
 
-    lax.fori_loop(0, tiles * tiles, one_pair, 0)
+    lax.fori_loop(0, off_diagonal(tiles), one_pair, 0)
+
+
+def each_pair(reach_tiles, class_ref, action):
+    tiles = class_ref.shape[0]
+    for a in range(tiles):
+        for b in range(a + 1, tiles):
+            slot = first_slot(a, tiles) + b - a - 1
+            pl.when(class_ref[a, b] < reach_tiles)(functools.partial(action, slot))
 
 
 def block_at(a, block_len):
     return pl.ds(pl.multiple_of(a * block_len, LANES), block_len)
 
 
-def pack_kernel(innovations_ref, obs_error_ref, packed_ref, row, arrived):
-    copies = [
-        pltpu.make_async_copy(ref, row.at[:, pl.ds(at * LANES, LANES)], arrived.at[at])
-        for at, ref in enumerate((innovations_ref, obs_error_ref))
-    ]
-    for copy in copies:
-        copy.start()
-    for copy in copies:
-        copy.wait()
-    packed_ref[...] = jnp.broadcast_to(row[...], packed_ref.shape)
+def pack_kernel(row_ref, packed_ref):
+    packed_ref[...] = jnp.broadcast_to(row_ref[...], packed_ref.shape)
 
 
 def share_kernel(reach_tiles, class_hbm, pos_hbm, own_ref, mate_ref, kept_ref, stored_ref, *scratch):
@@ -102,7 +108,7 @@
     for_each_pair(reach_tiles, class_ref, make_pair)
     lax.fori_loop(0, tiles - kept, make_stored, 0)
     lax.fori_loop(0, kept, make_kept, 0)
-    for_each_pair(reach_tiles, class_ref, lambda slot, a, b: out_copy(slot + tiles - kept).wait())
+    each_pair(reach_tiles, class_ref, lambda slot: out_copy(slot + tiles - kept).wait())
     for slot in range(tiles - kept):
         out_copy(slot).wait()
 
@@ -111,6 +117,12 @@
     for begin in range(0, column.shape[0], LANES):
         square = jnp.broadcast_to(row[:, begin : begin + LANES], (LANES, LANES))
         column[begin : begin + LANES, :] = square.T
+
+
+def spread_vector(vector, column):
+    for piece in range(vector.shape[0]):
+        square = jnp.broadcast_to(vector[piece : piece + 1, :], (LANES, LANES))
+        column[piece * LANES : (piece + 1) * LANES, :] = square.T
 
 
 def apply_share(
@@ -120,9 +132,6 @@
     kept = kept_ref.shape[0]
     block_len = kept_ref.shape[1]
     lanes = block_len // LANES
-    for piece in range(tiles * lanes):
-        square = jnp.broadcast_to(vector[piece : piece + 1, :], (LANES, LANES))
-        column[piece * LANES : (piece + 1) * LANES, :] = square.T
     sums[...] = jnp.zeros_like(sums)
 
     def add_diagonal(tile, a):
@@ -187,18 +196,22 @@
         out_ref[piece : piece + 1, :] = jnp.sum(sums[:, piece * LANES : (piece + 1) * LANES], axis=0, keepdims=True)
 
 
-def first_kernel(reach_tiles, inverse_members, class_ref, kept_ref, hbm_ref, vectors_ref, stored_ref, out_ref, *scratch):
-    vector, column, across, sums, arrived = scratch
+def first_kernel(reach_tiles, inverse_members, class_vmem, kept_ref, hbm_ref, vectors_ref, stored_ref, out_ref, *scratch):
+    class_ref, vector, column, across, sums, arrived, class_arrived = scratch
     tiles = class_ref.shape[0]
     kept = kept_ref.shape[0]
+    class_copy = pltpu.make_async_copy(class_vmem, class_ref, class_arrived)
+    class_copy.start()
 
     def in_copy(slot):
         return pltpu.make_async_copy(hbm_ref.at[slot], stored_ref.at[slot], arrived.at[slot])
 
     for slot in range(tiles - kept):
         in_copy(slot).start()
-    for_each_pair(reach_tiles, class_ref, lambda slot, a, b: in_copy(slot + tiles - kept).start())
     vector[...] = vectors_ref[:, 0, :LANES]
+    spread_vector(vector, column)
+    class_copy.wait()
+    each_pair(reach_tiles, class_ref, lambda slot: in_copy(slot + tiles - kept).start())
     ready = lambda slot: in_copy(slot).wait()
     refs = (class_ref, kept_ref, stored_ref, vector, column, across, sums, out_ref)
     apply_share(reach_tiles, inverse_members, *refs, ready)
@@ -208,10 +221,12 @@
     return jnp.sum(jnp.sum(x, axis=0, keepdims=True), axis=1, keepdims=True)
 
 
-def second_kernel(reach_tiles, inverse_members, peers, place_ref, class_ref, kept_ref, stored_ref, *refs):
+def second_kernel(reach_tiles, inverse_members, peers, class_vmem, kept_ref, stored_ref, *refs):
     vectors_ref, parts, refs = refs[0], refs[1 : peers + 1], refs[peers + 1 :]
     sent, refs = refs[:peers], refs[peers:]
-    state_ref, direction, residual, start, column, across, sums, product = refs
+    state_ref, class_ref, direction, residual, start, column, across, sums, product, class_arrived = refs
+    class_copy = pltpu.make_async_copy(class_vmem, class_ref, class_arrived)
+    class_copy.start()
     innovations, obs_error = vectors_ref[:, 0, :LANES], vectors_ref[:, 0, LANES:]
     image = obs_error * innovations
     for part in parts:
@@ -224,12 +239,16 @@
     residual[...] = residual_now
     direction[...] = direction_now
     start[...] = alpha * innovations
+    spread_vector(direction, column)
+    class_copy.wait()
     shared = (class_ref, kept_ref, stored_ref, direction, column, across, sums, product)
     apply_share(reach_tiles, inverse_members, *shared)
     curvature = total_of(direction_now * product[...])
     extra = obs_error * direction_now
     own_curvature = total_of(direction_now * extra)
-    row_index, within, per_row = place_ref[0], place_ref[1], place_ref[2]
+    row_index = lax.axis_index("row")
+    within = lax.axis_index("col") * lax.axis_size("sub") + lax.axis_index("sub")
+    per_row = lax.axis_size("col") * lax.axis_size("sub")
     for peer in range(peers):
         at = (row_index ^ peer) * per_row + within
         sent[peer][0:1, :] = product[pl.ds(at, 1), :]
@@ -273,8 +292,6 @@
     row_count = lax.axis_size("row")
     col_count = lax.axis_size("col")
     sub_count = lax.axis_size("sub")
-    row_index = lax.axis_index("row")
-    within = lax.axis_index("col") * sub_count + lax.axis_index("sub")
     local_members, total_obs = anomalies.shape
     member_total = local_members * row_count * sub_count
     inverse_members = 1.0 / (member_total - 1)
@@ -287,18 +304,18 @@
     packed = pl.pallas_call(
         pack_kernel,
         out_shape=pltpu.VMEM((devices, 1, 2 * LANES), f32),
-        in_specs=[HBM_SPEC, HBM_SPEC],
+        in_specs=[VMEM_SPEC],
         out_specs=VMEM_SPEC,
-        scratch_shapes=[pltpu.VMEM((1, 2 * LANES), f32), pltpu.SemaphoreType.DMA((2,))],
         compiler_params=pltpu.CompilerParams(vmem_limit_bytes=1024 * 1024),
         name="pack",
-    )(in_hbm(innovations.reshape(1, LANES)), in_hbm(obs_error.reshape(1, LANES)))
+    )(jnp.concatenate([innovations, obs_error]).reshape(1, 2 * LANES))
     mate = lax.ppermute(anomalies, "sub", [(0, 1), (1, 0)])
 
     block_len = total_obs // row_count
     kept_count = min(row_count, KEPT_BYTES // (4 * block_len * block_len))
     stored_count = row_count - kept_count + off_diagonal(row_count)
     kept_shape, stored_shape = (kept_count, block_len, block_len), (stored_count, block_len, block_len)
+    class_here = pltpu.SMEM(taper_class.shape, jnp.int32)
     work = [pltpu.VMEM((total_obs, LANES), f32), pltpu.VMEM((block_len, LANES), f32), pltpu.VMEM((8, total_obs), f32)]
     kept, stored = pl.pallas_call(
         functools.partial(share_kernel, reach_tiles),
@@ -306,7 +323,7 @@
         in_specs=[HBM_SPEC] * 4,
         out_specs=[VMEM_SPEC, HBM_SPEC],
         scratch_shapes=[
-            pltpu.SMEM(taper_class.shape, jnp.int32),
+            class_here,
             pltpu.VMEM((1, total_obs), f32),
             pltpu.VMEM((2 * local_members, total_obs), anomalies.dtype),
             pltpu.VMEM((total_obs, 2 * local_members), anomalies.dtype),
@@ -329,24 +346,28 @@
     stored, part = pl.pallas_call(
         functools.partial(first_kernel, reach_tiles, inverse_members),
         out_shape=[pltpu.VMEM(stored_shape, f32), pltpu.VMEM((pieces, LANES), f32)],
-        in_specs=[SMEM_SPEC, VMEM_SPEC, HBM_SPEC, VMEM_SPEC],
+        in_specs=[VMEM_SPEC, VMEM_SPEC, HBM_SPEC, VMEM_SPEC],
         out_specs=[VMEM_SPEC, VMEM_SPEC],
-        scratch_shapes=[pltpu.VMEM((pieces, LANES), f32)] + work + [pltpu.SemaphoreType.DMA((stored_count,))],
+        scratch_shapes=[class_here, pltpu.VMEM((pieces, LANES), f32)]
+        + work
+        + [pltpu.SemaphoreType.DMA((stored_count,)), pltpu.SemaphoreType.DMA(())],
         compiler_params=params,
         name="first",
     )(taper_class, kept, in_hbm(stored), vectors)
-    parts = [part] + [swap_rows(part, mask) for mask in reversed(range(1, row_count))]
-
-    place = jnp.stack([row_index, within, jnp.int32(per_row)]).astype(jnp.int32)
+    parts = [part] + [swap_rows(part, mask) for mask in range(1, row_count)]
+
     *sent, state = pl.pallas_call(
         functools.partial(second_kernel, reach_tiles, inverse_members, row_count),
         out_shape=[pltpu.VMEM((8, LANES), f32) for _ in range(row_count + 1)],
-        in_specs=[SMEM_SPEC, SMEM_SPEC] + [VMEM_SPEC] * (row_count + 3),
+        in_specs=[VMEM_SPEC] * (row_count + 4),
         out_specs=[VMEM_SPEC] * (row_count + 1),
-        scratch_shapes=[pltpu.VMEM((pieces, LANES), f32)] * 3 + work + [pltpu.VMEM((pieces, LANES), f32)],
+        scratch_shapes=[class_here]
+        + [pltpu.VMEM((pieces, LANES), f32)] * 3
+        + work
+        + [pltpu.VMEM((pieces, LANES), f32), pltpu.SemaphoreType.DMA(())],
         compiler_params=params,
         name="second",
-    )(place, taper_class, kept, stored, vectors, *parts)
+    )(taper_class, kept, stored, vectors, *parts)
     got = [sent[0]] + [swap_rows(sent[mask], mask) for mask in reversed(range(1, row_count))]
     solution_part, residual_part = pl.pallas_call(
         last_kernel,

time: 36.1 us -> 34.8 us (0.964)
  Pallas kernels: 12.4 us -> 9.88 us
  other arithmetic: 0.08 us -> 0.68 us
  waiting for transfers between devices: 5.45 us -> 6.03 us
    pallas_call x1, Pallas kernels: 2.76 us -> 1.98 us  [vectors_only(): pl.pallas_call(functools.partial(second_kernel, reach_tiles, inverse_memb...]
    pallas_call x1, Pallas kernels: 1.29 us -> 0.6 us  [vectors_only(): pl.pallas_call(pack_kernel, out_shape=pltpu.VMEM((devices, 1, 2 * LANES),...]
    concatenate x0 -> x1, other arithmetic: none -> 0.68 us  [vectors_only(): jnp.concatenate([innovations, obs_error]).reshape(1, 2 * LANES)]
    all_to_all x1, waiting for transfers between devices: 1.11 us -> 1.7 us  [vectors_only(): lax.all_to_all(packed, ('row', 'col', 'sub'), split_axis=0, concat_axis=0...]
    pallas_call x1, Pallas kernels: 4.55 us -> 3.97 us  [vectors_only(): pl.pallas_call(functools.partial(share_kernel, reach_tiles), out_shape=[p...]
    pallas_call x1, Pallas kernels: 3.25 us -> 2.8 us  [vectors_only(): pl.pallas_call(functools.partial(first_kernel, reach_tiles, inverse_membe...]
  transfers between devices with their start and end apart: 8 -> 8, of which waited for: 5 -> 6; matrix products, arithmetic and copies ran while one was open for 0% -> 2% of each run, Pallas kernels for 16% -> 13%
where the time goes in v4:
time: 34.8 us; the launch traced here: 34.5 us
  starting transfers between devices  16.4 us (47%)
  Pallas kernels  9.88 us (28%)
  waiting for transfers between devices  6.03 us (17%)
  local copies, waits for them, and re-layouts  0.8 us (2%)
  between operations  0.69 us (2%)
  other arithmetic  0.68 us (2%)
    ppermute x6, starting transfers between devices, swap_rows(): return lax.ppermute(x, 'row', [(i, i ^ mask) for i in range(row_count)])  8.91 us
    all_to_all x1, starting transfers between devices, vectors_only(): lax.all_to_all(packed, ('row', 'col', 'sub'), split_axis=0, concat_axis=0...  7.02 us
    ppermute x6, waiting for transfers between devices, swap_rows(): return lax.ppermute(x, 'row', [(i, i ^ mask) for i in range(row_count)])  4.33 us
    pallas_call x1, Pallas kernels, vectors_only(): pl.pallas_call(functools.partial(share_kernel, reach_tiles), out_shape=[p...  3.97 us
    pallas_call x1, Pallas kernels, vectors_only(): pl.pallas_call(functools.partial(first_kernel, reach_tiles, inverse_membe...  2.8 us
    pallas_call x1, Pallas kernels, vectors_only(): pl.pallas_call(functools.partial(second_kernel, reach_tiles, inverse_memb...  1.98 us
    all_to_all x1, waiting for transfers between devices, vectors_only(): lax.all_to_all(packed, ('row', 'col', 'sub'), split_axis=0, concat_axis=0...  1.7 us
    unnamed x4, local copies, waits for them, and re-layouts  0.8 us
  transfers between devices with their start and end apart: 8, of which 6 were waited for; matrix products, arithmetic and copies ran while one was open for 2% of the time, Pallas kernels for 13%

profile of v4, /device:TPU:0, one launch (start us, length us, event | category | flops | bytes accessed | tf_op | source)
XLA Modules:
  0.0 34.5 jit_solution(2137541998184429265)
XLA Ops:
  0.6 0.0 copy-start
  0.6 0.5 %collective-permute-start = (bf16[128,2048]{1,0:T(8,128)(2,1)}, bf16[128,2048]{1,0:T(8,128)(2,1)S(1)}, u32[]{:S(2)}, u32[]{:S(2)}) collective-permute-start(bf16[128,2048]{1,0:T(8,128)(2,1)} %own_ref.1), channel_id=1, source_target_pairs={{0,1},{1,0},{2,3},{3,2},{4,5},{5,4},{6,7},{7,6},{8,9},{9,8},{10,11... | collective-permute-start | bytes 1572872 | tf_op jit(solution)/shard_map/ppermute | solution.py:312
  1.2 0.7 %pad_maximum_fusion = f32[256]{0:T(256)S(1)} fusion(f32[128]{0:T(128)} %param.7, f32[128]{0:T(128)} %param.6), kind=kLoop, calls=%fused_computation | loop fusion | flops 256 | bytes 2048 | tf_op jit(solution)/shard_map/concatenate | solution.py:311
  1.8 0.6 %pack.1 = f32[16,1,256]{2,1,0:T(1,128)} custom-call(f32[1,256]{1,0:T(1,128)S(1)} %bitcast.4), custom_call_target="tpu_custom_call" | custom-call | tf_op jit(solution)/shard_map/pack/pallas_call | solution.py:304
  2.4 7.0 %all-to-all-start = ((f32[16,1,256]{2,1,0:T(1,128)}), f32[16,1,256]{2,1,0:T(1,128)S(1)}, u32[]{:S(2)}, u32[]{:S(2)}) async-start(f32[16,1,256]{2,1,0:T(1,128)} %pack.1), calls=%async_computation | async-start | bytes 32768 | tf_op jit(solution)/shard_map/all_to_all | solution.py:343
  9.5 0.0 collective-permute-done.mate_ref
  9.5 0.8 %copy-done.1 = bf16[128,2048]{1,0:T(8,128)(2,1)} copy-done((bf16[128,2048]{1,0:T(8,128)(2,1)}, bf16[128,2048]{1,0:T(8,128)(2,1)S(1)}, u32[]{:S(2)}) %copy-start.1) | copy-done | bytes 524312
  10.3 4.0 %share.1 = (f32[3,512,512]{2,1,0:T(8,128)S(1)}, f32[7,512,512]{2,1,0:T(8,128)}) custom-call(s32[4,4]{1,0:T(4,128)} %class_vmem.3, f32[1,2048]{1,0:T(1,128)} %bitcast.5, bf16[128,2048]{1,0:T(8,128)(2,1)} %own_ref.1, bf16[128,2048]{1,0:T(8,128)(2,1)} %copy-done.1), custom_call_target="tpu_custom_call" | custom-call | flops 2147483648 | bytes 16777216 | tf_op jit(solution)/shard_map/share/pallas_call | solution.py:320
  14.3 1.7 %all-to-all-done.vectors_ref.refs_0_ = f32[16,1,256]{2,1,0:T(1,128)S(1)} async-done(((f32[16,1,256]{2,1,0:T(1,128)}), f32[16,1,256]{2,1,0:T(1,128)S(1)}, u32[]{:S(2)}, u32[]{:S(2)}) %all-to-all-start) | async-done | bytes 16416 | tf_op jit(solution)/shard_map/all_to_all | solution.py:343
  16.0 2.8 %first.1 = (f32[7,512,512]{2,1,0:T(8,128)S(1)}, f32[16,128]{1,0:T(8,128)S(1)}) custom-call(s32[4,4]{1,0:T(4,128)S(1)} %copy-done, f32[3,512,512]{2,1,0:T(8,128)S(1)} %get-tuple-element.13.kept_ref, f32[7,512,512]{2,1,0:T(8,128)} %get-tuple-element.14.hbm_ref, f32[16,1,256]{2,1,0:T(1,128)S(1)} %all-to-all-done.vectors_ref.refs_0_), custom_call_target="tpu_custom_call" | custom-call | tf_op jit(solution)/shard_map/first/pallas_call | solution.py:346
  18.8 2.1 %collective-permute-start.3 = (f32[16,128]{1,0:T(8,128)S(1)}, f32[16,128]{1,0:T(8,128)S(1)}, u32[]{:S(2)}, u32[]{:S(2)}) collective-permute-start(f32[16,128]{1,0:T(8,128)S(1)} %get-tuple-element.16.refs_1_), channel_id=1, source_target_pairs={{0,12},{4,8},{8,4},{12,0},{1,13},{5,9},{9,5},{13,1},{2,14},{6,10},... | collective-permute-start | bytes 24584 | tf_op jit(solution)/shard_map/ppermute | solution.py:288
  20.9 0.0 collective-permute-start.2
  20.9 2.3 %collective-permute-start.1 = (f32[16,128]{1,0:T(8,128)S(1)}, f32[16,128]{1,0:T(8,128)S(1)}, u32[]{:S(2)}, u32[]{:S(2)}) collective-permute-start(f32[16,128]{1,0:T(8,128)S(1)} %get-tuple-element.16.refs_1_), channel_id=1, source_target_pairs={{0,4},{4,0},{8,12},{12,8},{1,5},{5,1},{9,13},{13,9},{2,6},{6,2},{1... | collective-permute-start | bytes 24584 | tf_op jit(solution)/shard_map/ppermute | solution.py:288
  23.2 1.1 %collective-permute-done.3.refs_4_ = f32[16,128]{1,0:T(8,128)S(1)} collective-permute-done((f32[16,128]{1,0:T(8,128)S(1)}, f32[16,128]{1,0:T(8,128)S(1)}, u32[]{:S(2)}, u32[]{:S(2)}) %collective-permute-start.3) | collective-permute-done | bytes 8224 | tf_op jit(solution)/shard_map/ppermute | solution.py:288
  24.3 1.1 %collective-permute-done.2.refs_3_ = f32[16,128]{1,0:T(8,128)S(1)} collective-permute-done((f32[16,128]{1,0:T(8,128)S(1)}, f32[16,128]{1,0:T(8,128)S(1)}, u32[]{:S(2)}, u32[]{:S(2)}) %collective-permute-start.2) | collective-permute-done | bytes 8224 | tf_op jit(solution)/shard_map/ppermute | solution.py:288
  25.4 0.0 collective-permute-done.1.refs_2_
  25.4 2.0 %second.1 = (f32[8,128]{1,0:T(8,128)S(1)}, f32[8,128]{1,0:T(8,128)S(1)}, f32[8,128]{1,0:T(8,128)S(1)}, f32[8,128]{1,0:T(8,128)S(1)}, f32[8,128]{1,0:T(8,128)S(1)}) custom-call(s32[4,4]{1,0:T(4,128)S(1)} %copy-done, f32[3,512,512]{2,1,0:T(8,128)S(1)} %get-tuple-element.13.kept_ref, f32[7,512,512]{2,1,0:T(8,128)S(1)} %get-tuple-element.15.stored_ref, ...), custom_call_target="tpu_custom_call" | custom-call | tf_op jit(solution)/shard_map/second/pallas_call | solution.py:359
  27.4 1.8 %collective-permute-start.4 = (f32[8,128]{1,0:T(8,128)S(1)}, f32[8,128]{1,0:T(8,128)S(1)}, u32[]{:S(2)}, u32[]{:S(2)}) collective-permute-start(f32[8,128]{1,0:T(8,128)S(1)} %get-tuple-element.19), channel_id=1, source_target_pairs={{0,12},{4,8},{8,4},{12,0},{1,13},{5,9},{9,5},{13,1},{2,14},{6,10},... | collective-permute-start | bytes 12296 | tf_op jit(solution)/shard_map/ppermute | solution.py:288
  29.3 1.1 %collective-permute-start.5 = (f32[8,128]{1,0:T(8,128)S(1)}, f32[8,128]{1,0:T(8,128)S(1)}, u32[]{:S(2)}, u32[]{:S(2)}) collective-permute-start(f32[8,128]{1,0:T(8,128)S(1)} %get-tuple-element.20), channel_id=1, source_target_pairs={{0,8},{4,12},{8,0},{12,4},{1,9},{5,13},{9,1},{13,5},{2,10},{6,14},... | collective-permute-start | bytes 12296 | tf_op jit(solution)/shard_map/ppermute | solution.py:288
  30.4 1.5 %collective-permute-start.6 = (f32[8,128]{1,0:T(8,128)S(1)}, f32[8,128]{1,0:T(8,128)S(1)}, u32[]{:S(2)}, u32[]{:S(2)}) collective-permute-start(f32[8,128]{1,0:T(8,128)S(1)} %get-tuple-element.21), channel_id=1, source_target_pairs={{0,4},{4,0},{8,12},{12,8},{1,5},{5,1},{9,13},{13,9},{2,6},{6,2},{1... | collective-permute-start | bytes 12296 | tf_op jit(solution)/shard_map/ppermute | solution.py:288
  31.9 1.0 %collective-permute-done.4.refs_1_ = f32[8,128]{1,0:T(8,128)S(1)} collective-permute-done((f32[8,128]{1,0:T(8,128)S(1)}, f32[8,128]{1,0:T(8,128)S(1)}, u32[]{:S(2)}, u32[]{:S(2)}) %collective-permute-start.4) | collective-permute-done | bytes 4128 | tf_op jit(solution)/shard_map/ppermute | solution.py:288
  32.9 0.9 %collective-permute-done.5.refs_2_ = f32[8,128]{1,0:T(8,128)S(1)} collective-permute-done((f32[8,128]{1,0:T(8,128)S(1)}, f32[8,128]{1,0:T(8,128)S(1)}, u32[]{:S(2)}, u32[]{:S(2)}) %collective-permute-start.5) | collective-permute-done | bytes 4128 | tf_op jit(solution)/shard_map/ppermute | solution.py:288
  33.8 0.2 collective-permute-done.6.refs_3_
  34.0 0.5 %last.1 = (f32[1,128]{1,0:T(1,128)}, f32[1,128]{1,0:T(1,128)}) custom-call(f32[8,128]{1,0:T(8,128)S(1)} %get-tuple-element.17.state_ref, f32[8,128]{1,0:T(8,128)S(1)} %get-tuple-element.18.refs_0_, f32[8,128]{1,0:T(8,128)S(1)} %collective-permute-done.4.refs_1_, f32[8,128]{1,0:T(8,128)S(1)} %collective-permute-done.5.refs_2_, ...), custom_call_target="tpu_custom_call" | custom-call | tf_op jit(solution)/shard_map/last/pallas_call | solution.py:372
  (2 shorter events, 0.0 us)
Async XLA Ops:
  0.6 15.3 %copy-start = (s32[4,4]{1,0:T(4,128)S(1)}, s32[4,4]{1,0:T(4,128)}, u32[]{:S(2)}) copy-start(s32[4,4]{1,0:T(4,128)} %class_vmem.3) | copy-start | bytes 196
  0.6 8.8 %collective-permute-start = (bf16[128,2048]{1,0:T(8,128)(2,1)}, bf16[128,2048]{1,0:T(8,128)(2,1)S(1)}, u32[]{:S(2)}, u32[]{:S(2)}) collective-permute-start(bf16[128,2048]{1,0:T(8,128)(2,1)} %own_ref.1), channel_id=1, source_target_pairs={{0,1},{1,0},{2,3},{3,2},{4,5},{5,4},{6,7},{7,6},{8,9},{9,8},{10,11... | collective-permute-start | bytes 1572872 | tf_op jit(solution)/shard_map/ppermute | solution.py:312
  2.4 13.5 %all-to-all-start = ((f32[16,1,256]{2,1,0:T(1,128)}), f32[16,1,256]{2,1,0:T(1,128)S(1)}, u32[]{:S(2)}, u32[]{:S(2)}) async-start(f32[16,1,256]{2,1,0:T(1,128)} %pack.1), calls=%async_computation | async-start | bytes 32768 | tf_op jit(solution)/shard_map/all_to_all | solution.py:343
  9.5 0.8 %copy-start.1 = (bf16[128,2048]{1,0:T(8,128)(2,1)}, bf16[128,2048]{1,0:T(8,128)(2,1)S(1)}, u32[]{:S(2)}) copy-start(bf16[128,2048]{1,0:T(8,128)(2,1)S(1)} %collective-permute-done.mate_ref) | copy-start | bytes 1572868
  18.8 5.5 %collective-permute-start.3 = (f32[16,128]{1,0:T(8,128)S(1)}, f32[16,128]{1,0:T(8,128)S(1)}, u32[]{:S(2)}, u32[]{:S(2)}) collective-permute-start(f32[16,128]{1,0:T(8,128)S(1)} %get-tuple-element.16.refs_1_), channel_id=1, source_target_pairs={{0,12},{4,8},{8,4},{12,0},{1,13},{5,9},{9,5},{13,1},{2,14},{6,10},... | collective-permute-start | bytes 24584 | tf_op jit(solution)/shard_map/ppermute | solution.py:288
  20.9 4.5 %collective-permute-start.2 = (f32[16,128]{1,0:T(8,128)S(1)}, f32[16,128]{1,0:T(8,128)S(1)}, u32[]{:S(2)}, u32[]{:S(2)}) collective-permute-start(f32[16,128]{1,0:T(8,128)S(1)} %get-tuple-element.16.refs_1_), channel_id=1, source_target_pairs={{0,8},{4,12},{8,0},{12,4},{1,9},{5,13},{9,1},{13,5},{2,10},{6,14},... | collective-permute-start | bytes 24584 | tf_op jit(solution)/shard_map/ppermute | solution.py:288
  20.9 4.5 %collective-permute-start.1 = (f32[16,128]{1,0:T(8,128)S(1)}, f32[16,128]{1,0:T(8,128)S(1)}, u32[]{:S(2)}, u32[]{:S(2)}) collective-permute-start(f32[16,128]{1,0:T(8,128)S(1)} %get-tuple-element.16.refs_1_), channel_id=1, source_target_pairs={{0,4},{4,0},{8,12},{12,8},{1,5},{5,1},{9,13},{13,9},{2,6},{6,2},{1... | collective-permute-start | bytes 24584 | tf_op jit(solution)/shard_map/ppermute | solution.py:288
  27.4 5.5 %collective-permute-start.4 = (f32[8,128]{1,0:T(8,128)S(1)}, f32[8,128]{1,0:T(8,128)S(1)}, u32[]{:S(2)}, u32[]{:S(2)}) collective-permute-start(f32[8,128]{1,0:T(8,128)S(1)} %get-tuple-element.19), channel_id=1, source_target_pairs={{0,12},{4,8},{8,4},{12,0},{1,13},{5,9},{9,5},{13,1},{2,14},{6,10},... | collective-permute-start | bytes 12296 | tf_op jit(solution)/shard_map/ppermute | solution.py:288
  29.3 4.5 %collective-permute-start.5 = (f32[8,128]{1,0:T(8,128)S(1)}, f32[8,128]{1,0:T(8,128)S(1)}, u32[]{:S(2)}, u32[]{:S(2)}) collective-permute-start(f32[8,128]{1,0:T(8,128)S(1)} %get-tuple-element.20), channel_id=1, source_target_pairs={{0,8},{4,12},{8,0},{12,4},{1,9},{5,13},{9,1},{13,5},{2,10},{6,14},... | collective-permute-start | bytes 12296 | tf_op jit(solution)/shard_map/ppermute | solution.py:288
  30.4 3.6 %collective-permute-start.6 = (f32[8,128]{1,0:T(8,128)S(1)}, f32[8,128]{1,0:T(8,128)S(1)}, u32[]{:S(2)}, u32[]{:S(2)}) collective-permute-start(f32[8,128]{1,0:T(8,128)S(1)} %get-tuple-element.21), channel_id=1, source_target_pairs={{0,4},{4,0},{8,12},{12,8},{1,5},{5,1},{9,13},{13,9},{2,6},{6,2},{1... | collective-permute-start | bytes 12296 | tf_op jit(solution)/shard_map/ppermute | solution.py:288

commit v5 on v4

v5 whole, which is shorter than its diff:
```python
import functools
import math

import jax
import jax.numpy as jnp
from jax import lax
from jax.experimental import pallas as pl
from jax.experimental.pallas import tpu as pltpu
from jax.sharding import PartitionSpec as P

ITERS = 2
LANES = 128


track_width = 0.0001
exp2_rate = -math.log2(math.e) / track_width


def off_diagonal(tiles):
    return tiles * (tiles - 1) // 2


def first_slot(a, tiles):
    return a * tiles - (a * (a + 1)) // 2


def for_each_pair(reach_tiles, class_ref, action):
    tiles = class_ref.shape[0]

    def one_pair(slot, carry):
        a = jnp.int32(0)
        for row in range(1, tiles - 1):
            a = a + (slot >= first_slot(row, tiles)).astype(jnp.int32)
        b = slot - first_slot(a, tiles) + a + 1
        pl.when(class_ref[a, b] < reach_tiles)(lambda: action(slot, a, b))
        return carry

    lax.fori_loop(0, off_diagonal(tiles), one_pair, 0)


def block_at(a, block_len):
    return pl.ds(pl.multiple_of(a * block_len, LANES), block_len)


def share_kernel(reach_tiles, class_hbm, pos_hbm, own_ref, mate_ref, share_ref, *scratch):
    class_ref, pos_ref, both, turned, column, arrived = scratch
    members, total_obs = own_ref.shape
    tiles = class_ref.shape[0]
    block_len = total_obs // tiles
    pos_copy = pltpu.make_async_copy(pos_hbm, pos_ref, arrived.at[0])
    own_copy = pltpu.make_async_copy(own_ref, both.at[pl.ds(0, members), :], arrived.at[1])
    class_copy = pltpu.make_async_copy(class_hbm, class_ref, arrived.at[2])
    for copy in (pos_copy, own_copy, class_copy):
        copy.start()
    both[members:, :] = mate_ref[...]
    turned[:, members:] = mate_ref[...].T
    pos_copy.wait()
    spread_columns(pos_ref[...], column)
    own_copy.wait()
    turned[:, :members] = both[:members, :].T
    class_copy.wait()
    rows = 128

    def make_tile(slot, a, b):
        rows_at, columns_at = block_at(a, block_len), block_at(b, block_len)
        right = both[:, columns_at]
        right_pos = pos_ref[:, columns_at]
        left_turned, left_column, tile = turned.at[rows_at, :], column.at[rows_at, :], share_ref.at[slot]
        for begin in range(0, block_len, rows):
            part = slice(begin, begin + rows)
            product = jnp.dot(left_turned[part, :], right, preferred_element_type=jnp.float32)
            left_pos = jnp.concatenate([left_column[part, :]] * (block_len // LANES), axis=1)
            distance = left_pos - right_pos
            tile[part, :] = product * jnp.exp2(distance * distance * exp2_rate)

    def make_diagonal(slot, carry):
        make_tile(slot, slot, slot)
        return carry

    lax.fori_loop(0, tiles, make_diagonal, 0)
    for_each_pair(reach_tiles, class_ref, lambda slot, a, b: make_tile(slot + tiles, a, b))


def spread_columns(row, column):
    for begin in range(0, column.shape[0], LANES):
        square = jnp.broadcast_to(row[:, begin : begin + LANES], (LANES, LANES))
        column[begin : begin + LANES, :] = square.T


def spread_vector(vector, column):
    for piece in range(vector.shape[0]):
        square = jnp.broadcast_to(vector[piece : piece + 1, :], (LANES, LANES))
        column[piece * LANES : (piece + 1) * LANES, :] = square.T


def tile_weight(klass, reach_tiles, inverse_members):
    return jnp.maximum(0.0, 1.0 - klass.astype(jnp.float32) / reach_tiles) * inverse_members


def add_sums(into, weight, totals):
    for lane, total in enumerate(totals):
        into[:, lane * LANES : (lane + 1) * LANES] += weight * total


def add_turned(into, weight, across):
    for lane in range(across.shape[0] // LANES):
        where = slice(lane * LANES, (lane + 1) * LANES)
        turned = across[where, :].T
        folded = turned[:8, :]
        for begin in range(8, LANES, 8):
            folded = folded + turned[begin : begin + 8, :]
        into[:, where] += weight * folded


def fold_sums(sums, out_ref):
    for piece in range(sums.shape[1] // LANES):
        out_ref[piece : piece + 1, :] = jnp.sum(sums[:, piece * LANES : (piece + 1) * LANES], axis=0, keepdims=True)


def apply_share(reach_tiles, inverse_members, class_ref, share_ref, vector, column, across, sums, out_ref):
    tiles = class_ref.shape[0]
    block_len = share_ref.shape[1]
    lanes = block_len // LANES
    sums[...] = jnp.zeros_like(sums)

    def add_diagonal(a, carry):
        at = block_at(a, block_len)
        tile, factor = share_ref.at[a], column.at[at, :]
        totals = [None] * lanes
        for begin in range(0, block_len, 8):
            part = slice(begin, begin + 8)
            for lane in range(lanes):
                term = tile[part, lane * LANES : (lane + 1) * LANES] * factor[part, :]
                totals[lane] = term if totals[lane] is None else totals[lane] + term
        add_sums(sums.at[:, at], tile_weight(class_ref[a, a], reach_tiles, inverse_members), totals)
        return carry

    def add_pair(slot, a, b):
        weight = tile_weight(class_ref[a, b], reach_tiles, inverse_members)
        at_a, at_b = block_at(a, block_len), block_at(b, block_len)
        tile, factor = share_ref.at[slot + tiles], column.at[at_a, :]
        rows_b = [jnp.broadcast_to(vector[pl.ds(b * lanes + lane, 1), :], (8, LANES)) for lane in range(lanes)]
        totals = [None] * lanes
        for begin in range(0, block_len, 8):
            part = slice(begin, begin + 8)
            line = None
            for lane in range(lanes):
                here = tile[part, lane * LANES : (lane + 1) * LANES]
                term = here * factor[part, :]
                totals[lane] = term if totals[lane] is None else totals[lane] + term
                term = here * rows_b[lane]
                line = term if line is None else line + term
            across[part, :] = line
        add_sums(sums.at[:, at_b], weight, totals)
        add_turned(sums.at[:, at_a], weight, across)

    lax.fori_loop(0, tiles, add_diagonal, 0)
    for_each_pair(reach_tiles, class_ref, add_pair)
    fold_sums(sums, out_ref)


def place():
    sub_count = lax.axis_size("sub")
    within = lax.axis_index("col") * sub_count + lax.axis_index("sub")
    return lax.axis_index("row"), within, lax.axis_size("col") * sub_count


def first_kernel(reach_tiles, inverse_members, masks, class_vmem, share_ref, error_ref, *refs):
    tiles = class_vmem.shape[0]
    chunks, refs = refs[:tiles], refs[tiles:]
    out_ref, class_ref, vector, column, across, sums, class_arrived = refs
    class_copy = pltpu.make_async_copy(class_vmem, class_ref, class_arrived)
    class_copy.start()
    row_index, within, per_row = place()
    block_len = share_ref.shape[1]
    lanes = block_len // LANES
    pieces = tiles * lanes
    for mask, chunk in zip(masks, chunks):
        vector[pl.ds(row_index ^ mask, 1), :] = chunk[...]
    spread_vector(vector, column)
    sums[...] = jnp.zeros_like(sums)
    chunk_at = pl.ds(pl.multiple_of(within * LANES, LANES), LANES)
    class_copy.wait()

    def sums_of_rows(tile, a):
        strip, factor = tile.at[chunk_at, :], column.at[pl.ds(pl.multiple_of(a * LANES, LANES), LANES), :]
        totals = [None] * lanes
        for begin in range(0, LANES, 8):
            part = slice(begin, begin + 8)
            for lane in range(lanes):
                term = strip[part, lane * LANES : (lane + 1) * LANES] * factor[part, :]
                totals[lane] = term if totals[lane] is None else totals[lane] + term
        return totals

    def add_diagonal(a, carry):
        weight = tile_weight(class_ref[a, a], reach_tiles, inverse_members)
        add_sums(sums.at[:, block_at(a, block_len)], weight, sums_of_rows(share_ref.at[a], a))
        return carry

    def add_pair(slot, a, b):
        weight = tile_weight(class_ref[a, b], reach_tiles, inverse_members)
        tile = share_ref.at[slot + tiles]
        add_sums(sums.at[:, block_at(b, block_len)], weight, sums_of_rows(tile, a))
        across[...] = tile[:, chunk_at] * vector[pl.ds(b, 1), :]
        add_turned(sums.at[:, block_at(a, block_len)], weight, across)

    lax.fori_loop(0, tiles, add_diagonal, 0)
    for_each_pair(reach_tiles, class_ref, add_pair)
    fold_sums(sums, out_ref)
    own = row_index * per_row + within
    out_ref[pl.ds(own, 1), :] += error_ref[...] * chunks[0][...]
    out_ref[pieces : pieces + tiles, :] = vector[...]
    out_ref[pieces + tiles : pieces + tiles + 1, :] = error_ref[...]


def middle_kernel(pieces, *refs):
    parts, out_ref = refs[:-1], refs[-1]
    total = parts[0][:pieces, :]
    for part in parts[1:]:
        total = total + part[:pieces, :]
    out_ref[...] = total


def gather_kernel(tiles, masks, *refs):
    parts, (innovations_ref, error_ref) = refs[:-2], refs[-2:]
    _, within, per_row = place()
    pieces = innovations_ref.shape[0]
    for mask, part in zip(masks, parts):
        there = within ^ mask
        for a in range(tiles):
            innovations_ref[pl.ds(a * per_row + there, 1), :] = part[pieces + a : pieces + a + 1, :]
        error_ref[pl.ds(there, 1), :] = part[pieces + tiles : pieces + tiles + 1, :]


def total_of(x):
    return jnp.sum(jnp.sum(x, axis=0, keepdims=True), axis=1, keepdims=True)


def second_kernel(reach_tiles, inverse_members, peers, class_vmem, share_ref, innovations_ref, error_ref, *refs):
    parts, refs = refs[:peers], refs[peers:]
    sent, refs = refs[:peers], refs[peers:]
    state_ref, class_ref, direction, residual, start, column, across, sums, product, class_arrived = refs
    class_copy = pltpu.make_async_copy(class_vmem, class_ref, class_arrived)
    class_copy.start()
    row_index, within, per_row = place()
    innovations = innovations_ref[...]
    image = parts[0][...]
    for part in parts[1:]:
        image = image + part[...]
    norm_now = total_of(innovations * innovations)
    alpha = norm_now / total_of(innovations * image)
    residual_now = innovations - alpha * image
    norm_next = total_of(residual_now * residual_now)
    direction_now = residual_now + (norm_next / norm_now) * innovations
    residual[...] = residual_now
    direction[...] = direction_now
    start[...] = alpha * innovations
    spread_vector(direction, column)
    class_copy.wait()
    shared = (class_ref, share_ref, direction, column, across, sums, product)
    apply_share(reach_tiles, inverse_members, *shared)
    of_row = direction[pl.ds(row_index * per_row, per_row), :]
    curvature = total_of(direction_now * product[...]) + total_of(error_ref[...] * of_row * of_row)
    for peer in range(peers):
        at = (row_index ^ peer) * per_row + within
        sent[peer][0:1, :] = product[pl.ds(at, 1), :]
        sent[peer][1:2, :] = jnp.broadcast_to(curvature, (1, LANES))
    own = pl.ds(row_index * per_row + within, 1)
    state_ref[0:1, :] = start[own, :]
    state_ref[1:2, :] = residual[own, :]
    state_ref[2:3, :] = direction[own, :]
    state_ref[3:4, :] = error_ref[pl.ds(within, 1), :] * direction[own, :]
    state_ref[4:5, :] = jnp.broadcast_to(norm_next, (1, LANES))


def last_kernel(state_ref, *refs):
    parts, (solution_ref, residual_ref) = refs[:-2], refs[-2:]
    image = state_ref[3:4, :] + parts[0][0:1, :]
    curvature = parts[0][1:2, :]
    for part in parts[1:]:
        image = image + part[0:1, :]
        curvature = curvature + part[1:2, :]
    alpha = state_ref[4:5, :] / curvature
    solution_ref[...] = state_ref[0:1, :] + alpha * state_ref[2:3, :]
    residual_ref[...] = state_ref[1:2, :] - alpha * image


VMEM_SPEC = pl.BlockSpec(memory_space=pltpu.VMEM)
SMEM_SPEC = pl.BlockSpec(memory_space=pltpu.SMEM)
HBM_SPEC = pl.BlockSpec(memory_space=pltpu.HBM)


def in_hbm(x):
    return pltpu.with_memory_space_constraint(x, pltpu.HBM)


def exchange(axes, masks, values):
    count = math.prod(lax.axis_size(axis) for axis in axes)
    return [
        lax.ppermute(value, axes, [(i, i ^ mask) for i in range(count)]) if mask else value
        for mask, value in zip(masks, values)
    ]


def nearest_first(count):
    return tuple(range(count))


def farthest_first(count):
    return (0,) + tuple(range(count - 1, 0, -1))


def vectors_only(anomalies, innovations, obs_error, track_pos, taper_class):
    row_count = lax.axis_size("row")
    sub_count = lax.axis_size("sub")
    per_row = lax.axis_size("col") * sub_count
    local_members, total_obs = anomalies.shape
    member_total = local_members * row_count * sub_count
    inverse_members = 1.0 / (member_total - 1)
    reach_tiles = max(2, row_count // 4)
    pieces = total_obs // LANES
    block_len = total_obs // row_count
    f32 = jnp.float32
    row, here = ("row",), ("col", "sub")
    params = pltpu.CompilerParams(vmem_limit_bytes=16 * 1024 * 1024)

    mate = lax.ppermute(anomalies, "sub", [(0, 1), (1, 0)])
    chunk = innovations.reshape(1, LANES)
    chunk_order = farthest_first(row_count)
    chunks = exchange(row, chunk_order, [chunk] * row_count)

    class_here = pltpu.SMEM(taper_class.shape, jnp.int32)
    work = [pltpu.VMEM((block_len, LANES), f32), pltpu.VMEM((8, total_obs), f32)]
    share = pl.pallas_call(
        functools.partial(share_kernel, reach_tiles),
        out_shape=pltpu.VMEM((row_count + off_diagonal(row_count), block_len, block_len), f32),
        in_specs=[HBM_SPEC] * 3 + [VMEM_SPEC],
        out_specs=VMEM_SPEC,
        scratch_shapes=[
            class_here,
            pltpu.VMEM((1, total_obs), f32),
            pltpu.VMEM((2 * local_members, total_obs), anomalies.dtype),
            pltpu.VMEM((total_obs, 2 * local_members), anomalies.dtype),
            pltpu.VMEM((total_obs, LANES), f32),
            pltpu.SemaphoreType.DMA((3,)),
        ],
        compiler_params=params,
        cost_estimate=pl.CostEstimate(
            flops=4 * local_members * total_obs * total_obs,
            bytes_accessed=4 * total_obs * total_obs,
            transcendentals=total_obs * total_obs,
        ),
        name="share",
    )(in_hbm(taper_class), in_hbm(track_pos.reshape(1, total_obs)), in_hbm(anomalies), mate)

    payload = pl.pallas_call(
        functools.partial(first_kernel, reach_tiles, inverse_members, chunk_order),
        out_shape=pltpu.VMEM((pieces + 8, LANES), f32),
        in_specs=[VMEM_SPEC] * (row_count + 3),
        out_specs=VMEM_SPEC,
        scratch_shapes=[class_here, pltpu.VMEM((row_count, LANES), f32), pltpu.VMEM((row_count * LANES, LANES), f32)]
        + work
        + [pltpu.SemaphoreType.DMA(())],
        compiler_params=params,
        name="first",
    )(taper_class, share, obs_error.reshape(1, LANES), *chunks)
    payload_order = farthest_first(per_row)
    payloads = exchange(here, payload_order, [payload] * per_row)
    part = pl.pallas_call(
        functools.partial(middle_kernel, pieces),
        out_shape=pltpu.VMEM((pieces, LANES), f32),
        in_specs=[VMEM_SPEC] * per_row,
        out_specs=VMEM_SPEC,
        compiler_params=params,
        name="middle",
    )(*payloads)
    parts = exchange(row, farthest_first(row_count), [part] * row_count)
    whole, error = pl.pallas_call(
        functools.partial(gather_kernel, row_count, payload_order),
        out_shape=[pltpu.VMEM((pieces, LANES), f32), pltpu.VMEM((per_row, LANES), f32)],
        in_specs=[VMEM_SPEC] * per_row,
        out_specs=[VMEM_SPEC] * 2,
        compiler_params=params,
        name="gather",
    )(*payloads)

    *sent, state = pl.pallas_call(
        functools.partial(second_kernel, reach_tiles, inverse_members, row_count),
        out_shape=[pltpu.VMEM((8, LANES), f32) for _ in range(row_count + 1)],
        in_specs=[VMEM_SPEC] * (row_count + 4),
        out_specs=[VMEM_SPEC] * (row_count + 1),
        scratch_shapes=[class_here]
        + [pltpu.VMEM((pieces, LANES), f32)] * 3
        + [pltpu.VMEM((total_obs, LANES), f32)]
        + work
        + [pltpu.VMEM((pieces, LANES), f32), pltpu.SemaphoreType.DMA(())],
        compiler_params=params,
        name="second",
    )(taper_class, share, whole, error, *parts)
    last_order = farthest_first(row_count)
    got = exchange(row, last_order, [sent[mask] for mask in last_order])
    solution_part, residual_part = pl.pallas_call(
        last_kernel,
        out_shape=[jax.ShapeDtypeStruct((1, LANES), f32)] * 2,
        in_specs=[VMEM_SPEC] * (row_count + 1),
        out_specs=[VMEM_SPEC] * 2,
        compiler_params=pltpu.CompilerParams(vmem_limit_bytes=1024 * 1024),
        name="last",
    )(state, *got)
    return solution_part.reshape(LANES), residual_part.reshape(LANES)


def fits(anomalies, innovations, obs_error, track_pos, taper_class):
    row_count = lax.axis_size("row")
    per_row = lax.axis_size("col") * lax.axis_size("sub")
    local_members, total_obs = anomalies.shape
    block_len = total_obs // row_count
    share_bytes = 4 * (row_count + off_diagonal(row_count)) * block_len * block_len
    return (
        ITERS == 2
        and row_count in (2, 4)
        and per_row in (2, 4)
        and lax.axis_size("sub") == 2
        and innovations.shape[0] == LANES
        and total_obs == row_count * per_row * LANES
        and local_members % LANES == 0
        and share_bytes <= 16 * 1024 * 1024
    )


def per_device(*args):
    return vectors_only(*args) if fits(*args) else blocks(*args)


def squares(residual):
    return lax.psum(jnp.sum(residual * residual), ("row", "col", "sub"))


def blocks(anomalies, innovations, obs_error, track_pos, taper_class):
    row_count = lax.axis_size("row")
    col_count = lax.axis_size("col")
    sub_count = lax.axis_size("sub")
    row_index = lax.axis_index("row")
    col_index = lax.axis_index("col")
    local_members, total_obs = anomalies.shape
    block_len = total_obs // row_count
    quarter_len = block_len // col_count
    member_total = local_members * row_count * sub_count
    inverse_members = 1.0 / (member_total - 1)
    reach_tiles = max(2, row_count // 4)
    class_row = lax.dynamic_index_in_dim(taper_class, row_index, 0, keepdims=False)
    tile_weight = jnp.maximum(0.0, 1.0 - class_row.astype(jnp.float32) / reach_tiles)
    row_pos = lax.dynamic_slice_in_dim(track_pos, row_index * block_len, block_len, 0)
    col_pos = lax.dynamic_index_in_dim(
        track_pos.reshape(row_count, col_count, quarter_len), col_index, 1, keepdims=False
    )
    own_block = lax.all_to_all(anomalies, "row", split_axis=1, concat_axis=0, tiled=True)
    own_quarter = lax.dynamic_slice_in_dim(own_block, col_index * quarter_len, quarter_len, 1)

    def one_tile(piece, block_index, keep_factor):
        product = jnp.einsum("mi,mq->iq", own_block, piece, preferred_element_type=jnp.float32)
        column_pos = lax.dynamic_index_in_dim(col_pos, block_index, 0, keepdims=False)
        weight_here = lax.dynamic_index_in_dim(tile_weight, block_index, 0, keepdims=False)
        distance = row_pos[:, None] - column_pos[None, :]
        taper = weight_here * keep_factor * jnp.exp(-(distance * distance) / track_width)
        return product * (taper * inverse_members)

    def one_entry(entry):
        return one_tile(entry[0], entry[1], 1.0)

    piece = lax.all_gather(own_quarter[None], "row", axis=0, tiled=True)
    indices = jnp.arange(piece.shape[0], dtype=jnp.int32)
    tiles = lax.map(one_entry, (piece, indices))
    solution = jnp.zeros_like(innovations)
    residual = innovations
    direction_vec = innovations
    norm_now = squares(residual)
    for turn_index in range(ITERS):
        column_vec = lax.all_gather(direction_vec, ("row", "sub"), axis=0, tiled=True).reshape(
            row_count, quarter_len
        )
        direct = jnp.einsum("jiq,jq->i", tiles, column_vec, precision=lax.Precision.HIGHEST)
        extra = obs_error * direction_vec
        own_part = lax.psum_scatter(direct, ("col", "sub"), scatter_dimension=0, tiled=True)
        image = own_part + extra
        alpha = norm_now / lax.psum(jnp.sum(direction_vec * image), ("row", "col", "sub"))
        solution = solution + alpha * direction_vec
        residual = residual - alpha * image
        if turn_index + 1 < ITERS:
            norm_next = squares(residual)
            direction_vec = residual + norm_next / norm_now * direction_vec
            norm_now = norm_next
    return (solution, residual)


def solution(mesh):
    in_specs = (
        P(("group", "row", "sub"), None),
        P(("group", "row", "col", "sub")),
        P(("group", "row", "col", "sub")),
        P("group"),
        P("group", None),
    )
    out_specs = (P(("group", "row", "col", "sub")), P(("group", "row", "col", "sub")))
    return jax.shard_map(
        per_device, mesh=mesh, in_specs=in_specs, out_specs=out_specs, check_vma=False
    )
```

time: 34.8 us -> 33.3 us (0.957)
  Pallas kernels: 9.88 us -> 7.6 us
  waiting for transfers between devices: 6.03 us -> 8.14 us
  local copies, waits for them, and re-layouts: 0.8 us -> 0.01 us
  other arithmetic: 0.68 us -> 0 us
    ppermute x6 -> x12, starting transfers between devices: 8.91 us -> 16.2 us  [exchange(): lax.ppermute(value, axes, [(i, i ^ mask) for i in range(count)])]
    all_to_all x1 -> x0, starting transfers between devices: 7.02 us -> none  [vectors_only(): lax.all_to_all(packed, ('row', 'col', 'sub'), split_axis=0, concat_axis=0...]
    ppermute x6 -> x12, waiting for transfers between devices: 4.33 us -> 8.13 us  [exchange(): lax.ppermute(value, axes, [(i, i ^ mask) for i in range(count)])]
    all_to_all x1 -> x0, waiting for transfers between devices: 1.7 us -> none  [vectors_only(): lax.all_to_all(packed, ('row', 'col', 'sub'), split_axis=0, concat_axis=0...]
    pallas_call x1, Pallas kernels: 2.8 us -> 1.35 us  [vectors_only(): pl.pallas_call(functools.partial(first_kernel, reach_tiles, inverse_membe...]
    pallas_call x2 -> x3, Pallas kernels: 4.57 us -> 3.74 us  [the longest x1 3.73 us: vectors_only(): pl.pallas_call(functools.partial(share_kernel, reach_tiles), out_shape=pl...]
    unnamed x4 -> x6, local copies, waits for them, and re-layouts: 0.8 us -> 0.01 us
    concatenate x1 -> x0, other arithmetic: 0.68 us -> none  [vectors_only(): jnp.concatenate([innovations, obs_error]).reshape(1, 2 * LANES)]
  transfers between devices with their start and end apart: 8 -> 13, of which waited for: 6 -> 7; matrix products, arithmetic and copies ran while one was open for 2% -> 0% of each run, Pallas kernels for 13% -> 11%
where the time goes in v5:
time: 33.3 us; the launch traced here: 33.1 us
  starting transfers between devices  16.7 us (50%)
  waiting for transfers between devices  8.14 us (24%)
  Pallas kernels  7.6 us (23%)
  between operations  0.72 us (2%)
    ppermute x12, starting transfers between devices, exchange(): lax.ppermute(value, axes, [(i, i ^ mask) for i in range(count)])  16.2 us
    ppermute x12, waiting for transfers between devices, exchange(): lax.ppermute(value, axes, [(i, i ^ mask) for i in range(count)])  8.13 us
    pallas_call x1, Pallas kernels, vectors_only(): pl.pallas_call(functools.partial(share_kernel, reach_tiles), out_shape=pl...  3.73 us
    pallas_call x1, Pallas kernels, vectors_only(): pl.pallas_call(functools.partial(second_kernel, reach_tiles, inverse_memb...  1.97 us
    pallas_call x1, Pallas kernels, vectors_only(): pl.pallas_call(functools.partial(first_kernel, reach_tiles, inverse_membe...  1.35 us
  transfers between devices with their start and end apart: 13, of which 7 were waited for; matrix products, arithmetic and copies ran while one was open for 0% of the time, Pallas kernels for 11%

profile of v5, /device:TPU:0, one launch (start us, length us, event | category | flops | bytes accessed | tf_op | source)
XLA Modules:
  0.0 33.1 jit_solution(8575828053276644212)
XLA Ops:
  0.7 0.5 %collective-permute-start = (bf16[128,2048]{1,0:T(8,128)(2,1)}, bf16[128,2048]{1,0:T(8,128)(2,1)S(1)}, u32[]{:S(2)}, u32[]{:S(2)}) collective-permute-start(bf16[128,2048]{1,0:T(8,128)(2,1)} %own_ref.1), channel_id=1, source_target_pairs={{0,1},{1,0},{2,3},{3,2},{4,5},{5,4},{6,7},{7,6},{8,9},{9,8},{10,11... | collective-permute-start | bytes 1572872 | tf_op jit(solution)/shard_map/ppermute | solution.py:327
  1.2 4.7 %collective-permute-start.1 = (f32[1,128]{1,0:T(1,128)}, f32[1,128]{1,0:T(1,128)S(1)}, u32[]{:S(2)}, u32[]{:S(2)}) collective-permute-start(f32[1,128]{1,0:T(1,128)} %bitcast.6), channel_id=1, source_target_pairs={{0,12},{4,8},{8,4},{12,0},{1,13},{5,9},{9,5},{13,1},{2,14},{6,10},... | collective-permute-start | bytes 1544 | tf_op jit(solution)/shard_map/ppermute | solution.py:300
  5.9 0.0 collective-permute-start.2
  5.9 0.7 %collective-permute-start.3 = (f32[1,128]{1,0:T(1,128)}, f32[1,128]{1,0:T(1,128)S(1)}, u32[]{:S(2)}, u32[]{:S(2)}) collective-permute-start(f32[1,128]{1,0:T(1,128)} %bitcast.8), channel_id=1, source_target_pairs={{0,4},{4,0},{8,12},{12,8},{1,5},{5,1},{9,13},{13,9},{2,6},{6,2},{1... | collective-permute-start | bytes 1544 | tf_op jit(solution)/shard_map/ppermute | solution.py:300
  6.5 3.7 %share.1.share_ref = f32[10,512,512]{2,1,0:T(8,128)S(1)} custom-call(s32[4,4]{1,0:T(4,128)} %class_vmem.3, f32[1,2048]{1,0:T(1,128)} %bitcast.10, bf16[128,2048]{1,0:T(8,128)(2,1)} %own_ref.1, bf16[128,2048]{1,0:T(8,128)(2,1)S(1)} %collective-permute-done.mate_ref), custom_call_target="tpu_custom_call" | custom-call | flops 2147483648 | bytes 16777216 | tf_op jit(solution)/shard_map/share/pallas_call | solution.py:334
  10.3 0.2 collective-permute-done.2.refs_2_
  10.4 1.4 %first.1.refs_0_ = f32[24,128]{1,0:T(8,128)S(1)} custom-call(s32[4,4]{1,0:T(4,128)S(1)} %copy-done, f32[10,512,512]{2,1,0:T(8,128)S(1)} %share.1.share_ref, f32[1,128]{1,0:T(1,128)S(1)} %bitcast.5, f32[1,128]{1,0:T(1,128)S(1)} %bitcast.9, f32[1,128]{1,0:T(1,128)S(1)} %collective-permute-done.1.refs_1_, f32[1,128]{1,0:T(1,128)S(1)} %collective-permute-done.2.refs_2_, ...), custom_call_target="tpu_custom_call" | custom-call | tf_op jit(solution)/shard_map/first/pallas_call | solution.py:356
  11.8 0.8 %collective-permute-start.4 = (f32[24,128]{1,0:T(8,128)S(1)}, f32[24,128]{1,0:T(8,128)S(1)}, u32[]{:S(2)}, u32[]{:S(2)}) collective-permute-start(f32[24,128]{1,0:T(8,128)S(1)} %first.1.refs_0_), channel_id=1, source_target_pairs={{0,3},{1,2},{2,1},{3,0},{4,7},{5,6},{6,5},{7,4},{8,11},{9,10},{10,... | collective-permute-start | bytes 36872 | tf_op jit(solution)/shard_map/ppermute | solution.py:300
  12.6 0.8 %collective-permute-start.5 = (f32[24,128]{1,0:T(8,128)S(1)}, f32[24,128]{1,0:T(8,128)S(1)}, u32[]{:S(2)}, u32[]{:S(2)}) collective-permute-start(f32[24,128]{1,0:T(8,128)S(1)} %first.1.refs_0_), channel_id=1, source_target_pairs={{0,2},{1,3},{2,0},{3,1},{4,6},{5,7},{6,4},{7,5},{8,10},{9,11},{10,... | collective-permute-start | bytes 36872 | tf_op jit(solution)/shard_map/ppermute | solution.py:300
  13.4 0.3 collective-permute-start.6
  13.7 1.3 %collective-permute-done.4.refs_1_ = f32[24,128]{1,0:T(8,128)S(1)} collective-permute-done((f32[24,128]{1,0:T(8,128)S(1)}, f32[24,128]{1,0:T(8,128)S(1)}, u32[]{:S(2)}, u32[]{:S(2)}) %collective-permute-start.4) | collective-permute-done | bytes 12320 | tf_op jit(solution)/shard_map/ppermute | solution.py:300
  15.1 1.3 %collective-permute-done.5.refs_2_ = f32[24,128]{1,0:T(8,128)S(1)} collective-permute-done((f32[24,128]{1,0:T(8,128)S(1)}, f32[24,128]{1,0:T(8,128)S(1)}, u32[]{:S(2)}, u32[]{:S(2)}) %collective-permute-start.5) | collective-permute-done | bytes 12320 | tf_op jit(solution)/shard_map/ppermute | solution.py:300
  16.4 3.6 %collective-permute-start.7 = (f32[16,128]{1,0:T(8,128)S(1)}, f32[16,128]{1,0:T(8,128)S(1)}, u32[]{:S(2)}, u32[]{:S(2)}) collective-permute-start(f32[16,128]{1,0:T(8,128)S(1)} %middle.1.refs_0_), channel_id=1, source_target_pairs={{0,12},{4,8},{8,4},{12,0},{1,13},{5,9},{9,5},{13,1},{2,14},{6,10},... | collective-permute-start | bytes 24584 | tf_op jit(solution)/shard_map/ppermute | solution.py:300
  20.0 0.8 %collective-permute-start.9 = (f32[16,128]{1,0:T(8,128)S(1)}, f32[16,128]{1,0:T(8,128)S(1)}, u32[]{:S(2)}, u32[]{:S(2)}) collective-permute-start(f32[16,128]{1,0:T(8,128)S(1)} %middle.1.refs_0_), channel_id=1, source_target_pairs={{0,4},{4,0},{8,12},{12,8},{1,5},{5,1},{9,13},{13,9},{2,6},{6,2},{1... | collective-permute-start | bytes 24584 | tf_op jit(solution)/shard_map/ppermute | solution.py:300
  20.8 1.0 %collective-permute-done.7.refs_1_ = f32[16,128]{1,0:T(8,128)S(1)} collective-permute-done((f32[16,128]{1,0:T(8,128)S(1)}, f32[16,128]{1,0:T(8,128)S(1)}, u32[]{:S(2)}, u32[]{:S(2)}) %collective-permute-start.7) | collective-permute-done | bytes 8224 | tf_op jit(solution)/shard_map/ppermute | solution.py:300
  21.9 2.7 %collective-permute-done.8.refs_2_ = f32[16,128]{1,0:T(8,128)S(1)} collective-permute-done((f32[16,128]{1,0:T(8,128)S(1)}, f32[16,128]{1,0:T(8,128)S(1)}, u32[]{:S(2)}, u32[]{:S(2)}) %collective-permute-start.8) | collective-permute-done | bytes 8224 | tf_op jit(solution)/shard_map/ppermute | solution.py:300
  24.6 2.0 %second.1 = (f32[8,128]{1,0:T(8,128)S(1)}, f32[8,128]{1,0:T(8,128)S(1)}, f32[8,128]{1,0:T(8,128)S(1)}, f32[8,128]{1,0:T(8,128)S(1)}, f32[8,128]{1,0:T(8,128)S(1)}) custom-call(s32[4,4]{1,0:T(4,128)S(1)} %copy-done, f32[10,512,512]{2,1,0:T(8,128)S(1)} %share.1.share_ref, f32[16,128]{1,0:T(8,128)S(1)} %get-tuple-element.11.innovations_ref, ...), custom_call_target="tpu_custom_call" | custom-call | tf_op jit(solution)/shard_map/second/pallas_call | solution.py:387
  26.5 1.5 %collective-permute-start.10 = (f32[8,128]{1,0:T(8,128)S(1)}, f32[8,128]{1,0:T(8,128)S(1)}, u32[]{:S(2)}, u32[]{:S(2)}) collective-permute-start(f32[8,128]{1,0:T(8,128)S(1)} %get-tuple-element.15), channel_id=1, source_target_pairs={{0,12},{4,8},{8,4},{12,0},{1,13},{5,9},{9,5},{13,1},{2,14},{6,10},... | collective-permute-start | bytes 12296 | tf_op jit(solution)/shard_map/ppermute | solution.py:300
  28.1 0.6 %collective-permute-start.11 = (f32[8,128]{1,0:T(8,128)S(1)}, f32[8,128]{1,0:T(8,128)S(1)}, u32[]{:S(2)}, u32[]{:S(2)}) collective-permute-start(f32[8,128]{1,0:T(8,128)S(1)} %get-tuple-element.16), channel_id=1, source_target_pairs={{0,8},{4,12},{8,0},{12,4},{1,9},{5,13},{9,1},{13,5},{2,10},{6,14},... | collective-permute-start | bytes 12296 | tf_op jit(solution)/shard_map/ppermute | solution.py:300
  28.7 2.3 %collective-permute-start.12 = (f32[8,128]{1,0:T(8,128)S(1)}, f32[8,128]{1,0:T(8,128)S(1)}, u32[]{:S(2)}, u32[]{:S(2)}) collective-permute-start(f32[8,128]{1,0:T(8,128)S(1)} %get-tuple-element.17), channel_id=1, source_target_pairs={{0,4},{4,0},{8,12},{12,8},{1,5},{5,1},{9,13},{13,9},{2,6},{6,2},{1... | collective-permute-start | bytes 12296 | tf_op jit(solution)/shard_map/ppermute | solution.py:300
  31.0 1.0 %collective-permute-done.10.refs_1_ = f32[8,128]{1,0:T(8,128)S(1)} collective-permute-done((f32[8,128]{1,0:T(8,128)S(1)}, f32[8,128]{1,0:T(8,128)S(1)}, u32[]{:S(2)}, u32[]{:S(2)}) %collective-permute-start.10) | collective-permute-done | bytes 4128 | tf_op jit(solution)/shard_map/ppermute | solution.py:300
  32.0 0.6 %collective-permute-done.11.refs_2_ = f32[8,128]{1,0:T(8,128)S(1)} collective-permute-done((f32[8,128]{1,0:T(8,128)S(1)}, f32[8,128]{1,0:T(8,128)S(1)}, u32[]{:S(2)}, u32[]{:S(2)}) %collective-permute-start.11) | collective-permute-done | bytes 4128 | tf_op jit(solution)/shard_map/ppermute | solution.py:300
  32.6 0.0 collective-permute-done.12.refs_3_
  32.6 0.5 %last.1 = (f32[1,128]{1,0:T(1,128)}, f32[1,128]{1,0:T(1,128)}) custom-call(f32[8,128]{1,0:T(8,128)S(1)} %get-tuple-element.13.state_ref, f32[8,128]{1,0:T(8,128)S(1)} %get-tuple-element.14.refs_0_, f32[8,128]{1,0:T(8,128)S(1)} %collective-permute-done.10.refs_1_, f32[8,128]{1,0:T(8,128)S(1)} %collective-permute-done.11.refs_2_, ...), custom_call_target="tpu_custom_call" | custom-call | tf_op jit(solution)/shard_map/last/pallas_call | solution.py:402
  (14 shorter events, 0.0 us)
Async XLA Ops:
  0.6 9.8 %copy-start.2 = (f32[128]{0:T(128)S(1)}, f32[128]{0:T(128)}, u32[]{:S(2)}) copy-start(f32[128]{0:T(128)} %param.6) | copy-start | bytes 1540
  0.6 9.8 %copy-start = (s32[4,4]{1,0:T(4,128)S(1)}, s32[4,4]{1,0:T(4,128)}, u32[]{:S(2)}) copy-start(s32[4,4]{1,0:T(4,128)} %class_vmem.3) | copy-start | bytes 196
  0.7 9.8 %copy-start.1 = (f32[128]{0:T(128)S(1)}, f32[128]{0:T(128)}, u32[]{:S(2)}) copy-start(f32[128]{0:T(128)} %param.7) | copy-start | bytes 1540
  0.7 5.9 %collective-permute-start = (bf16[128,2048]{1,0:T(8,128)(2,1)}, bf16[128,2048]{1,0:T(8,128)(2,1)S(1)}, u32[]{:S(2)}, u32[]{:S(2)}) collective-permute-start(bf16[128,2048]{1,0:T(8,128)(2,1)} %own_ref.1), channel_id=1, source_target_pairs={{0,1},{1,0},{2,3},{3,2},{4,5},{5,4},{6,7},{7,6},{8,9},{9,8},{10,11... | collective-permute-start | bytes 1572872 | tf_op jit(solution)/shard_map/ppermute | solution.py:327
  1.2 9.1 %collective-permute-start.1 = (f32[1,128]{1,0:T(1,128)}, f32[1,128]{1,0:T(1,128)S(1)}, u32[]{:S(2)}, u32[]{:S(2)}) collective-permute-start(f32[1,128]{1,0:T(1,128)} %bitcast.6), channel_id=1, source_target_pairs={{0,12},{4,8},{8,4},{12,0},{1,13},{5,9},{9,5},{13,1},{2,14},{6,10},... | collective-permute-start | bytes 1544 | tf_op jit(solution)/shard_map/ppermute | solution.py:300
  5.9 4.6 %collective-permute-start.2 = (f32[1,128]{1,0:T(1,128)}, f32[1,128]{1,0:T(1,128)S(1)}, u32[]{:S(2)}, u32[]{:S(2)}) collective-permute-start(f32[1,128]{1,0:T(1,128)} %bitcast.7), channel_id=1, source_target_pairs={{0,8},{4,12},{8,0},{12,4},{1,9},{5,13},{9,1},{13,5},{2,10},{6,14},... | collective-permute-start | bytes 1544 | tf_op jit(solution)/shard_map/ppermute | solution.py:300
  5.9 4.6 %collective-permute-start.3 = (f32[1,128]{1,0:T(1,128)}, f32[1,128]{1,0:T(1,128)S(1)}, u32[]{:S(2)}, u32[]{:S(2)}) collective-permute-start(f32[1,128]{1,0:T(1,128)} %bitcast.8), channel_id=1, source_target_pairs={{0,4},{4,0},{8,12},{12,8},{1,5},{5,1},{9,13},{13,9},{2,6},{6,2},{1... | collective-permute-start | bytes 1544 | tf_op jit(solution)/shard_map/ppermute | solution.py:300
  11.8 3.3 %collective-permute-start.4 = (f32[24,128]{1,0:T(8,128)S(1)}, f32[24,128]{1,0:T(8,128)S(1)}, u32[]{:S(2)}, u32[]{:S(2)}) collective-permute-start(f32[24,128]{1,0:T(8,128)S(1)} %first.1.refs_0_), channel_id=1, source_target_pairs={{0,3},{1,2},{2,1},{3,0},{4,7},{5,6},{6,5},{7,4},{8,11},{9,10},{10,... | collective-permute-start | bytes 36872 | tf_op jit(solution)/shard_map/ppermute | solution.py:300
  12.6 3.7 %collective-permute-start.5 = (f32[24,128]{1,0:T(8,128)S(1)}, f32[24,128]{1,0:T(8,128)S(1)}, u32[]{:S(2)}, u32[]{:S(2)}) collective-permute-start(f32[24,128]{1,0:T(8,128)S(1)} %first.1.refs_0_), channel_id=1, source_target_pairs={{0,2},{1,3},{2,0},{3,1},{4,6},{5,7},{6,4},{7,5},{8,10},{9,11},{10,... | collective-permute-start | bytes 36872 | tf_op jit(solution)/shard_map/ppermute | solution.py:300
  13.4 2.9 %collective-permute-start.6 = (f32[24,128]{1,0:T(8,128)S(1)}, f32[24,128]{1,0:T(8,128)S(1)}, u32[]{:S(2)}, u32[]{:S(2)}) collective-permute-start(f32[24,128]{1,0:T(8,128)S(1)} %first.1.refs_0_), channel_id=1, source_target_pairs={{0,1},{1,0},{2,3},{3,2},{4,5},{5,4},{6,7},{7,6},{8,9},{9,8},{10,11... | collective-permute-start | bytes 36872 | tf_op jit(solution)/shard_map/ppermute | solution.py:300
  16.4 5.5 %collective-permute-start.7 = (f32[16,128]{1,0:T(8,128)S(1)}, f32[16,128]{1,0:T(8,128)S(1)}, u32[]{:S(2)}, u32[]{:S(2)}) collective-permute-start(f32[16,128]{1,0:T(8,128)S(1)} %middle.1.refs_0_), channel_id=1, source_target_pairs={{0,12},{4,8},{8,4},{12,0},{1,13},{5,9},{9,5},{13,1},{2,14},{6,10},... | collective-permute-start | bytes 24584 | tf_op jit(solution)/shard_map/ppermute | solution.py:300
  20.0 4.5 %collective-permute-start.8 = (f32[16,128]{1,0:T(8,128)S(1)}, f32[16,128]{1,0:T(8,128)S(1)}, u32[]{:S(2)}, u32[]{:S(2)}) collective-permute-start(f32[16,128]{1,0:T(8,128)S(1)} %middle.1.refs_0_), channel_id=1, source_target_pairs={{0,8},{4,12},{8,0},{12,4},{1,9},{5,13},{9,1},{13,5},{2,10},{6,14},... | collective-permute-start | bytes 24584 | tf_op jit(solution)/shard_map/ppermute | solution.py:300
  20.0 4.5 %collective-permute-start.9 = (f32[16,128]{1,0:T(8,128)S(1)}, f32[16,128]{1,0:T(8,128)S(1)}, u32[]{:S(2)}, u32[]{:S(2)}) collective-permute-start(f32[16,128]{1,0:T(8,128)S(1)} %middle.1.refs_0_), channel_id=1, source_target_pairs={{0,4},{4,0},{8,12},{12,8},{1,5},{5,1},{9,13},{13,9},{2,6},{6,2},{1... | collective-permute-start | bytes 24584 | tf_op jit(solution)/shard_map/ppermute | solution.py:300
  26.5 5.5 %collective-permute-start.10 = (f32[8,128]{1,0:T(8,128)S(1)}, f32[8,128]{1,0:T(8,128)S(1)}, u32[]{:S(2)}, u32[]{:S(2)}) collective-permute-start(f32[8,128]{1,0:T(8,128)S(1)} %get-tuple-element.15), channel_id=1, source_target_pairs={{0,12},{4,8},{8,4},{12,0},{1,13},{5,9},{9,5},{13,1},{2,14},{6,10},... | collective-permute-start | bytes 12296 | tf_op jit(solution)/shard_map/ppermute | solution.py:300
  28.1 4.5 %collective-permute-start.11 = (f32[8,128]{1,0:T(8,128)S(1)}, f32[8,128]{1,0:T(8,128)S(1)}, u32[]{:S(2)}, u32[]{:S(2)}) collective-permute-start(f32[8,128]{1,0:T(8,128)S(1)} %get-tuple-element.16), channel_id=1, source_target_pairs={{0,8},{4,12},{8,0},{12,4},{1,9},{5,13},{9,1},{13,5},{2,10},{6,14},... | collective-permute-start | bytes 12296 | tf_op jit(solution)/shard_map/ppermute | solution.py:300
  28.7 3.9 %collective-permute-start.12 = (f32[8,128]{1,0:T(8,128)S(1)}, f32[8,128]{1,0:T(8,128)S(1)}, u32[]{:S(2)}, u32[]{:S(2)}) collective-permute-start(f32[8,128]{1,0:T(8,128)S(1)} %get-tuple-element.17), channel_id=1, source_target_pairs={{0,4},{4,0},{8,12},{12,8},{1,5},{5,1},{9,13},{13,9},{2,6},{6,2},{1... | collective-permute-start | bytes 12296 | tf_op jit(solution)/shard_map/ppermute | solution.py:300

commit v6 on v5

--- a/solution.py
+++ b/solution.py
@@ -42,15 +42,20 @@
     return pl.ds(pl.multiple_of(a * block_len, LANES), block_len)
 
 
-def share_kernel(reach_tiles, class_hbm, pos_hbm, own_ref, mate_ref, share_ref, *scratch):
-    class_ref, pos_ref, both, turned, column, arrived = scratch
+def share_kernel(
+    reach_tiles, class_hbm, pos_hbm, chunk_hbm, error_hbm, own_ref, mate_ref, share_ref, class_ref, chunk_ref, error_ref,
+    *scratch
+):
+    pos_ref, both, turned, column, arrived = scratch
     members, total_obs = own_ref.shape
     tiles = class_ref.shape[0]
     block_len = total_obs // tiles
     pos_copy = pltpu.make_async_copy(pos_hbm, pos_ref, arrived.at[0])
     own_copy = pltpu.make_async_copy(own_ref, both.at[pl.ds(0, members), :], arrived.at[1])
     class_copy = pltpu.make_async_copy(class_hbm, class_ref, arrived.at[2])
-    for copy in (pos_copy, own_copy, class_copy):
+    chunk_copy = pltpu.make_async_copy(chunk_hbm, chunk_ref, arrived.at[3])
+    error_copy = pltpu.make_async_copy(error_hbm, error_ref, arrived.at[4])
+    for copy in (pos_copy, own_copy, class_copy, chunk_copy, error_copy):
         copy.start()
     both[members:, :] = mate_ref[...]
     turned[:, members:] = mate_ref[...].T
@@ -58,7 +63,8 @@
     spread_columns(pos_ref[...], column)
     own_copy.wait()
     turned[:, :members] = both[:members, :].T
-    class_copy.wait()
+    for copy in (class_copy, chunk_copy, error_copy):
+        copy.wait()
     rows = 128
 
     def make_tile(slot, a, b):
@@ -165,12 +171,10 @@
     return lax.axis_index("row"), within, lax.axis_size("col") * sub_count
 
 
-def first_kernel(reach_tiles, inverse_members, masks, class_vmem, share_ref, error_ref, *refs):
-    tiles = class_vmem.shape[0]
+def first_kernel(reach_tiles, inverse_members, masks, class_ref, share_ref, error_ref, *refs):
+    tiles = class_ref.shape[0]
     chunks, refs = refs[:tiles], refs[tiles:]
-    out_ref, class_ref, vector, column, across, sums, class_arrived = refs
-    class_copy = pltpu.make_async_copy(class_vmem, class_ref, class_arrived)
-    class_copy.start()
+    out_ref, vector, column, across, sums = refs
     row_index, within, per_row = place()
     block_len = share_ref.shape[1]
     lanes = block_len // LANES
@@ -180,7 +184,6 @@
     spread_vector(vector, column)
     sums[...] = jnp.zeros_like(sums)
     chunk_at = pl.ds(pl.multiple_of(within * LANES, LANES), LANES)
-    class_copy.wait()
 
     def sums_of_rows(tile, a):
         strip, factor = tile.at[chunk_at, :], column.at[pl.ds(pl.multiple_of(a * LANES, LANES), LANES), :]
@@ -236,12 +239,10 @@
     return jnp.sum(jnp.sum(x, axis=0, keepdims=True), axis=1, keepdims=True)
 
 
-def second_kernel(reach_tiles, inverse_members, peers, class_vmem, share_ref, innovations_ref, error_ref, *refs):
+def second_kernel(reach_tiles, inverse_members, peers, class_ref, share_ref, innovations_ref, error_ref, *refs):
     parts, refs = refs[:peers], refs[peers:]
     sent, refs = refs[:peers], refs[peers:]
-    state_ref, class_ref, direction, residual, start, column, across, sums, product, class_arrived = refs
-    class_copy = pltpu.make_async_copy(class_vmem, class_ref, class_arrived)
-    class_copy.start()
+    state_ref, direction, residual, start, column, across, sums, product = refs
     row_index, within, per_row = place()
     innovations = innovations_ref[...]
     image = parts[0][...]
@@ -256,7 +257,6 @@
     direction[...] = direction_now
     start[...] = alpha * innovations
     spread_vector(direction, column)
-    class_copy.wait()
     shared = (class_ref, share_ref, direction, column, across, sums, product)
     apply_share(reach_tiles, inverse_members, *shared)
     of_row = direction[pl.ds(row_index * per_row, per_row), :]
@@ -326,23 +326,27 @@
 
     mate = lax.ppermute(anomalies, "sub", [(0, 1), (1, 0)])
     chunk = innovations.reshape(1, LANES)
+    error = obs_error.reshape(1, LANES)
     chunk_order = farthest_first(row_count)
     chunks = exchange(row, chunk_order, [chunk] * row_count)
 
-    class_here = pltpu.SMEM(taper_class.shape, jnp.int32)
     work = [pltpu.VMEM((block_len, LANES), f32), pltpu.VMEM((8, total_obs), f32)]
-    share = pl.pallas_call(
+    share, classes, own_chunk, own_error = pl.pallas_call(
         functools.partial(share_kernel, reach_tiles),
-        out_shape=pltpu.VMEM((row_count + off_diagonal(row_count), block_len, block_len), f32),
-        in_specs=[HBM_SPEC] * 3 + [VMEM_SPEC],
-        out_specs=VMEM_SPEC,
+        out_shape=[
+            pltpu.VMEM((row_count + off_diagonal(row_count), block_len, block_len), f32),
+            pltpu.SMEM(taper_class.shape, jnp.int32),
+            pltpu.VMEM((1, LANES), f32),
+            pltpu.VMEM((1, LANES), f32),
+        ],
+        in_specs=[HBM_SPEC] * 5 + [VMEM_SPEC],
+        out_specs=[VMEM_SPEC, SMEM_SPEC, VMEM_SPEC, VMEM_SPEC],
         scratch_shapes=[
-            class_here,
             pltpu.VMEM((1, total_obs), f32),
             pltpu.VMEM((2 * local_members, total_obs), anomalies.dtype),
             pltpu.VMEM((total_obs, 2 * local_members), anomalies.dtype),
             pltpu.VMEM((total_obs, LANES), f32),
-            pltpu.SemaphoreType.DMA((3,)),
+            pltpu.SemaphoreType.DMA((5,)),
         ],
         compiler_params=params,
         cost_estimate=pl.CostEstimate(
@@ -351,19 +355,18 @@
             transcendentals=total_obs * total_obs,
         ),
         name="share",
-    )(in_hbm(taper_class), in_hbm(track_pos.reshape(1, total_obs)), in_hbm(anomalies), mate)
+    )(*[in_hbm(x) for x in (taper_class, track_pos.reshape(1, total_obs), chunk, error, anomalies)], mate)
 
     payload = pl.pallas_call(
         functools.partial(first_kernel, reach_tiles, inverse_members, chunk_order),
         out_shape=pltpu.VMEM((pieces + 8, LANES), f32),
-        in_specs=[VMEM_SPEC] * (row_count + 3),
+        in_specs=[SMEM_SPEC] + [VMEM_SPEC] * (row_count + 2),
         out_specs=VMEM_SPEC,
-        scratch_shapes=[class_here, pltpu.VMEM((row_count, LANES), f32), pltpu.VMEM((row_count * LANES, LANES), f32)]
-        + work
-        + [pltpu.SemaphoreType.DMA(())],
+        scratch_shapes=[pltpu.VMEM((row_count, LANES), f32), pltpu.VMEM((row_count * LANES, LANES), f32)]
+        + work,
         compiler_params=params,
         name="first",
-    )(taper_class, share, obs_error.reshape(1, LANES), *chunks)
+    )(classes, share, own_error, own_chunk, *chunks[1:])
     payload_order = farthest_first(per_row)
     payloads = exchange(here, payload_order, [payload] * per_row)
     part = pl.pallas_call(
@@ -387,16 +390,15 @@
     *sent, state = pl.pallas_call(
         functools.partial(second_kernel, reach_tiles, inverse_members, row_count),
         out_shape=[pltpu.VMEM((8, LANES), f32) for _ in range(row_count + 1)],
-        in_specs=[VMEM_SPEC] * (row_count + 4),
+        in_specs=[SMEM_SPEC] + [VMEM_SPEC] * (row_count + 3),
         out_specs=[VMEM_SPEC] * (row_count + 1),
-        scratch_shapes=[class_here]
-        + [pltpu.VMEM((pieces, LANES), f32)] * 3
+        scratch_shapes=[pltpu.VMEM((pieces, LANES), f32)] * 3
         + [pltpu.VMEM((total_obs, LANES), f32)]
         + work
-        + [pltpu.VMEM((pieces, LANES), f32), pltpu.SemaphoreType.DMA(())],
+        + [pltpu.VMEM((pieces, LANES), f32)],
         compiler_params=params,
         name="second",
-    )(taper_class, share, whole, error, *parts)
+    )(classes, share, whole, error, *parts)
     last_order = farthest_first(row_count)
     got = exchange(row, last_order, [sent[mask] for mask in last_order])
     solution_part, residual_part = pl.pallas_call(

time: 33.3 us -> 32.7 us (0.982)
  Pallas kernels: 7.6 us -> 7.04 us
    pallas_call x1, Pallas kernels: 1.35 us -> 0.93 us  [vectors_only(): pl.pallas_call(functools.partial(first_kernel, reach_tiles, inverse_membe...]
  transfers between devices with their start and end apart: 13 -> 13, of which waited for: 7 -> 7; matrix products, arithmetic and copies ran while one was open for 0% -> 0% of each run, Pallas kernels for 11% -> 12%
where the time goes in v6:
time: 32.7 us; the launch traced here: 32.5 us
  starting transfers between devices  16.6 us (51%)
  waiting for transfers between devices  8.17 us (25%)
  Pallas kernels  7.04 us (22%)
  between operations  0.67 us (2%)
    ppermute x12, starting transfers between devices, exchange(): lax.ppermute(value, axes, [(i, i ^ mask) for i in range(count)])  16.1 us
    ppermute x12, waiting for transfers between devices, exchange(): lax.ppermute(value, axes, [(i, i ^ mask) for i in range(count)])  8.16 us
    pallas_call x1, Pallas kernels, vectors_only(): pl.pallas_call(functools.partial(share_kernel, reach_tiles), out_shape=[p...  3.73 us
    pallas_call x1, Pallas kernels, vectors_only(): pl.pallas_call(functools.partial(second_kernel, reach_tiles, inverse_memb...  1.84 us
    pallas_call x1, Pallas kernels, vectors_only(): pl.pallas_call(functools.partial(first_kernel, reach_tiles, inverse_membe...  0.93 us
  transfers between devices with their start and end apart: 13, of which 7 were waited for; matrix products, arithmetic and copies ran while one was open for 0% of the time, Pallas kernels for 12%

profile of v6, /device:TPU:0, one launch (start us, length us, event | category | flops | bytes accessed | tf_op | source)
XLA Modules:
  0.0 32.5 jit_solution(17485405506327857215)
XLA Ops:
  0.6 0.5 %collective-permute-start = (bf16[128,2048]{1,0:T(8,128)(2,1)}, bf16[128,2048]{1,0:T(8,128)(2,1)S(1)}, u32[]{:S(2)}, u32[]{:S(2)}) collective-permute-start(bf16[128,2048]{1,0:T(8,128)(2,1)} %own_ref.1), channel_id=1, source_target_pairs={{0,1},{1,0},{2,3},{3,2},{4,5},{5,4},{6,7},{7,6},{8,9},{9,8},{10,11... | collective-permute-start | bytes 1572872 | tf_op jit(solution)/shard_map/ppermute | solution.py:327
  1.1 4.7 %collective-permute-start.1 = (f32[1,128]{1,0:T(1,128)}, f32[1,128]{1,0:T(1,128)S(1)}, u32[]{:S(2)}, u32[]{:S(2)}) collective-permute-start(f32[1,128]{1,0:T(1,128)} %bitcast.7), channel_id=1, source_target_pairs={{0,12},{4,8},{8,4},{12,0},{1,13},{5,9},{9,5},{13,1},{2,14},{6,10},... | collective-permute-start | bytes 1544 | tf_op jit(solution)/shard_map/ppermute | solution.py:300
  5.8 0.7 %collective-permute-start.3 = (f32[1,128]{1,0:T(1,128)}, f32[1,128]{1,0:T(1,128)S(1)}, u32[]{:S(2)}, u32[]{:S(2)}) collective-permute-start(f32[1,128]{1,0:T(1,128)} %bitcast.9), channel_id=1, source_target_pairs={{0,4},{4,0},{8,12},{12,8},{1,5},{5,1},{9,13},{13,9},{2,6},{6,2},{1... | collective-permute-start | bytes 1544 | tf_op jit(solution)/shard_map/ppermute | solution.py:300
  6.5 3.7 %share.1 = (f32[10,512,512]{2,1,0:T(8,128)S(1)}, s32[4,4]{1,0:T(4,128)S(4)}, f32[1,128]{1,0:T(1,128)S(1)}, f32[1,128]{1,0:T(1,128)S(1)}) custom-call(s32[4,4]{1,0:T(4,128)} %class_hbm.1, f32[1,2048]{1,0:T(1,128)} %bitcast.5, f32[1,128]{1,0:T(1,128)} %bitcast.10, f32[1,128]{1,0:T(1,128)} %bitcast.6, bf16[128,2048]{1,0:T(8,128)(2,1)} %own_ref.1, ...), custom_call_target="tpu_custom_call" | custom-call | flops 2147483648 | bytes 16777216 | tf_op jit(solution)/shard_map/share/pallas_call | solution.py:334
  10.2 0.0 collective-permute-done.1.refs_1_
  10.2 0.2 collective-permute-done.2.refs_2_
  10.4 0.9 %first.1.refs_0_ = f32[24,128]{1,0:T(8,128)S(1)} custom-call(s32[4,4]{1,0:T(4,128)S(4)} %get-tuple-element.15.class_ref, f32[10,512,512]{2,1,0:T(8,128)S(1)} %get-tuple-element.16.share_ref, f32[1,128]{1,0:T(1,128)S(1)} %get-tuple-element.17.error_ref, f32[1,128]{1,0:T(1,128)S(1)} %get-tuple-element.18.refs_0_, f32[1,128]{1,0:T(1,128)S(1)} %collective-permute-done.1.refs_1_, ...), custom_call_target="tpu_custom_call" | custom-call | tf_op jit(solution)/shard_map/first/pallas_call | solution.py:360
  11.3 0.8 %collective-permute-start.4 = (f32[24,128]{1,0:T(8,128)S(1)}, f32[24,128]{1,0:T(8,128)S(1)}, u32[]{:S(2)}, u32[]{:S(2)}) collective-permute-start(f32[24,128]{1,0:T(8,128)S(1)} %first.1.refs_0_), channel_id=1, source_target_pairs={{0,3},{1,2},{2,1},{3,0},{4,7},{5,6},{6,5},{7,4},{8,11},{9,10},{10,... | collective-permute-start | bytes 36872 | tf_op jit(solution)/shard_map/ppermute | solution.py:300
  12.2 0.8 %collective-permute-start.5 = (f32[24,128]{1,0:T(8,128)S(1)}, f32[24,128]{1,0:T(8,128)S(1)}, u32[]{:S(2)}, u32[]{:S(2)}) collective-permute-start(f32[24,128]{1,0:T(8,128)S(1)} %first.1.refs_0_), channel_id=1, source_target_pairs={{0,2},{1,3},{2,0},{3,1},{4,6},{5,7},{6,4},{7,5},{8,10},{9,11},{10,... | collective-permute-start | bytes 36872 | tf_op jit(solution)/shard_map/ppermute | solution.py:300
  13.0 0.3 collective-permute-start.6
  13.3 1.3 %collective-permute-done.4.refs_1_ = f32[24,128]{1,0:T(8,128)S(1)} collective-permute-done((f32[24,128]{1,0:T(8,128)S(1)}, f32[24,128]{1,0:T(8,128)S(1)}, u32[]{:S(2)}, u32[]{:S(2)}) %collective-permute-start.4) | collective-permute-done | bytes 12320 | tf_op jit(solution)/shard_map/ppermute | solution.py:300
  14.6 1.3 %collective-permute-done.5.refs_2_ = f32[24,128]{1,0:T(8,128)S(1)} collective-permute-done((f32[24,128]{1,0:T(8,128)S(1)}, f32[24,128]{1,0:T(8,128)S(1)}, u32[]{:S(2)}, u32[]{:S(2)}) %collective-permute-start.5) | collective-permute-done | bytes 12320 | tf_op jit(solution)/shard_map/ppermute | solution.py:300
  15.9 3.7 %collective-permute-start.7 = (f32[16,128]{1,0:T(8,128)S(1)}, f32[16,128]{1,0:T(8,128)S(1)}, u32[]{:S(2)}, u32[]{:S(2)}) collective-permute-start(f32[16,128]{1,0:T(8,128)S(1)} %middle.1.refs_0_), channel_id=1, source_target_pairs={{0,12},{4,8},{8,4},{12,0},{1,13},{5,9},{9,5},{13,1},{2,14},{6,10},... | collective-permute-start | bytes 24584 | tf_op jit(solution)/shard_map/ppermute | solution.py:300
  19.6 0.8 %collective-permute-start.9 = (f32[16,128]{1,0:T(8,128)S(1)}, f32[16,128]{1,0:T(8,128)S(1)}, u32[]{:S(2)}, u32[]{:S(2)}) collective-permute-start(f32[16,128]{1,0:T(8,128)S(1)} %middle.1.refs_0_), channel_id=1, source_target_pairs={{0,4},{4,0},{8,12},{12,8},{1,5},{5,1},{9,13},{13,9},{2,6},{6,2},{1... | collective-permute-start | bytes 24584 | tf_op jit(solution)/shard_map/ppermute | solution.py:300
  20.4 1.0 %collective-permute-done.7.refs_1_ = f32[16,128]{1,0:T(8,128)S(1)} collective-permute-done((f32[16,128]{1,0:T(8,128)S(1)}, f32[16,128]{1,0:T(8,128)S(1)}, u32[]{:S(2)}, u32[]{:S(2)}) %collective-permute-start.7) | collective-permute-done | bytes 8224 | tf_op jit(solution)/shard_map/ppermute | solution.py:300
  21.4 2.7 %collective-permute-done.8.refs_2_ = f32[16,128]{1,0:T(8,128)S(1)} collective-permute-done((f32[16,128]{1,0:T(8,128)S(1)}, f32[16,128]{1,0:T(8,128)S(1)}, u32[]{:S(2)}, u32[]{:S(2)}) %collective-permute-start.8) | collective-permute-done | bytes 8224 | tf_op jit(solution)/shard_map/ppermute | solution.py:300
  24.1 1.8 %second.1 = (f32[8,128]{1,0:T(8,128)S(1)}, f32[8,128]{1,0:T(8,128)S(1)}, f32[8,128]{1,0:T(8,128)S(1)}, f32[8,128]{1,0:T(8,128)S(1)}, f32[8,128]{1,0:T(8,128)S(1)}) custom-call(s32[4,4]{1,0:T(4,128)S(4)} %get-tuple-element.15.class_ref, f32[10,512,512]{2,1,0:T(8,128)S(1)} %get-tuple-element.16.share_ref, f32[16,128]{1,0:T(8,128)S(1)} %get-tuple-element.19.innovations_ref, ...), custom_call_target="tpu_custom_call" | custom-call | tf_op jit(solution)/shard_map/second/pallas_call | solution.py:390
  26.0 1.5 %collective-permute-start.10 = (f32[8,128]{1,0:T(8,128)S(1)}, f32[8,128]{1,0:T(8,128)S(1)}, u32[]{:S(2)}, u32[]{:S(2)}) collective-permute-start(f32[8,128]{1,0:T(8,128)S(1)} %get-tuple-element.23), channel_id=1, source_target_pairs={{0,12},{4,8},{8,4},{12,0},{1,13},{5,9},{9,5},{13,1},{2,14},{6,10},... | collective-permute-start | bytes 12296 | tf_op jit(solution)/shard_map/ppermute | solution.py:300
  27.4 0.6 %collective-permute-start.11 = (f32[8,128]{1,0:T(8,128)S(1)}, f32[8,128]{1,0:T(8,128)S(1)}, u32[]{:S(2)}, u32[]{:S(2)}) collective-permute-start(f32[8,128]{1,0:T(8,128)S(1)} %get-tuple-element.24), channel_id=1, source_target_pairs={{0,8},{4,12},{8,0},{12,4},{1,9},{5,13},{9,1},{13,5},{2,10},{6,14},... | collective-permute-start | bytes 12296 | tf_op jit(solution)/shard_map/ppermute | solution.py:300
  28.1 2.3 %collective-permute-start.12 = (f32[8,128]{1,0:T(8,128)S(1)}, f32[8,128]{1,0:T(8,128)S(1)}, u32[]{:S(2)}, u32[]{:S(2)}) collective-permute-start(f32[8,128]{1,0:T(8,128)S(1)} %get-tuple-element.25), channel_id=1, source_target_pairs={{0,4},{4,0},{8,12},{12,8},{1,5},{5,1},{9,13},{13,9},{2,6},{6,2},{1... | collective-permute-start | bytes 12296 | tf_op jit(solution)/shard_map/ppermute | solution.py:300
  30.3 1.0 %collective-permute-done.10.refs_1_ = f32[8,128]{1,0:T(8,128)S(1)} collective-permute-done((f32[8,128]{1,0:T(8,128)S(1)}, f32[8,128]{1,0:T(8,128)S(1)}, u32[]{:S(2)}, u32[]{:S(2)}) %collective-permute-start.10) | collective-permute-done | bytes 4128 | tf_op jit(solution)/shard_map/ppermute | solution.py:300
  31.4 0.6 %collective-permute-done.11.refs_2_ = f32[8,128]{1,0:T(8,128)S(1)} collective-permute-done((f32[8,128]{1,0:T(8,128)S(1)}, f32[8,128]{1,0:T(8,128)S(1)}, u32[]{:S(2)}, u32[]{:S(2)}) %collective-permute-start.11) | collective-permute-done | bytes 4128 | tf_op jit(solution)/shard_map/ppermute | solution.py:300
  31.9 0.0 collective-permute-done.12.refs_3_
  32.0 0.5 %last.1 = (f32[1,128]{1,0:T(1,128)}, f32[1,128]{1,0:T(1,128)}) custom-call(f32[8,128]{1,0:T(8,128)S(1)} %get-tuple-element.21.state_ref, f32[8,128]{1,0:T(8,128)S(1)} %get-tuple-element.22.refs_0_, f32[8,128]{1,0:T(8,128)S(1)} %collective-permute-done.10.refs_1_, f32[8,128]{1,0:T(8,128)S(1)} %collective-permute-done.11.refs_2_, ...), custom_call_target="tpu_custom_call" | custom-call | tf_op jit(solution)/shard_map/last/pallas_call | solution.py:404
  (8 shorter events, 0.0 us)
Async XLA Ops:
  0.6 5.9 %collective-permute-start = (bf16[128,2048]{1,0:T(8,128)(2,1)}, bf16[128,2048]{1,0:T(8,128)(2,1)S(1)}, u32[]{:S(2)}, u32[]{:S(2)}) collective-permute-start(bf16[128,2048]{1,0:T(8,128)(2,1)} %own_ref.1), channel_id=1, source_target_pairs={{0,1},{1,0},{2,3},{3,2},{4,5},{5,4},{6,7},{7,6},{8,9},{9,8},{10,11... | collective-permute-start | bytes 1572872 | tf_op jit(solution)/shard_map/ppermute | solution.py:327
  1.1 9.1 %collective-permute-start.1 = (f32[1,128]{1,0:T(1,128)}, f32[1,128]{1,0:T(1,128)S(1)}, u32[]{:S(2)}, u32[]{:S(2)}) collective-permute-start(f32[1,128]{1,0:T(1,128)} %bitcast.7), channel_id=1, source_target_pairs={{0,12},{4,8},{8,4},{12,0},{1,13},{5,9},{9,5},{13,1},{2,14},{6,10},... | collective-permute-start | bytes 1544 | tf_op jit(solution)/shard_map/ppermute | solution.py:300
  5.8 4.6 %collective-permute-start.2 = (f32[1,128]{1,0:T(1,128)}, f32[1,128]{1,0:T(1,128)S(1)}, u32[]{:S(2)}, u32[]{:S(2)}) collective-permute-start(f32[1,128]{1,0:T(1,128)} %bitcast.8), channel_id=1, source_target_pairs={{0,8},{4,12},{8,0},{12,4},{1,9},{5,13},{9,1},{13,5},{2,10},{6,14},... | collective-permute-start | bytes 1544 | tf_op jit(solution)/shard_map/ppermute | solution.py:300
  5.8 4.6 %collective-permute-start.3 = (f32[1,128]{1,0:T(1,128)}, f32[1,128]{1,0:T(1,128)S(1)}, u32[]{:S(2)}, u32[]{:S(2)}) collective-permute-start(f32[1,128]{1,0:T(1,128)} %bitcast.9), channel_id=1, source_target_pairs={{0,4},{4,0},{8,12},{12,8},{1,5},{5,1},{9,13},{13,9},{2,6},{6,2},{1... | collective-permute-start | bytes 1544 | tf_op jit(solution)/shard_map/ppermute | solution.py:300
  11.3 3.3 %collective-permute-start.4 = (f32[24,128]{1,0:T(8,128)S(1)}, f32[24,128]{1,0:T(8,128)S(1)}, u32[]{:S(2)}, u32[]{:S(2)}) collective-permute-start(f32[24,128]{1,0:T(8,128)S(1)} %first.1.refs_0_), channel_id=1, source_target_pairs={{0,3},{1,2},{2,1},{3,0},{4,7},{5,6},{6,5},{7,4},{8,11},{9,10},{10,... | collective-permute-start | bytes 36872 | tf_op jit(solution)/shard_map/ppermute | solution.py:300
  12.2 3.7 %collective-permute-start.5 = (f32[24,128]{1,0:T(8,128)S(1)}, f32[24,128]{1,0:T(8,128)S(1)}, u32[]{:S(2)}, u32[]{:S(2)}) collective-permute-start(f32[24,128]{1,0:T(8,128)S(1)} %first.1.refs_0_), channel_id=1, source_target_pairs={{0,2},{1,3},{2,0},{3,1},{4,6},{5,7},{6,4},{7,5},{8,10},{9,11},{10,... | collective-permute-start | bytes 36872 | tf_op jit(solution)/shard_map/ppermute | solution.py:300
  13.0 2.9 %collective-permute-start.6 = (f32[24,128]{1,0:T(8,128)S(1)}, f32[24,128]{1,0:T(8,128)S(1)}, u32[]{:S(2)}, u32[]{:S(2)}) collective-permute-start(f32[24,128]{1,0:T(8,128)S(1)} %first.1.refs_0_), channel_id=1, source_target_pairs={{0,1},{1,0},{2,3},{3,2},{4,5},{5,4},{6,7},{7,6},{8,9},{9,8},{10,11... | collective-permute-start | bytes 36872 | tf_op jit(solution)/shard_map/ppermute | solution.py:300
  15.9 5.5 %collective-permute-start.7 = (f32[16,128]{1,0:T(8,128)S(1)}, f32[16,128]{1,0:T(8,128)S(1)}, u32[]{:S(2)}, u32[]{:S(2)}) collective-permute-start(f32[16,128]{1,0:T(8,128)S(1)} %middle.1.refs_0_), channel_id=1, source_target_pairs={{0,12},{4,8},{8,4},{12,0},{1,13},{5,9},{9,5},{13,1},{2,14},{6,10},... | collective-permute-start | bytes 24584 | tf_op jit(solution)/shard_map/ppermute | solution.py:300
  19.6 4.5 %collective-permute-start.8 = (f32[16,128]{1,0:T(8,128)S(1)}, f32[16,128]{1,0:T(8,128)S(1)}, u32[]{:S(2)}, u32[]{:S(2)}) collective-permute-start(f32[16,128]{1,0:T(8,128)S(1)} %middle.1.refs_0_), channel_id=1, source_target_pairs={{0,8},{4,12},{8,0},{12,4},{1,9},{5,13},{9,1},{13,5},{2,10},{6,14},... | collective-permute-start | bytes 24584 | tf_op jit(solution)/shard_map/ppermute | solution.py:300
  19.6 4.5 %collective-permute-start.9 = (f32[16,128]{1,0:T(8,128)S(1)}, f32[16,128]{1,0:T(8,128)S(1)}, u32[]{:S(2)}, u32[]{:S(2)}) collective-permute-start(f32[16,128]{1,0:T(8,128)S(1)} %middle.1.refs_0_), channel_id=1, source_target_pairs={{0,4},{4,0},{8,12},{12,8},{1,5},{5,1},{9,13},{13,9},{2,6},{6,2},{1... | collective-permute-start | bytes 24584 | tf_op jit(solution)/shard_map/ppermute | solution.py:300
  26.0 5.4 %collective-permute-start.10 = (f32[8,128]{1,0:T(8,128)S(1)}, f32[8,128]{1,0:T(8,128)S(1)}, u32[]{:S(2)}, u32[]{:S(2)}) collective-permute-start(f32[8,128]{1,0:T(8,128)S(1)} %get-tuple-element.23), channel_id=1, source_target_pairs={{0,12},{4,8},{8,4},{12,0},{1,13},{5,9},{9,5},{13,1},{2,14},{6,10},... | collective-permute-start | bytes 12296 | tf_op jit(solution)/shard_map/ppermute | solution.py:300
  27.4 4.5 %collective-permute-start.11 = (f32[8,128]{1,0:T(8,128)S(1)}, f32[8,128]{1,0:T(8,128)S(1)}, u32[]{:S(2)}, u32[]{:S(2)}) collective-permute-start(f32[8,128]{1,0:T(8,128)S(1)} %get-tuple-element.24), channel_id=1, source_target_pairs={{0,8},{4,12},{8,0},{12,4},{1,9},{5,13},{9,1},{13,5},{2,10},{6,14},... | collective-permute-start | bytes 12296 | tf_op jit(solution)/shard_map/ppermute | solution.py:300
  28.1 3.9 %collective-permute-start.12 = (f32[8,128]{1,0:T(8,128)S(1)}, f32[8,128]{1,0:T(8,128)S(1)}, u32[]{:S(2)}, u32[]{:S(2)}) collective-permute-start(f32[8,128]{1,0:T(8,128)S(1)} %get-tuple-element.25), channel_id=1, source_target_pairs={{0,4},{4,0},{8,12},{12,8},{1,5},{5,1},{9,13},{13,9},{2,6},{6,2},{1... | collective-permute-start | bytes 12296 | tf_op jit(solution)/shard_map/ppermute | solution.py:300

commit v7 on v6

--- a/solution.py
+++ b/solution.py
@@ -42,42 +42,69 @@
     return pl.ds(pl.multiple_of(a * block_len, LANES), block_len)
 
 
-def share_kernel(
-    reach_tiles, class_hbm, pos_hbm, chunk_hbm, error_hbm, own_ref, mate_ref, share_ref, class_ref, chunk_ref, error_ref,
-    *scratch
+def make_part(target, left_turned, right, left_column, right_pos):
+    product = jnp.dot(left_turned, right, preferred_element_type=jnp.float32)
+    left_pos = jnp.concatenate([left_column] * (right_pos.shape[1] // LANES), axis=1)
+    distance = left_pos - right_pos
+    target[...] = product * jnp.exp2(distance * distance * exp2_rate)
+
+
+def turn_kernel(mate_ref, turned_ref):
+    turned_ref[...] = mate_ref[...].T
+
+
+def strips_kernel(
+    reach_tiles, class_hbm, pos_ref, own_ref, mate_ref, turned_mate_ref, row_strips, column_strips, class_ref, both,
+    turned, column, arrived,
 ):
-    pos_ref, both, turned, column, arrived = scratch
     members, total_obs = own_ref.shape
     tiles = class_ref.shape[0]
     block_len = total_obs // tiles
-    pos_copy = pltpu.make_async_copy(pos_hbm, pos_ref, arrived.at[0])
-    own_copy = pltpu.make_async_copy(own_ref, both.at[pl.ds(0, members), :], arrived.at[1])
-    class_copy = pltpu.make_async_copy(class_hbm, class_ref, arrived.at[2])
-    chunk_copy = pltpu.make_async_copy(chunk_hbm, chunk_ref, arrived.at[3])
-    error_copy = pltpu.make_async_copy(error_hbm, error_ref, arrived.at[4])
-    for copy in (pos_copy, own_copy, class_copy, chunk_copy, error_copy):
-        copy.start()
+    class_copy = pltpu.make_async_copy(class_hbm, class_ref, arrived)
+    class_copy.start()
+    both[:members, :] = own_ref[...]
     both[members:, :] = mate_ref[...]
-    turned[:, members:] = mate_ref[...].T
-    pos_copy.wait()
+    turned[:, :members] = own_ref[...].T
+    turned[:, members:] = turned_mate_ref[...]
     spread_columns(pos_ref[...], column)
-    own_copy.wait()
-    turned[:, :members] = both[:members, :].T
-    for copy in (class_copy, chunk_copy, error_copy):
-        copy.wait()
-    rows = 128
+    _, within, _ = place()
+
+    def chunk_of(a):
+        return pl.ds(pl.multiple_of(a * block_len + within * LANES, LANES), LANES)
+
+    def row_strip(target, a, b):
+        at, columns_at = chunk_of(a), block_at(b, block_len)
+        make_part(target, turned[at, :], both[:, columns_at], column[at, :], pos_ref[:, columns_at])
+
+    def make_diagonal(slot, carry):
+        row_strip(row_strips.at[slot], slot, slot)
+        return carry
+
+    def make_pair(slot, a, b):
+        row_strip(row_strips.at[slot + tiles], a, b)
+        at, columns_at = block_at(a, block_len), chunk_of(b)
+        make_part(column_strips.at[slot], turned[at, :], both[:, columns_at], column[at, :], pos_ref[:, columns_at])
+
+    lax.fori_loop(0, tiles, make_diagonal, 0)
+    class_copy.wait()
+    for_each_pair(reach_tiles, class_ref, make_pair)
+
+
+def share_kernel(reach_tiles, class_ref, pos_ref, both, turned, column, row_strips, share_ref):
+    tiles = class_ref.shape[0]
+    block_len = share_ref.shape[1]
+    _, within, per_row = place()
 
     def make_tile(slot, a, b):
-        rows_at, columns_at = block_at(a, block_len), block_at(b, block_len)
-        right = both[:, columns_at]
-        right_pos = pos_ref[:, columns_at]
-        left_turned, left_column, tile = turned.at[rows_at, :], column.at[rows_at, :], share_ref.at[slot]
-        for begin in range(0, block_len, rows):
-            part = slice(begin, begin + rows)
-            product = jnp.dot(left_turned[part, :], right, preferred_element_type=jnp.float32)
-            left_pos = jnp.concatenate([left_column[part, :]] * (block_len // LANES), axis=1)
-            distance = left_pos - right_pos
-            tile[part, :] = product * jnp.exp2(distance * distance * exp2_rate)
+        tile, columns_at = share_ref.at[slot], block_at(b, block_len)
+        right, right_pos = both[:, columns_at], pos_ref[:, columns_at]
+        here = pl.ds(pl.multiple_of(within * LANES, LANES), LANES)
+        tile[here, :] = row_strips[slot]
+        for turn in range(1, per_row):
+            begin = lax.rem(within + turn, per_row) * LANES
+            here = pl.ds(pl.multiple_of(begin, LANES), LANES)
+            at = pl.ds(pl.multiple_of(a * block_len + begin, LANES), LANES)
+            make_part(tile.at[here, :], turned[at, :], right, column[at, :], right_pos)
 
     def make_diagonal(slot, carry):
         make_tile(slot, slot, slot)
@@ -171,22 +198,21 @@
     return lax.axis_index("row"), within, lax.axis_size("col") * sub_count
 
 
-def first_kernel(reach_tiles, inverse_members, masks, class_ref, share_ref, error_ref, *refs):
+def first_kernel(reach_tiles, inverse_members, masks, class_ref, row_strips, column_strips, error_ref, *refs):
     tiles = class_ref.shape[0]
     chunks, refs = refs[:tiles], refs[tiles:]
     out_ref, vector, column, across, sums = refs
     row_index, within, per_row = place()
-    block_len = share_ref.shape[1]
+    block_len = row_strips.shape[2]
     lanes = block_len // LANES
     pieces = tiles * lanes
     for mask, chunk in zip(masks, chunks):
         vector[pl.ds(row_index ^ mask, 1), :] = chunk[...]
     spread_vector(vector, column)
     sums[...] = jnp.zeros_like(sums)
-    chunk_at = pl.ds(pl.multiple_of(within * LANES, LANES), LANES)
-
-    def sums_of_rows(tile, a):
-        strip, factor = tile.at[chunk_at, :], column.at[pl.ds(pl.multiple_of(a * LANES, LANES), LANES), :]
+
+    def sums_of_rows(strip, a):
+        factor = column.at[pl.ds(pl.multiple_of(a * LANES, LANES), LANES), :]
         totals = [None] * lanes
         for begin in range(0, LANES, 8):
             part = slice(begin, begin + 8)
@@ -197,14 +223,13 @@
 
     def add_diagonal(a, carry):
         weight = tile_weight(class_ref[a, a], reach_tiles, inverse_members)
-        add_sums(sums.at[:, block_at(a, block_len)], weight, sums_of_rows(share_ref.at[a], a))
+        add_sums(sums.at[:, block_at(a, block_len)], weight, sums_of_rows(row_strips.at[a], a))
         return carry
 
     def add_pair(slot, a, b):
         weight = tile_weight(class_ref[a, b], reach_tiles, inverse_members)
-        tile = share_ref.at[slot + tiles]
-        add_sums(sums.at[:, block_at(b, block_len)], weight, sums_of_rows(tile, a))
-        across[...] = tile[:, chunk_at] * vector[pl.ds(b, 1), :]
+        add_sums(sums.at[:, block_at(b, block_len)], weight, sums_of_rows(row_strips.at[slot + tiles], a))
+        across[...] = column_strips[slot] * vector[pl.ds(b, 1), :]
         add_turned(sums.at[:, block_at(a, block_len)], weight, across)
 
     lax.fori_loop(0, tiles, add_diagonal, 0)
@@ -327,47 +352,56 @@
     mate = lax.ppermute(anomalies, "sub", [(0, 1), (1, 0)])
     chunk = innovations.reshape(1, LANES)
     error = obs_error.reshape(1, LANES)
-    chunk_order = farthest_first(row_count)
+    chunk_order = nearest_first(row_count)
     chunks = exchange(row, chunk_order, [chunk] * row_count)
 
     work = [pltpu.VMEM((block_len, LANES), f32), pltpu.VMEM((8, total_obs), f32)]
-    share, classes, own_chunk, own_error = pl.pallas_call(
-        functools.partial(share_kernel, reach_tiles),
+    pairs = off_diagonal(row_count)
+    part_elements = (row_count + pairs) * block_len * block_len
+    mate_bytes = anomalies.size * anomalies.dtype.itemsize
+    turned_mate = pl.pallas_call(
+        turn_kernel,
+        out_shape=pltpu.VMEM((total_obs, local_members), anomalies.dtype),
+        in_specs=[VMEM_SPEC],
+        out_specs=VMEM_SPEC,
+        compiler_params=params,
+        cost_estimate=pl.CostEstimate(flops=4 * local_members * total_obs * total_obs, bytes_accessed=16 * mate_bytes, transcendentals=0),
+        name="turn",
+    )(mate)
+    positions = track_pos.reshape(1, total_obs)
+    strips, strip_columns, classes, both, turned, column = pl.pallas_call(
+        functools.partial(strips_kernel, reach_tiles),
         out_shape=[
-            pltpu.VMEM((row_count + off_diagonal(row_count), block_len, block_len), f32),
+            pltpu.VMEM((row_count + pairs, LANES, block_len), f32),
+            pltpu.VMEM((pairs, block_len, LANES), f32),
             pltpu.SMEM(taper_class.shape, jnp.int32),
-            pltpu.VMEM((1, LANES), f32),
-            pltpu.VMEM((1, LANES), f32),
-        ],
-        in_specs=[HBM_SPEC] * 5 + [VMEM_SPEC],
-        out_specs=[VMEM_SPEC, SMEM_SPEC, VMEM_SPEC, VMEM_SPEC],
-        scratch_shapes=[
-            pltpu.VMEM((1, total_obs), f32),
             pltpu.VMEM((2 * local_members, total_obs), anomalies.dtype),
             pltpu.VMEM((total_obs, 2 * local_members), anomalies.dtype),
             pltpu.VMEM((total_obs, LANES), f32),
-            pltpu.SemaphoreType.DMA((5,)),
         ],
+        in_specs=[HBM_SPEC] + [VMEM_SPEC] * 4,
+        out_specs=[VMEM_SPEC] * 2 + [SMEM_SPEC] + [VMEM_SPEC] * 3,
+        scratch_shapes=[pltpu.SemaphoreType.DMA(())],
         compiler_params=params,
         cost_estimate=pl.CostEstimate(
-            flops=4 * local_members * total_obs * total_obs,
-            bytes_accessed=4 * total_obs * total_obs,
-            transcendentals=total_obs * total_obs,
+            flops=2 * local_members * part_elements,
+            bytes_accessed=2 * part_elements,
+            transcendentals=part_elements // 2,
         ),
-        name="share",
-    )(*[in_hbm(x) for x in (taper_class, track_pos.reshape(1, total_obs), chunk, error, anomalies)], mate)
+        name="strips",
+    )(in_hbm(taper_class), positions, anomalies, mate, turned_mate)
 
     payload = pl.pallas_call(
         functools.partial(first_kernel, reach_tiles, inverse_members, chunk_order),
         out_shape=pltpu.VMEM((pieces + 8, LANES), f32),
-        in_specs=[SMEM_SPEC] + [VMEM_SPEC] * (row_count + 2),
+        in_specs=[SMEM_SPEC] + [VMEM_SPEC] * (row_count + 3),
         out_specs=VMEM_SPEC,
         scratch_shapes=[pltpu.VMEM((row_count, LANES), f32), pltpu.VMEM((row_count * LANES, LANES), f32)]
         + work,
         compiler_params=params,
         name="first",
-    )(classes, share, own_error, own_chunk, *chunks[1:])
-    payload_order = farthest_first(per_row)
+    )(classes, strips, strip_columns, error, *chunks)
+    payload_order = nearest_first(per_row)
     payloads = exchange(here, payload_order, [payload] * per_row)
     part = pl.pallas_call(
         functools.partial(middle_kernel, pieces),
@@ -377,7 +411,7 @@
         compiler_params=params,
         name="middle",
     )(*payloads)
-    parts = exchange(row, farthest_first(row_count), [part] * row_count)
+    parts = exchange(row, nearest_first(row_count), [part] * row_count)
     whole, error = pl.pallas_call(
         functools.partial(gather_kernel, row_count, payload_order),
         out_shape=[pltpu.VMEM((pieces, LANES), f32), pltpu.VMEM((per_row, LANES), f32)],
@@ -387,6 +421,19 @@
         name="gather",
     )(*payloads)
 
+    share = pl.pallas_call(
+        functools.partial(share_kernel, reach_tiles),
+        out_shape=pltpu.VMEM((row_count + pairs, block_len, block_len), f32),
+        in_specs=[SMEM_SPEC] + [VMEM_SPEC] * 5,
+        out_specs=VMEM_SPEC,
+        compiler_params=params,
+        cost_estimate=pl.CostEstimate(
+            flops=4 * local_members * part_elements,
+            bytes_accessed=4 * part_elements,
+            transcendentals=part_elements,
+        ),
+        name="share",
+    )(classes, positions, both, turned, column, strips)
     *sent, state = pl.pallas_call(
         functools.partial(second_kernel, reach_tiles, inverse_members, row_count),
         out_shape=[pltpu.VMEM((8, LANES), f32) for _ in range(row_count + 1)],

time: 32.7 us -> 32 us (0.979)
  waiting for transfers between devices: 8.17 us -> 6.58 us
  Pallas kernels: 7.04 us -> 7.89 us
    ppermute x12, waiting for transfers between devices: 8.16 us -> 6.57 us  [exchange(): lax.ppermute(value, axes, [(i, i ^ mask) for i in range(count)])]
    pallas_call x1 -> x3, Pallas kernels: 3.73 us -> 4.59 us  [the longest x1 2.28 us: vectors_only(): pl.pallas_call(functools.partial(strips_kernel, reach_tiles), out_shape=[...]
  transfers between devices with their start and end apart: 13 -> 13, of which waited for: 7 -> 6; matrix products, arithmetic and copies ran while one was open for 0% -> 0% of each run, Pallas kernels for 12% -> 14%
where the time goes in v7:
time: 32 us; the launch traced here: 31.8 us
  starting transfers between devices  16.6 us (52%)
  Pallas kernels  7.89 us (25%)
  waiting for transfers between devices  6.58 us (21%)
  between operations  0.72 us (2%)
    ppermute x12, starting transfers between devices, exchange(): lax.ppermute(value, axes, [(i, i ^ mask) for i in range(count)])  16.1 us
    ppermute x12, waiting for transfers between devices, exchange(): lax.ppermute(value, axes, [(i, i ^ mask) for i in range(count)])  6.57 us
    pallas_call x1, Pallas kernels, vectors_only(): pl.pallas_call(functools.partial(strips_kernel, reach_tiles), out_shape=[...  2.28 us
    pallas_call x1, Pallas kernels, vectors_only(): pl.pallas_call(functools.partial(share_kernel, reach_tiles), out_shape=pl...  2.12 us
    pallas_call x1, Pallas kernels, vectors_only(): pl.pallas_call(functools.partial(second_kernel, reach_tiles, inverse_memb...  1.88 us
    pallas_call x1, Pallas kernels, vectors_only(): pl.pallas_call(functools.partial(first_kernel, reach_tiles, inverse_membe...  0.87 us
  transfers between devices with their start and end apart: 13, of which 6 were waited for; matrix products, arithmetic and copies ran while one was open for 0% of the time, Pallas kernels for 14%

profile of v7, /device:TPU:0, one launch (start us, length us, event | category | flops | bytes accessed | tf_op | source)
XLA Modules:
  0.0 31.8 jit_solution(16856367374723325123)
XLA Ops:
  0.6 0.5 %collective-permute-start = (bf16[128,2048]{1,0:T(8,128)(2,1)}, bf16[128,2048]{1,0:T(8,128)(2,1)S(1)}, u32[]{:S(2)}, u32[]{:S(2)}) collective-permute-start(bf16[128,2048]{1,0:T(8,128)(2,1)} %own_ref.1), channel_id=1, source_target_pairs={{0,1},{1,0},{2,3},{3,2},{4,5},{5,4},{6,7},{7,6},{8,9},{9,8},{10,11... | collective-permute-start | bytes 1572872 | tf_op jit(solution)/shard_map/ppermute | solution.py:352
  1.2 4.7 %collective-permute-start.3 = (f32[1,128]{1,0:T(1,128)}, f32[1,128]{1,0:T(1,128)S(1)}, u32[]{:S(2)}, u32[]{:S(2)}) collective-permute-start(f32[1,128]{1,0:T(1,128)} %bitcast.8), channel_id=1, source_target_pairs={{0,12},{4,8},{8,4},{12,0},{1,13},{5,9},{9,5},{13,1},{2,14},{6,10},... | collective-permute-start | bytes 1544 | tf_op jit(solution)/shard_map/ppermute | solution.py:325
  5.9 0.0 collective-permute-start.2
  5.9 0.6 %collective-permute-start.1 = (f32[1,128]{1,0:T(1,128)}, f32[1,128]{1,0:T(1,128)S(1)}, u32[]{:S(2)}, u32[]{:S(2)}) collective-permute-start(f32[1,128]{1,0:T(1,128)} %bitcast.10), channel_id=1, source_target_pairs={{0,4},{4,0},{8,12},{12,8},{1,5},{5,1},{9,13},{13,9},{2,6},{6,2},{1... | collective-permute-start | bytes 1544 | tf_op jit(solution)/shard_map/ppermute | solution.py:325
  6.5 0.2 turn.1.turned_mate_ref
  6.7 2.3 %strips.1 = (f32[10,128,512]{2,1,0:T(8,128)S(1)}, f32[6,512,128]{2,1,0:T(8,128)S(1)}, s32[4,4]{1,0:T(4,128)S(4)}, bf16[256,2048]{1,0:T(8,128)(2,1)S(1)}, bf16[20...) custom-call(s32[4,4]{1,0:T(4,128)} %class_hbm.1, f32[1,2048]{1,0:T(1,128)S(1)} %bitcast.5, ...), custom_call_target="tpu_custom_call" | custom-call | flops 671088640 | bytes 5242880 | tf_op jit(solution)/shard_map/strips/pallas_call | solution.py:372
  9.0 1.4 %collective-permute-done.2.refs_2_ = f32[1,128]{1,0:T(1,128)S(1)} collective-permute-done((f32[1,128]{1,0:T(1,128)}, f32[1,128]{1,0:T(1,128)S(1)}, u32[]{:S(2)}, u32[]{:S(2)}) %collective-permute-start.2) | collective-permute-done | bytes 544 | tf_op jit(solution)/shard_map/ppermute | solution.py:325
  10.4 0.9 %first.1.refs_0_ = f32[24,128]{1,0:T(8,128)S(1)} custom-call(s32[4,4]{1,0:T(4,128)S(4)} %get-tuple-element.17.class_ref, f32[10,128,512]{2,1,0:T(8,128)S(1)} %get-tuple-element.21.row_strips, f32[6,512,128]{2,1,0:T(8,128)S(1)} %get-tuple-element.22.column_strips, f32[1,128]{1,0:T(1,128)S(1)} %bitcast.7, f32[1,128]{1,0:T(1,128)S(1)} %bitcast.11, ...), custom_call_target="tpu_custom_call" | custom-call | tf_op jit(solution)/shard_map/first/pallas_call | solution.py:394
  11.3 0.2 collective-permute-start.6
  11.5 1.4 %collective-permute-start.5 = (f32[24,128]{1,0:T(8,128)S(1)}, f32[24,128]{1,0:T(8,128)S(1)}, u32[]{:S(2)}, u32[]{:S(2)}) collective-permute-start(f32[24,128]{1,0:T(8,128)S(1)} %first.1.refs_0_), channel_id=1, source_target_pairs={{0,2},{1,3},{2,0},{3,1},{4,6},{5,7},{6,4},{7,5},{8,10},{9,11},{10,... | collective-permute-start | bytes 36872 | tf_op jit(solution)/shard_map/ppermute | solution.py:325
  13.0 0.3 collective-permute-start.4
  13.3 1.3 %collective-permute-done.6.refs_3_ = f32[24,128]{1,0:T(8,128)S(1)} collective-permute-done((f32[24,128]{1,0:T(8,128)S(1)}, f32[24,128]{1,0:T(8,128)S(1)}, u32[]{:S(2)}, u32[]{:S(2)}) %collective-permute-start.6) | collective-permute-done | bytes 12320 | tf_op jit(solution)/shard_map/ppermute | solution.py:325
  14.6 0.6 %collective-permute-done.5.refs_2_ = f32[24,128]{1,0:T(8,128)S(1)} collective-permute-done((f32[24,128]{1,0:T(8,128)S(1)}, f32[24,128]{1,0:T(8,128)S(1)}, u32[]{:S(2)}, u32[]{:S(2)}) %collective-permute-start.5) | collective-permute-done | bytes 12320 | tf_op jit(solution)/shard_map/ppermute | solution.py:325
  15.2 3.1 %collective-permute-start.9 = (f32[16,128]{1,0:T(8,128)S(1)}, f32[16,128]{1,0:T(8,128)S(1)}, u32[]{:S(2)}, u32[]{:S(2)}) collective-permute-start(f32[16,128]{1,0:T(8,128)S(1)} %middle.1.refs_0_), channel_id=1, source_target_pairs={{0,12},{4,8},{8,4},{12,0},{1,13},{5,9},{9,5},{13,1},{2,14},{6,10},... | collective-permute-start | bytes 24584 | tf_op jit(solution)/shard_map/ppermute | solution.py:325
  18.3 1.4 %collective-permute-start.7 = (f32[16,128]{1,0:T(8,128)S(1)}, f32[16,128]{1,0:T(8,128)S(1)}, u32[]{:S(2)}, u32[]{:S(2)}) collective-permute-start(f32[16,128]{1,0:T(8,128)S(1)} %middle.1.refs_0_), channel_id=1, source_target_pairs={{0,4},{4,0},{8,12},{12,8},{1,5},{5,1},{9,13},{13,9},{2,6},{6,2},{1... | collective-permute-start | bytes 24584 | tf_op jit(solution)/shard_map/ppermute | solution.py:325
  19.7 2.1 %share.1.share_ref = f32[10,512,512]{2,1,0:T(8,128)S(1)} custom-call(s32[4,4]{1,0:T(4,128)S(4)} %get-tuple-element.17.class_ref, f32[1,2048]{1,0:T(1,128)S(1)} %bitcast.6, bf16[256,2048]{1,0:T(8,128)(2,1)S(1)} %get-tuple-element.18.both, bf16[2048,256]{1,0:T(8,128)(2,1)S(1)} %get-tuple-element.19.turned, f32[2048,128]{1,0:T(8,128)S(1)} %get-tuple-element.20.column, ...), custom_call_target="tpu_custom_call" | custom-call | flops 1342177280 | bytes 10485760 | tf_op jit(solution)/shard_map/share/pallas_call | solution.py:424
  21.9 1.0 %collective-permute-done.8.refs_2_ = f32[16,128]{1,0:T(8,128)S(1)} collective-permute-done((f32[16,128]{1,0:T(8,128)S(1)}, f32[16,128]{1,0:T(8,128)S(1)}, u32[]{:S(2)}, u32[]{:S(2)}) %collective-permute-start.8) | collective-permute-done | bytes 8224 | tf_op jit(solution)/shard_map/ppermute | solution.py:325
  22.8 1.9 %second.1 = (f32[8,128]{1,0:T(8,128)S(1)}, f32[8,128]{1,0:T(8,128)S(1)}, f32[8,128]{1,0:T(8,128)S(1)}, f32[8,128]{1,0:T(8,128)S(1)}, f32[8,128]{1,0:T(8,128)S(1)}) custom-call(s32[4,4]{1,0:T(4,128)S(4)} %get-tuple-element.17.class_ref, f32[10,512,512]{2,1,0:T(8,128)S(1)} %share.1.share_ref, f32[16,128]{1,0:T(8,128)S(1)} %get-tuple-element.23.innovations_ref, ...), custom_call_target="tpu_custom_call" | custom-call | tf_op jit(solution)/shard_map/second/pallas_call | solution.py:437
  24.7 2.0 %collective-permute-start.10 = (f32[8,128]{1,0:T(8,128)S(1)}, f32[8,128]{1,0:T(8,128)S(1)}, u32[]{:S(2)}, u32[]{:S(2)}) collective-permute-start(f32[8,128]{1,0:T(8,128)S(1)} %get-tuple-element.27), channel_id=1, source_target_pairs={{0,12},{4,8},{8,4},{12,0},{1,13},{5,9},{9,5},{13,1},{2,14},{6,10},... | collective-permute-start | bytes 12296 | tf_op jit(solution)/shard_map/ppermute | solution.py:325
  26.8 0.1 collective-permute-start.11
  26.8 2.3 %collective-permute-start.12 = (f32[8,128]{1,0:T(8,128)S(1)}, f32[8,128]{1,0:T(8,128)S(1)}, u32[]{:S(2)}, u32[]{:S(2)}) collective-permute-start(f32[8,128]{1,0:T(8,128)S(1)} %get-tuple-element.29), channel_id=1, source_target_pairs={{0,4},{4,0},{8,12},{12,8},{1,5},{5,1},{9,13},{13,9},{2,6},{6,2},{1... | collective-permute-start | bytes 12296 | tf_op jit(solution)/shard_map/ppermute | solution.py:325
  29.1 1.0 %collective-permute-done.10.refs_1_ = f32[8,128]{1,0:T(8,128)S(1)} collective-permute-done((f32[8,128]{1,0:T(8,128)S(1)}, f32[8,128]{1,0:T(8,128)S(1)}, u32[]{:S(2)}, u32[]{:S(2)}) %collective-permute-start.10) | collective-permute-done | bytes 4128 | tf_op jit(solution)/shard_map/ppermute | solution.py:325
  30.1 1.2 %collective-permute-done.11.refs_2_ = f32[8,128]{1,0:T(8,128)S(1)} collective-permute-done((f32[8,128]{1,0:T(8,128)S(1)}, f32[8,128]{1,0:T(8,128)S(1)}, u32[]{:S(2)}, u32[]{:S(2)}) %collective-permute-start.11) | collective-permute-done | bytes 4128 | tf_op jit(solution)/shard_map/ppermute | solution.py:325
  31.3 0.5 %last.1 = (f32[1,128]{1,0:T(1,128)}, f32[1,128]{1,0:T(1,128)}) custom-call(f32[8,128]{1,0:T(8,128)S(1)} %get-tuple-element.25.state_ref, f32[8,128]{1,0:T(8,128)S(1)} %get-tuple-element.26.refs_0_, f32[8,128]{1,0:T(8,128)S(1)} %collective-permute-done.10.refs_1_, f32[8,128]{1,0:T(8,128)S(1)} %collective-permute-done.11.refs_2_, ...), custom_call_target="tpu_custom_call" | custom-call | tf_op jit(solution)/shard_map/last/pallas_call | solution.py:451
  (18 shorter events, 0.1 us)
Async XLA Ops:
  0.6 5.9 %collective-permute-start = (bf16[128,2048]{1,0:T(8,128)(2,1)}, bf16[128,2048]{1,0:T(8,128)(2,1)S(1)}, u32[]{:S(2)}, u32[]{:S(2)}) collective-permute-start(bf16[128,2048]{1,0:T(8,128)(2,1)} %own_ref.1), channel_id=1, source_target_pairs={{0,1},{1,0},{2,3},{3,2},{4,5},{5,4},{6,7},{7,6},{8,9},{9,8},{10,11... | collective-permute-start | bytes 1572872 | tf_op jit(solution)/shard_map/ppermute | solution.py:352
  1.1 5.6 %copy-start = (f32[2048]{0:T(1024)S(1)}, f32[2048]{0:T(1024)}, u32[]{:S(2)}) copy-start(f32[2048]{0:T(1024)} %param.8) | copy-start | bytes 24580
  1.2 5.6 %copy-start.3 = (bf16[128,2048]{1,0:T(8,128)(2,1)S(1)}, bf16[128,2048]{1,0:T(8,128)(2,1)}, u32[]{:S(2)}) copy-start(bf16[128,2048]{1,0:T(8,128)(2,1)} %own_ref.1) | copy-start | bytes 1572868
  1.2 9.3 %copy-start.1 = (f32[128]{0:T(128)S(1)}, f32[128]{0:T(128)}, u32[]{:S(2)}) copy-start(f32[128]{0:T(128)} %param.7) | copy-start | bytes 1540
  1.2 9.3 %copy-start.2 = (f32[128]{0:T(128)S(1)}, f32[128]{0:T(128)}, u32[]{:S(2)}) copy-start(f32[128]{0:T(128)} %param.6) | copy-start | bytes 1540
  1.2 7.9 %collective-permute-start.3 = (f32[1,128]{1,0:T(1,128)}, f32[1,128]{1,0:T(1,128)S(1)}, u32[]{:S(2)}, u32[]{:S(2)}) collective-permute-start(f32[1,128]{1,0:T(1,128)} %bitcast.8), channel_id=1, source_target_pairs={{0,12},{4,8},{8,4},{12,0},{1,13},{5,9},{9,5},{13,1},{2,14},{6,10},... | collective-permute-start | bytes 1544 | tf_op jit(solution)/shard_map/ppermute | solution.py:325
  5.9 4.6 %collective-permute-start.2 = (f32[1,128]{1,0:T(1,128)}, f32[1,128]{1,0:T(1,128)S(1)}, u32[]{:S(2)}, u32[]{:S(2)}) collective-permute-start(f32[1,128]{1,0:T(1,128)} %bitcast.9), channel_id=1, source_target_pairs={{0,8},{4,12},{8,0},{12,4},{1,9},{5,13},{9,1},{13,5},{2,10},{6,14},... | collective-permute-start | bytes 1544 | tf_op jit(solution)/shard_map/ppermute | solution.py:325
  5.9 4.6 %collective-permute-start.1 = (f32[1,128]{1,0:T(1,128)}, f32[1,128]{1,0:T(1,128)S(1)}, u32[]{:S(2)}, u32[]{:S(2)}) collective-permute-start(f32[1,128]{1,0:T(1,128)} %bitcast.10), channel_id=1, source_target_pairs={{0,4},{4,0},{8,12},{12,8},{1,5},{5,1},{9,13},{13,9},{2,6},{6,2},{1... | collective-permute-start | bytes 1544 | tf_op jit(solution)/shard_map/ppermute | solution.py:325
  11.3 3.3 %collective-permute-start.6 = (f32[24,128]{1,0:T(8,128)S(1)}, f32[24,128]{1,0:T(8,128)S(1)}, u32[]{:S(2)}, u32[]{:S(2)}) collective-permute-start(f32[24,128]{1,0:T(8,128)S(1)} %first.1.refs_0_), channel_id=1, source_target_pairs={{0,3},{1,2},{2,1},{3,0},{4,7},{5,6},{6,5},{7,4},{8,11},{9,10},{10,... | collective-permute-start | bytes 36872 | tf_op jit(solution)/shard_map/ppermute | solution.py:325
  11.5 3.7 %collective-permute-start.5 = (f32[24,128]{1,0:T(8,128)S(1)}, f32[24,128]{1,0:T(8,128)S(1)}, u32[]{:S(2)}, u32[]{:S(2)}) collective-permute-start(f32[24,128]{1,0:T(8,128)S(1)} %first.1.refs_0_), channel_id=1, source_target_pairs={{0,2},{1,3},{2,0},{3,1},{4,6},{5,7},{6,4},{7,5},{8,10},{9,11},{10,... | collective-permute-start | bytes 36872 | tf_op jit(solution)/shard_map/ppermute | solution.py:325
  13.0 2.3 %collective-permute-start.4 = (f32[24,128]{1,0:T(8,128)S(1)}, f32[24,128]{1,0:T(8,128)S(1)}, u32[]{:S(2)}, u32[]{:S(2)}) collective-permute-start(f32[24,128]{1,0:T(8,128)S(1)} %first.1.refs_0_), channel_id=1, source_target_pairs={{0,1},{1,0},{2,3},{3,2},{4,5},{5,4},{6,7},{7,6},{8,9},{9,8},{10,11... | collective-permute-start | bytes 36872 | tf_op jit(solution)/shard_map/ppermute | solution.py:325
  15.2 6.6 %collective-permute-start.9 = (f32[16,128]{1,0:T(8,128)S(1)}, f32[16,128]{1,0:T(8,128)S(1)}, u32[]{:S(2)}, u32[]{:S(2)}) collective-permute-start(f32[16,128]{1,0:T(8,128)S(1)} %middle.1.refs_0_), channel_id=1, source_target_pairs={{0,12},{4,8},{8,4},{12,0},{1,13},{5,9},{9,5},{13,1},{2,14},{6,10},... | collective-permute-start | bytes 24584 | tf_op jit(solution)/shard_map/ppermute | solution.py:325
  18.3 4.5 %collective-permute-start.8 = (f32[16,128]{1,0:T(8,128)S(1)}, f32[16,128]{1,0:T(8,128)S(1)}, u32[]{:S(2)}, u32[]{:S(2)}) collective-permute-start(f32[16,128]{1,0:T(8,128)S(1)} %middle.1.refs_0_), channel_id=1, source_target_pairs={{0,8},{4,12},{8,0},{12,4},{1,9},{5,13},{9,1},{13,5},{2,10},{6,14},... | collective-permute-start | bytes 24584 | tf_op jit(solution)/shard_map/ppermute | solution.py:325
  18.3 4.5 %collective-permute-start.7 = (f32[16,128]{1,0:T(8,128)S(1)}, f32[16,128]{1,0:T(8,128)S(1)}, u32[]{:S(2)}, u32[]{:S(2)}) collective-permute-start(f32[16,128]{1,0:T(8,128)S(1)} %middle.1.refs_0_), channel_id=1, source_target_pairs={{0,4},{4,0},{8,12},{12,8},{1,5},{5,1},{9,13},{13,9},{2,6},{6,2},{1... | collective-permute-start | bytes 24584 | tf_op jit(solution)/shard_map/ppermute | solution.py:325
  24.7 5.4 %collective-permute-start.10 = (f32[8,128]{1,0:T(8,128)S(1)}, f32[8,128]{1,0:T(8,128)S(1)}, u32[]{:S(2)}, u32[]{:S(2)}) collective-permute-start(f32[8,128]{1,0:T(8,128)S(1)} %get-tuple-element.27), channel_id=1, source_target_pairs={{0,12},{4,8},{8,4},{12,0},{1,13},{5,9},{9,5},{13,1},{2,14},{6,10},... | collective-permute-start | bytes 12296 | tf_op jit(solution)/shard_map/ppermute | solution.py:325
  26.8 4.5 %collective-permute-start.11 = (f32[8,128]{1,0:T(8,128)S(1)}, f32[8,128]{1,0:T(8,128)S(1)}, u32[]{:S(2)}, u32[]{:S(2)}) collective-permute-start(f32[8,128]{1,0:T(8,128)S(1)} %get-tuple-element.28), channel_id=1, source_target_pairs={{0,8},{4,12},{8,0},{12,4},{1,9},{5,13},{9,1},{13,5},{2,10},{6,14},... | collective-permute-start | bytes 12296 | tf_op jit(solution)/shard_map/ppermute | solution.py:325
  26.8 4.5 %collective-permute-start.12 = (f32[8,128]{1,0:T(8,128)S(1)}, f32[8,128]{1,0:T(8,128)S(1)}, u32[]{:S(2)}, u32[]{:S(2)}) collective-permute-start(f32[8,128]{1,0:T(8,128)S(1)} %get-tuple-element.29), channel_id=1, source_target_pairs={{0,4},{4,0},{8,12},{12,8},{1,5},{5,1},{9,13},{13,9},{2,6},{6,2},{1... | collective-permute-start | bytes 12296 | tf_op jit(solution)/shard_map/ppermute | solution.py:325

commit v8 on v7

--- a/solution.py
+++ b/solution.py
@@ -76,16 +76,13 @@
         at, columns_at = chunk_of(a), block_at(b, block_len)
         make_part(target, turned[at, :], both[:, columns_at], column[at, :], pos_ref[:, columns_at])
 
-    def make_diagonal(slot, carry):
-        row_strip(row_strips.at[slot], slot, slot)
-        return carry
-
     def make_pair(slot, a, b):
         row_strip(row_strips.at[slot + tiles], a, b)
         at, columns_at = block_at(a, block_len), chunk_of(b)
         make_part(column_strips.at[slot], turned[at, :], both[:, columns_at], column[at, :], pos_ref[:, columns_at])
 
-    lax.fori_loop(0, tiles, make_diagonal, 0)
+    for slot in range(tiles):
+        row_strip(row_strips.at[slot], slot, slot)
     class_copy.wait()
     for_each_pair(reach_tiles, class_ref, make_pair)
 
@@ -221,18 +218,15 @@
                 totals[lane] = term if totals[lane] is None else totals[lane] + term
         return totals
 
-    def add_diagonal(a, carry):
-        weight = tile_weight(class_ref[a, a], reach_tiles, inverse_members)
-        add_sums(sums.at[:, block_at(a, block_len)], weight, sums_of_rows(row_strips.at[a], a))
-        return carry
-
     def add_pair(slot, a, b):
         weight = tile_weight(class_ref[a, b], reach_tiles, inverse_members)
         add_sums(sums.at[:, block_at(b, block_len)], weight, sums_of_rows(row_strips.at[slot + tiles], a))
         across[...] = column_strips[slot] * vector[pl.ds(b, 1), :]
         add_turned(sums.at[:, block_at(a, block_len)], weight, across)
 
-    lax.fori_loop(0, tiles, add_diagonal, 0)
+    for a in range(tiles):
+        weight = tile_weight(class_ref[a, a], reach_tiles, inverse_members)
+        add_sums(sums.at[:, a * block_len : (a + 1) * block_len], weight, sums_of_rows(row_strips.at[a], a))
     for_each_pair(reach_tiles, class_ref, add_pair)
     fold_sums(sums, out_ref)
     own = row_index * per_row + within

time: 32 us -> 31.4 us (0.981)
  Pallas kernels: 7.89 us -> 7.31 us
    pallas_call x1, Pallas kernels: 2.28 us -> 1.84 us  [vectors_only(): pl.pallas_call(functools.partial(strips_kernel, reach_tiles), out_shape=[...]
  transfers between devices with their start and end apart: 13 -> 13, of which waited for: 6 -> 6; matrix products, arithmetic and copies ran while one was open for 0% -> 0% of each run, Pallas kernels for 14% -> 13%
where the time goes in v8:
time: 31.4 us; the launch traced here: 31.3 us
  starting transfers between devices  16.6 us (53%)
  Pallas kernels  7.31 us (23%)
  waiting for transfers between devices  6.58 us (21%)
  between operations  0.72 us (2%)
    ppermute x12, starting transfers between devices, exchange(): lax.ppermute(value, axes, [(i, i ^ mask) for i in range(count)])  16.1 us
    ppermute x12, waiting for transfers between devices, exchange(): lax.ppermute(value, axes, [(i, i ^ mask) for i in range(count)])  6.57 us
    pallas_call x1, Pallas kernels, vectors_only(): pl.pallas_call(functools.partial(share_kernel, reach_tiles), out_shape=pl...  2.12 us
    pallas_call x1, Pallas kernels, vectors_only(): pl.pallas_call(functools.partial(second_kernel, reach_tiles, inverse_memb...  1.88 us
    pallas_call x1, Pallas kernels, vectors_only(): pl.pallas_call(functools.partial(strips_kernel, reach_tiles), out_shape=[...  1.84 us
    pallas_call x1, Pallas kernels, vectors_only(): pl.pallas_call(functools.partial(first_kernel, reach_tiles, inverse_membe...  0.74 us
  transfers between devices with their start and end apart: 13, of which 6 were waited for; matrix products, arithmetic and copies ran while one was open for 0% of the time, Pallas kernels for 13%

profile of v8, /device:TPU:0, one launch (start us, length us, event | category | flops | bytes accessed | tf_op | source)
XLA Modules:
  0.0 31.3 jit_solution(12628573954897392667)
XLA Ops:
  0.6 0.5 %collective-permute-start = (bf16[128,2048]{1,0:T(8,128)(2,1)}, bf16[128,2048]{1,0:T(8,128)(2,1)S(1)}, u32[]{:S(2)}, u32[]{:S(2)}) collective-permute-start(bf16[128,2048]{1,0:T(8,128)(2,1)} %own_ref.1), channel_id=1, source_target_pairs={{0,1},{1,0},{2,3},{3,2},{4,5},{5,4},{6,7},{7,6},{8,9},{9,8},{10,11... | collective-permute-start | bytes 1572872 | tf_op jit(solution)/shard_map/ppermute | solution.py:346
  1.2 4.7 %collective-permute-start.3 = (f32[1,128]{1,0:T(1,128)}, f32[1,128]{1,0:T(1,128)S(1)}, u32[]{:S(2)}, u32[]{:S(2)}) collective-permute-start(f32[1,128]{1,0:T(1,128)} %bitcast.8), channel_id=1, source_target_pairs={{0,12},{4,8},{8,4},{12,0},{1,13},{5,9},{9,5},{13,1},{2,14},{6,10},... | collective-permute-start | bytes 1544 | tf_op jit(solution)/shard_map/ppermute | solution.py:319
  5.9 0.0 collective-permute-start.2
  5.9 0.6 %collective-permute-start.1 = (f32[1,128]{1,0:T(1,128)}, f32[1,128]{1,0:T(1,128)S(1)}, u32[]{:S(2)}, u32[]{:S(2)}) collective-permute-start(f32[1,128]{1,0:T(1,128)} %bitcast.10), channel_id=1, source_target_pairs={{0,4},{4,0},{8,12},{12,8},{1,5},{5,1},{9,13},{13,9},{2,6},{6,2},{1... | collective-permute-start | bytes 1544 | tf_op jit(solution)/shard_map/ppermute | solution.py:319
  6.5 0.2 turn.1.turned_mate_ref
  6.7 1.8 %strips.1 = (f32[10,128,512]{2,1,0:T(8,128)S(1)}, f32[6,512,128]{2,1,0:T(8,128)S(1)}, s32[4,4]{1,0:T(4,128)S(4)}, bf16[256,2048]{1,0:T(8,128)(2,1)S(1)}, bf16[20...) custom-call(s32[4,4]{1,0:T(4,128)} %class_hbm.1, f32[1,2048]{1,0:T(1,128)S(1)} %bitcast.5, ...), custom_call_target="tpu_custom_call" | custom-call | flops 671088640 | bytes 5242880 | tf_op jit(solution)/shard_map/strips/pallas_call | solution.py:366
  8.6 1.9 %collective-permute-done.2.refs_2_ = f32[1,128]{1,0:T(1,128)S(1)} collective-permute-done((f32[1,128]{1,0:T(1,128)}, f32[1,128]{1,0:T(1,128)S(1)}, u32[]{:S(2)}, u32[]{:S(2)}) %collective-permute-start.2) | collective-permute-done | bytes 544 | tf_op jit(solution)/shard_map/ppermute | solution.py:319
  10.4 0.7 %first.1.refs_0_ = f32[24,128]{1,0:T(8,128)S(1)} custom-call(s32[4,4]{1,0:T(4,128)S(4)} %get-tuple-element.17.class_ref, f32[10,128,512]{2,1,0:T(8,128)S(1)} %get-tuple-element.21.row_strips, f32[6,512,128]{2,1,0:T(8,128)S(1)} %get-tuple-element.22.column_strips, f32[1,128]{1,0:T(1,128)S(1)} %bitcast.7, f32[1,128]{1,0:T(1,128)S(1)} %bitcast.11, ...), custom_call_target="tpu_custom_call" | custom-call | tf_op jit(solution)/shard_map/first/pallas_call | solution.py:388
  11.2 0.2 collective-permute-start.6
  11.4 1.4 %collective-permute-start.5 = (f32[24,128]{1,0:T(8,128)S(1)}, f32[24,128]{1,0:T(8,128)S(1)}, u32[]{:S(2)}, u32[]{:S(2)}) collective-permute-start(f32[24,128]{1,0:T(8,128)S(1)} %first.1.refs_0_), channel_id=1, source_target_pairs={{0,2},{1,3},{2,0},{3,1},{4,6},{5,7},{6,4},{7,5},{8,10},{9,11},{10,... | collective-permute-start | bytes 36872 | tf_op jit(solution)/shard_map/ppermute | solution.py:319
  12.8 0.3 collective-permute-start.4
  13.1 1.3 %collective-permute-done.6.refs_3_ = f32[24,128]{1,0:T(8,128)S(1)} collective-permute-done((f32[24,128]{1,0:T(8,128)S(1)}, f32[24,128]{1,0:T(8,128)S(1)}, u32[]{:S(2)}, u32[]{:S(2)}) %collective-permute-start.6) | collective-permute-done | bytes 12320 | tf_op jit(solution)/shard_map/ppermute | solution.py:319
  14.5 0.6 %collective-permute-done.5.refs_2_ = f32[24,128]{1,0:T(8,128)S(1)} collective-permute-done((f32[24,128]{1,0:T(8,128)S(1)}, f32[24,128]{1,0:T(8,128)S(1)}, u32[]{:S(2)}, u32[]{:S(2)}) %collective-permute-start.5) | collective-permute-done | bytes 12320 | tf_op jit(solution)/shard_map/ppermute | solution.py:319
  15.1 2.6 %collective-permute-start.9 = (f32[16,128]{1,0:T(8,128)S(1)}, f32[16,128]{1,0:T(8,128)S(1)}, u32[]{:S(2)}, u32[]{:S(2)}) collective-permute-start(f32[16,128]{1,0:T(8,128)S(1)} %middle.1.refs_0_), channel_id=1, source_target_pairs={{0,12},{4,8},{8,4},{12,0},{1,13},{5,9},{9,5},{13,1},{2,14},{6,10},... | collective-permute-start | bytes 24584 | tf_op jit(solution)/shard_map/ppermute | solution.py:319
  17.7 1.8 %collective-permute-start.7 = (f32[16,128]{1,0:T(8,128)S(1)}, f32[16,128]{1,0:T(8,128)S(1)}, u32[]{:S(2)}, u32[]{:S(2)}) collective-permute-start(f32[16,128]{1,0:T(8,128)S(1)} %middle.1.refs_0_), channel_id=1, source_target_pairs={{0,4},{4,0},{8,12},{12,8},{1,5},{5,1},{9,13},{13,9},{2,6},{6,2},{1... | collective-permute-start | bytes 24584 | tf_op jit(solution)/shard_map/ppermute | solution.py:319
  19.6 2.1 %share.1.share_ref = f32[10,512,512]{2,1,0:T(8,128)S(1)} custom-call(s32[4,4]{1,0:T(4,128)S(4)} %get-tuple-element.17.class_ref, f32[1,2048]{1,0:T(1,128)S(1)} %bitcast.6, bf16[256,2048]{1,0:T(8,128)(2,1)S(1)} %get-tuple-element.18.both, bf16[2048,256]{1,0:T(8,128)(2,1)S(1)} %get-tuple-element.19.turned, f32[2048,128]{1,0:T(8,128)S(1)} %get-tuple-element.20.column, ...), custom_call_target="tpu_custom_call" | custom-call | flops 1342177280 | bytes 10485760 | tf_op jit(solution)/shard_map/share/pallas_call | solution.py:418
  21.7 0.5 %collective-permute-done.8.refs_2_ = f32[16,128]{1,0:T(8,128)S(1)} collective-permute-done((f32[16,128]{1,0:T(8,128)S(1)}, f32[16,128]{1,0:T(8,128)S(1)}, u32[]{:S(2)}, u32[]{:S(2)}) %collective-permute-start.8) | collective-permute-done | bytes 8224 | tf_op jit(solution)/shard_map/ppermute | solution.py:319
  22.3 1.9 %second.1 = (f32[8,128]{1,0:T(8,128)S(1)}, f32[8,128]{1,0:T(8,128)S(1)}, f32[8,128]{1,0:T(8,128)S(1)}, f32[8,128]{1,0:T(8,128)S(1)}, f32[8,128]{1,0:T(8,128)S(1)}) custom-call(s32[4,4]{1,0:T(4,128)S(4)} %get-tuple-element.17.class_ref, f32[10,512,512]{2,1,0:T(8,128)S(1)} %share.1.share_ref, f32[16,128]{1,0:T(8,128)S(1)} %get-tuple-element.23.innovations_ref, ...), custom_call_target="tpu_custom_call" | custom-call | tf_op jit(solution)/shard_map/second/pallas_call | solution.py:431
  24.1 2.0 %collective-permute-start.10 = (f32[8,128]{1,0:T(8,128)S(1)}, f32[8,128]{1,0:T(8,128)S(1)}, u32[]{:S(2)}, u32[]{:S(2)}) collective-permute-start(f32[8,128]{1,0:T(8,128)S(1)} %get-tuple-element.27), channel_id=1, source_target_pairs={{0,12},{4,8},{8,4},{12,0},{1,13},{5,9},{9,5},{13,1},{2,14},{6,10},... | collective-permute-start | bytes 12296 | tf_op jit(solution)/shard_map/ppermute | solution.py:319
  26.2 0.4 %collective-permute-start.11 = (f32[8,128]{1,0:T(8,128)S(1)}, f32[8,128]{1,0:T(8,128)S(1)}, u32[]{:S(2)}, u32[]{:S(2)}) collective-permute-start(f32[8,128]{1,0:T(8,128)S(1)} %get-tuple-element.28), channel_id=1, source_target_pairs={{0,8},{4,12},{8,0},{12,4},{1,9},{5,13},{9,1},{13,5},{2,10},{6,14},... | collective-permute-start | bytes 12296 | tf_op jit(solution)/shard_map/ppermute | solution.py:319
  26.6 2.0 %collective-permute-start.12 = (f32[8,128]{1,0:T(8,128)S(1)}, f32[8,128]{1,0:T(8,128)S(1)}, u32[]{:S(2)}, u32[]{:S(2)}) collective-permute-start(f32[8,128]{1,0:T(8,128)S(1)} %get-tuple-element.29), channel_id=1, source_target_pairs={{0,4},{4,0},{8,12},{12,8},{1,5},{5,1},{9,13},{13,9},{2,6},{6,2},{1... | collective-permute-start | bytes 12296 | tf_op jit(solution)/shard_map/ppermute | solution.py:319
  28.5 1.0 %collective-permute-done.10.refs_1_ = f32[8,128]{1,0:T(8,128)S(1)} collective-permute-done((f32[8,128]{1,0:T(8,128)S(1)}, f32[8,128]{1,0:T(8,128)S(1)}, u32[]{:S(2)}, u32[]{:S(2)}) %collective-permute-start.10) | collective-permute-done | bytes 4128 | tf_op jit(solution)/shard_map/ppermute | solution.py:319
  29.6 1.2 %collective-permute-done.11.refs_2_ = f32[8,128]{1,0:T(8,128)S(1)} collective-permute-done((f32[8,128]{1,0:T(8,128)S(1)}, f32[8,128]{1,0:T(8,128)S(1)}, u32[]{:S(2)}, u32[]{:S(2)}) %collective-permute-start.11) | collective-permute-done | bytes 4128 | tf_op jit(solution)/shard_map/ppermute | solution.py:319
  30.7 0.5 %last.1 = (f32[1,128]{1,0:T(1,128)}, f32[1,128]{1,0:T(1,128)}) custom-call(f32[8,128]{1,0:T(8,128)S(1)} %get-tuple-element.25.state_ref, f32[8,128]{1,0:T(8,128)S(1)} %get-tuple-element.26.refs_0_, f32[8,128]{1,0:T(8,128)S(1)} %collective-permute-done.10.refs_1_, f32[8,128]{1,0:T(8,128)S(1)} %collective-permute-done.11.refs_2_, ...), custom_call_target="tpu_custom_call" | custom-call | tf_op jit(solution)/shard_map/last/pallas_call | solution.py:445
  (18 shorter events, 0.1 us)
Async XLA Ops:
  0.6 5.9 %collective-permute-start = (bf16[128,2048]{1,0:T(8,128)(2,1)}, bf16[128,2048]{1,0:T(8,128)(2,1)S(1)}, u32[]{:S(2)}, u32[]{:S(2)}) collective-permute-start(bf16[128,2048]{1,0:T(8,128)(2,1)} %own_ref.1), channel_id=1, source_target_pairs={{0,1},{1,0},{2,3},{3,2},{4,5},{5,4},{6,7},{7,6},{8,9},{9,8},{10,11... | collective-permute-start | bytes 1572872 | tf_op jit(solution)/shard_map/ppermute | solution.py:346
  1.1 5.6 %copy-start = (f32[2048]{0:T(1024)S(1)}, f32[2048]{0:T(1024)}, u32[]{:S(2)}) copy-start(f32[2048]{0:T(1024)} %param.8) | copy-start | bytes 24580
  1.2 5.6 %copy-start.3 = (bf16[128,2048]{1,0:T(8,128)(2,1)S(1)}, bf16[128,2048]{1,0:T(8,128)(2,1)}, u32[]{:S(2)}) copy-start(bf16[128,2048]{1,0:T(8,128)(2,1)} %own_ref.1) | copy-start | bytes 1572868
  1.2 9.3 %copy-start.1 = (f32[128]{0:T(128)S(1)}, f32[128]{0:T(128)}, u32[]{:S(2)}) copy-start(f32[128]{0:T(128)} %param.7) | copy-start | bytes 1540
  1.2 9.3 %copy-start.2 = (f32[128]{0:T(128)S(1)}, f32[128]{0:T(128)}, u32[]{:S(2)}) copy-start(f32[128]{0:T(128)} %param.6) | copy-start | bytes 1540
  1.2 7.4 %collective-permute-start.3 = (f32[1,128]{1,0:T(1,128)}, f32[1,128]{1,0:T(1,128)S(1)}, u32[]{:S(2)}, u32[]{:S(2)}) collective-permute-start(f32[1,128]{1,0:T(1,128)} %bitcast.8), channel_id=1, source_target_pairs={{0,12},{4,8},{8,4},{12,0},{1,13},{5,9},{9,5},{13,1},{2,14},{6,10},... | collective-permute-start | bytes 1544 | tf_op jit(solution)/shard_map/ppermute | solution.py:319
  5.9 4.6 %collective-permute-start.2 = (f32[1,128]{1,0:T(1,128)}, f32[1,128]{1,0:T(1,128)S(1)}, u32[]{:S(2)}, u32[]{:S(2)}) collective-permute-start(f32[1,128]{1,0:T(1,128)} %bitcast.9), channel_id=1, source_target_pairs={{0,8},{4,12},{8,0},{12,4},{1,9},{5,13},{9,1},{13,5},{2,10},{6,14},... | collective-permute-start | bytes 1544 | tf_op jit(solution)/shard_map/ppermute | solution.py:319
  5.9 4.6 %collective-permute-start.1 = (f32[1,128]{1,0:T(1,128)}, f32[1,128]{1,0:T(1,128)S(1)}, u32[]{:S(2)}, u32[]{:S(2)}) collective-permute-start(f32[1,128]{1,0:T(1,128)} %bitcast.10), channel_id=1, source_target_pairs={{0,4},{4,0},{8,12},{12,8},{1,5},{5,1},{9,13},{13,9},{2,6},{6,2},{1... | collective-permute-start | bytes 1544 | tf_op jit(solution)/shard_map/ppermute | solution.py:319
  11.2 3.3 %collective-permute-start.6 = (f32[24,128]{1,0:T(8,128)S(1)}, f32[24,128]{1,0:T(8,128)S(1)}, u32[]{:S(2)}, u32[]{:S(2)}) collective-permute-start(f32[24,128]{1,0:T(8,128)S(1)} %first.1.refs_0_), channel_id=1, source_target_pairs={{0,3},{1,2},{2,1},{3,0},{4,7},{5,6},{6,5},{7,4},{8,11},{9,10},{10,... | collective-permute-start | bytes 36872 | tf_op jit(solution)/shard_map/ppermute | solution.py:319
  11.4 3.7 %collective-permute-start.5 = (f32[24,128]{1,0:T(8,128)S(1)}, f32[24,128]{1,0:T(8,128)S(1)}, u32[]{:S(2)}, u32[]{:S(2)}) collective-permute-start(f32[24,128]{1,0:T(8,128)S(1)} %first.1.refs_0_), channel_id=1, source_target_pairs={{0,2},{1,3},{2,0},{3,1},{4,6},{5,7},{6,4},{7,5},{8,10},{9,11},{10,... | collective-permute-start | bytes 36872 | tf_op jit(solution)/shard_map/ppermute | solution.py:319
  12.8 2.3 %collective-permute-start.4 = (f32[24,128]{1,0:T(8,128)S(1)}, f32[24,128]{1,0:T(8,128)S(1)}, u32[]{:S(2)}, u32[]{:S(2)}) collective-permute-start(f32[24,128]{1,0:T(8,128)S(1)} %first.1.refs_0_), channel_id=1, source_target_pairs={{0,1},{1,0},{2,3},{3,2},{4,5},{5,4},{6,7},{7,6},{8,9},{9,8},{10,11... | collective-permute-start | bytes 36872 | tf_op jit(solution)/shard_map/ppermute | solution.py:319
  15.1 6.6 %collective-permute-start.9 = (f32[16,128]{1,0:T(8,128)S(1)}, f32[16,128]{1,0:T(8,128)S(1)}, u32[]{:S(2)}, u32[]{:S(2)}) collective-permute-start(f32[16,128]{1,0:T(8,128)S(1)} %middle.1.refs_0_), channel_id=1, source_target_pairs={{0,12},{4,8},{8,4},{12,0},{1,13},{5,9},{9,5},{13,1},{2,14},{6,10},... | collective-permute-start | bytes 24584 | tf_op jit(solution)/shard_map/ppermute | solution.py:319
  17.7 4.5 %collective-permute-start.8 = (f32[16,128]{1,0:T(8,128)S(1)}, f32[16,128]{1,0:T(8,128)S(1)}, u32[]{:S(2)}, u32[]{:S(2)}) collective-permute-start(f32[16,128]{1,0:T(8,128)S(1)} %middle.1.refs_0_), channel_id=1, source_target_pairs={{0,8},{4,12},{8,0},{12,4},{1,9},{5,13},{9,1},{13,5},{2,10},{6,14},... | collective-permute-start | bytes 24584 | tf_op jit(solution)/shard_map/ppermute | solution.py:319
  17.7 4.5 %collective-permute-start.7 = (f32[16,128]{1,0:T(8,128)S(1)}, f32[16,128]{1,0:T(8,128)S(1)}, u32[]{:S(2)}, u32[]{:S(2)}) collective-permute-start(f32[16,128]{1,0:T(8,128)S(1)} %middle.1.refs_0_), channel_id=1, source_target_pairs={{0,4},{4,0},{8,12},{12,8},{1,5},{5,1},{9,13},{13,9},{2,6},{6,2},{1... | collective-permute-start | bytes 24584 | tf_op jit(solution)/shard_map/ppermute | solution.py:319
  24.1 5.4 %collective-permute-start.10 = (f32[8,128]{1,0:T(8,128)S(1)}, f32[8,128]{1,0:T(8,128)S(1)}, u32[]{:S(2)}, u32[]{:S(2)}) collective-permute-start(f32[8,128]{1,0:T(8,128)S(1)} %get-tuple-element.27), channel_id=1, source_target_pairs={{0,12},{4,8},{8,4},{12,0},{1,13},{5,9},{9,5},{13,1},{2,14},{6,10},... | collective-permute-start | bytes 12296 | tf_op jit(solution)/shard_map/ppermute | solution.py:319
  26.2 4.5 %collective-permute-start.11 = (f32[8,128]{1,0:T(8,128)S(1)}, f32[8,128]{1,0:T(8,128)S(1)}, u32[]{:S(2)}, u32[]{:S(2)}) collective-permute-start(f32[8,128]{1,0:T(8,128)S(1)} %get-tuple-element.28), channel_id=1, source_target_pairs={{0,8},{4,12},{8,0},{12,4},{1,9},{5,13},{9,1},{13,5},{2,10},{6,14},... | collective-permute-start | bytes 12296 | tf_op jit(solution)/shard_map/ppermute | solution.py:319
  26.6 4.2 %collective-permute-start.12 = (f32[8,128]{1,0:T(8,128)S(1)}, f32[8,128]{1,0:T(8,128)S(1)}, u32[]{:S(2)}, u32[]{:S(2)}) collective-permute-start(f32[8,128]{1,0:T(8,128)S(1)} %get-tuple-element.29), channel_id=1, source_target_pairs={{0,4},{4,0},{8,12},{12,8},{1,5},{5,1},{9,13},{13,9},{2,6},{6,2},{1... | collective-permute-start | bytes 12296 | tf_op jit(solution)/shard_map/ppermute | solution.py:319

commit v9 on v8

--- a/solution.py
+++ b/solution.py
@@ -36,6 +36,14 @@
         return carry
 
     lax.fori_loop(0, off_diagonal(tiles), one_pair, 0)
+
+
+def each_pair(reach_tiles, class_ref, action):
+    tiles = class_ref.shape[0]
+    for a in range(tiles):
+        for b in range(a + 1, tiles):
+            slot = first_slot(a, tiles) + b - a - 1
+            pl.when(class_ref[a, b] < reach_tiles)(functools.partial(action, slot, a, b))
 
 
 def block_at(a, block_len):
@@ -84,7 +92,7 @@
     for slot in range(tiles):
         row_strip(row_strips.at[slot], slot, slot)
     class_copy.wait()
-    for_each_pair(reach_tiles, class_ref, make_pair)
+    each_pair(reach_tiles, class_ref, make_pair)
 
 
 def share_kernel(reach_tiles, class_ref, pos_ref, both, turned, column, row_strips, share_ref):
@@ -103,12 +111,9 @@
             at = pl.ds(pl.multiple_of(a * block_len + begin, LANES), LANES)
             make_part(tile.at[here, :], turned[at, :], right, column[at, :], right_pos)
 
-    def make_diagonal(slot, carry):
+    for slot in range(tiles):
         make_tile(slot, slot, slot)
-        return carry
-
-    lax.fori_loop(0, tiles, make_diagonal, 0)
-    for_each_pair(reach_tiles, class_ref, lambda slot, a, b: make_tile(slot + tiles, a, b))
+    each_pair(reach_tiles, class_ref, lambda slot, a, b: make_tile(slot + tiles, a, b))
 
 
 def spread_columns(row, column):
@@ -153,7 +158,7 @@
     lanes = block_len // LANES
     sums[...] = jnp.zeros_like(sums)
 
-    def add_diagonal(a, carry):
+    def add_diagonal(a):
         at = block_at(a, block_len)
         tile, factor = share_ref.at[a], column.at[at, :]
         totals = [None] * lanes
@@ -163,7 +168,6 @@
                 term = tile[part, lane * LANES : (lane + 1) * LANES] * factor[part, :]
                 totals[lane] = term if totals[lane] is None else totals[lane] + term
         add_sums(sums.at[:, at], tile_weight(class_ref[a, a], reach_tiles, inverse_members), totals)
-        return carry
 
     def add_pair(slot, a, b):
         weight = tile_weight(class_ref[a, b], reach_tiles, inverse_members)
@@ -184,8 +188,9 @@
         add_sums(sums.at[:, at_b], weight, totals)
         add_turned(sums.at[:, at_a], weight, across)
 
-    lax.fori_loop(0, tiles, add_diagonal, 0)
-    for_each_pair(reach_tiles, class_ref, add_pair)
+    for a in range(tiles):
+        add_diagonal(a)
+    each_pair(reach_tiles, class_ref, add_pair)
     fold_sums(sums, out_ref)
 
 
@@ -227,7 +232,7 @@
     for a in range(tiles):
         weight = tile_weight(class_ref[a, a], reach_tiles, inverse_members)
         add_sums(sums.at[:, a * block_len : (a + 1) * block_len], weight, sums_of_rows(row_strips.at[a], a))
-    for_each_pair(reach_tiles, class_ref, add_pair)
+    each_pair(reach_tiles, class_ref, add_pair)
     fold_sums(sums, out_ref)
     own = row_index * per_row + within
     out_ref[pl.ds(own, 1), :] += error_ref[...] * chunks[0][...]

time: 31.4 us -> 30.1 us (0.959)
  Pallas kernels: 7.31 us -> 6 us
    pallas_call x1, Pallas kernels: 1.88 us -> 1.28 us  [vectors_only(): pl.pallas_call(functools.partial(second_kernel, reach_tiles, inverse_memb...]
    pallas_call x1, Pallas kernels: 2.12 us -> 1.64 us  [vectors_only(): pl.pallas_call(functools.partial(share_kernel, reach_tiles), out_shape=pl...]
  transfers between devices with their start and end apart: 13 -> 13, of which waited for: 6 -> 7; matrix products, arithmetic and copies ran while one was open for 0% -> 0% of each run, Pallas kernels for 13% -> 12%
where the time goes in v9:
time: 30.1 us; the launch traced here: 30 us
  starting transfers between devices  16.6 us (55%)
  waiting for transfers between devices  6.6 us (22%)
  Pallas kernels  6 us (20%)
  between operations  0.72 us (2%)
    ppermute x12, starting transfers between devices, exchange(): lax.ppermute(value, axes, [(i, i ^ mask) for i in range(count)])  16.1 us
    ppermute x12, waiting for transfers between devices, exchange(): lax.ppermute(value, axes, [(i, i ^ mask) for i in range(count)])  6.6 us
    pallas_call x1, Pallas kernels, vectors_only(): pl.pallas_call(functools.partial(strips_kernel, reach_tiles), out_shape=[...  1.72 us
    pallas_call x1, Pallas kernels, vectors_only(): pl.pallas_call(functools.partial(share_kernel, reach_tiles), out_shape=pl...  1.64 us
    pallas_call x1, Pallas kernels, vectors_only(): pl.pallas_call(functools.partial(second_kernel, reach_tiles, inverse_memb...  1.28 us
    pallas_call x1, Pallas kernels, vectors_only(): pl.pallas_call(functools.partial(first_kernel, reach_tiles, inverse_membe...  0.61 us
  transfers between devices with their start and end apart: 13, of which 7 were waited for; matrix products, arithmetic and copies ran while one was open for 0% of the time, Pallas kernels for 12%

profile of v9, /device:TPU:0, one launch (start us, length us, event | category | flops | bytes accessed | tf_op | source)
XLA Modules:
  0.0 30.0 jit_solution(11449507935641191400)
XLA Ops:
  0.6 0.5 %collective-permute-start = (bf16[128,2048]{1,0:T(8,128)(2,1)}, bf16[128,2048]{1,0:T(8,128)(2,1)S(1)}, u32[]{:S(2)}, u32[]{:S(2)}) collective-permute-start(bf16[128,2048]{1,0:T(8,128)(2,1)} %own_ref.1), channel_id=1, source_target_pairs={{0,1},{1,0},{2,3},{3,2},{4,5},{5,4},{6,7},{7,6},{8,9},{9,8},{10,11... | collective-permute-start | bytes 1572872 | tf_op jit(solution)/shard_map/ppermute | solution.py:351
  1.2 4.7 %collective-permute-start.3 = (f32[1,128]{1,0:T(1,128)}, f32[1,128]{1,0:T(1,128)S(1)}, u32[]{:S(2)}, u32[]{:S(2)}) collective-permute-start(f32[1,128]{1,0:T(1,128)} %bitcast.8), channel_id=1, source_target_pairs={{0,12},{4,8},{8,4},{12,0},{1,13},{5,9},{9,5},{13,1},{2,14},{6,10},... | collective-permute-start | bytes 1544 | tf_op jit(solution)/shard_map/ppermute | solution.py:324
  5.9 0.6 %collective-permute-start.1 = (f32[1,128]{1,0:T(1,128)}, f32[1,128]{1,0:T(1,128)S(1)}, u32[]{:S(2)}, u32[]{:S(2)}) collective-permute-start(f32[1,128]{1,0:T(1,128)} %bitcast.10), channel_id=1, source_target_pairs={{0,4},{4,0},{8,12},{12,8},{1,5},{5,1},{9,13},{13,9},{2,6},{6,2},{1... | collective-permute-start | bytes 1544 | tf_op jit(solution)/shard_map/ppermute | solution.py:324
  6.5 0.2 turn.1.turned_mate_ref
  6.7 1.7 %strips.1 = (f32[10,128,512]{2,1,0:T(8,128)S(1)}, f32[6,512,128]{2,1,0:T(8,128)S(1)}, s32[4,4]{1,0:T(4,128)S(4)}, bf16[256,2048]{1,0:T(8,128)(2,1)S(1)}, bf16[20...) custom-call(s32[4,4]{1,0:T(4,128)} %class_hbm.1, f32[1,2048]{1,0:T(1,128)S(1)} %bitcast.5, ...), custom_call_target="tpu_custom_call" | custom-call | flops 671088640 | bytes 5242880 | tf_op jit(solution)/shard_map/strips/pallas_call | solution.py:371
  8.5 2.0 %collective-permute-done.2.refs_2_ = f32[1,128]{1,0:T(1,128)S(1)} collective-permute-done((f32[1,128]{1,0:T(1,128)}, f32[1,128]{1,0:T(1,128)S(1)}, u32[]{:S(2)}, u32[]{:S(2)}) %collective-permute-start.2) | collective-permute-done | bytes 544 | tf_op jit(solution)/shard_map/ppermute | solution.py:324
  10.4 0.6 %first.1.refs_0_ = f32[24,128]{1,0:T(8,128)S(1)} custom-call(s32[4,4]{1,0:T(4,128)S(4)} %get-tuple-element.17.class_ref, f32[10,128,512]{2,1,0:T(8,128)S(1)} %get-tuple-element.21.row_strips, f32[6,512,128]{2,1,0:T(8,128)S(1)} %get-tuple-element.22.column_strips, f32[1,128]{1,0:T(1,128)S(1)} %bitcast.7, f32[1,128]{1,0:T(1,128)S(1)} %bitcast.11, ...), custom_call_target="tpu_custom_call" | custom-call | tf_op jit(solution)/shard_map/first/pallas_call | solution.py:393
  11.1 0.2 collective-permute-start.6
  11.3 1.4 %collective-permute-start.5 = (f32[24,128]{1,0:T(8,128)S(1)}, f32[24,128]{1,0:T(8,128)S(1)}, u32[]{:S(2)}, u32[]{:S(2)}) collective-permute-start(f32[24,128]{1,0:T(8,128)S(1)} %first.1.refs_0_), channel_id=1, source_target_pairs={{0,2},{1,3},{2,0},{3,1},{4,6},{5,7},{6,4},{7,5},{8,10},{9,11},{10,... | collective-permute-start | bytes 36872 | tf_op jit(solution)/shard_map/ppermute | solution.py:324
  12.7 0.3 collective-permute-start.4
  13.0 1.3 %collective-permute-done.6.refs_3_ = f32[24,128]{1,0:T(8,128)S(1)} collective-permute-done((f32[24,128]{1,0:T(8,128)S(1)}, f32[24,128]{1,0:T(8,128)S(1)}, u32[]{:S(2)}, u32[]{:S(2)}) %collective-permute-start.6) | collective-permute-done | bytes 12320 | tf_op jit(solution)/shard_map/ppermute | solution.py:324
  14.3 0.6 %collective-permute-done.5.refs_2_ = f32[24,128]{1,0:T(8,128)S(1)} collective-permute-done((f32[24,128]{1,0:T(8,128)S(1)}, f32[24,128]{1,0:T(8,128)S(1)}, u32[]{:S(2)}, u32[]{:S(2)}) %collective-permute-start.5) | collective-permute-done | bytes 12320 | tf_op jit(solution)/shard_map/ppermute | solution.py:324
  15.0 2.5 %collective-permute-start.9 = (f32[16,128]{1,0:T(8,128)S(1)}, f32[16,128]{1,0:T(8,128)S(1)}, u32[]{:S(2)}, u32[]{:S(2)}) collective-permute-start(f32[16,128]{1,0:T(8,128)S(1)} %middle.1.refs_0_), channel_id=1, source_target_pairs={{0,12},{4,8},{8,4},{12,0},{1,13},{5,9},{9,5},{13,1},{2,14},{6,10},... | collective-permute-start | bytes 24584 | tf_op jit(solution)/shard_map/ppermute | solution.py:324
  17.5 2.0 %collective-permute-start.7 = (f32[16,128]{1,0:T(8,128)S(1)}, f32[16,128]{1,0:T(8,128)S(1)}, u32[]{:S(2)}, u32[]{:S(2)}) collective-permute-start(f32[16,128]{1,0:T(8,128)S(1)} %middle.1.refs_0_), channel_id=1, source_target_pairs={{0,4},{4,0},{8,12},{12,8},{1,5},{5,1},{9,13},{13,9},{2,6},{6,2},{1... | collective-permute-start | bytes 24584 | tf_op jit(solution)/shard_map/ppermute | solution.py:324
  19.4 1.6 %share.1.share_ref = f32[10,512,512]{2,1,0:T(8,128)S(1)} custom-call(s32[4,4]{1,0:T(4,128)S(4)} %get-tuple-element.17.class_ref, f32[1,2048]{1,0:T(1,128)S(1)} %bitcast.6, bf16[256,2048]{1,0:T(8,128)(2,1)S(1)} %get-tuple-element.18.both, bf16[2048,256]{1,0:T(8,128)(2,1)S(1)} %get-tuple-element.19.turned, f32[2048,128]{1,0:T(8,128)S(1)} %get-tuple-element.20.column, ...), custom_call_target="tpu_custom_call" | custom-call | flops 1342177280 | bytes 10485760 | tf_op jit(solution)/shard_map/share/pallas_call | solution.py:423
  21.1 0.9 %collective-permute-done.8.refs_2_ = f32[16,128]{1,0:T(8,128)S(1)} collective-permute-done((f32[16,128]{1,0:T(8,128)S(1)}, f32[16,128]{1,0:T(8,128)S(1)}, u32[]{:S(2)}, u32[]{:S(2)}) %collective-permute-start.8) | collective-permute-done | bytes 8224 | tf_op jit(solution)/shard_map/ppermute | solution.py:324
  22.0 1.3 %second.1 = (f32[8,128]{1,0:T(8,128)S(1)}, f32[8,128]{1,0:T(8,128)S(1)}, f32[8,128]{1,0:T(8,128)S(1)}, f32[8,128]{1,0:T(8,128)S(1)}, f32[8,128]{1,0:T(8,128)S(1)}) custom-call(s32[4,4]{1,0:T(4,128)S(4)} %get-tuple-element.17.class_ref, f32[10,512,512]{2,1,0:T(8,128)S(1)} %share.1.share_ref, f32[16,128]{1,0:T(8,128)S(1)} %get-tuple-element.23.innovations_ref, ...), custom_call_target="tpu_custom_call" | custom-call | tf_op jit(solution)/shard_map/second/pallas_call | solution.py:436
  23.3 1.6 %collective-permute-start.10 = (f32[8,128]{1,0:T(8,128)S(1)}, f32[8,128]{1,0:T(8,128)S(1)}, u32[]{:S(2)}, u32[]{:S(2)}) collective-permute-start(f32[8,128]{1,0:T(8,128)S(1)} %get-tuple-element.27), channel_id=1, source_target_pairs={{0,12},{4,8},{8,4},{12,0},{1,13},{5,9},{9,5},{13,1},{2,14},{6,10},... | collective-permute-start | bytes 12296 | tf_op jit(solution)/shard_map/ppermute | solution.py:324
  24.9 0.9 %collective-permute-start.11 = (f32[8,128]{1,0:T(8,128)S(1)}, f32[8,128]{1,0:T(8,128)S(1)}, u32[]{:S(2)}, u32[]{:S(2)}) collective-permute-start(f32[8,128]{1,0:T(8,128)S(1)} %get-tuple-element.28), channel_id=1, source_target_pairs={{0,8},{4,12},{8,0},{12,4},{1,9},{5,13},{9,1},{13,5},{2,10},{6,14},... | collective-permute-start | bytes 12296 | tf_op jit(solution)/shard_map/ppermute | solution.py:324
  25.8 1.9 %collective-permute-start.12 = (f32[8,128]{1,0:T(8,128)S(1)}, f32[8,128]{1,0:T(8,128)S(1)}, u32[]{:S(2)}, u32[]{:S(2)}) collective-permute-start(f32[8,128]{1,0:T(8,128)S(1)} %get-tuple-element.29), channel_id=1, source_target_pairs={{0,4},{4,0},{8,12},{12,8},{1,5},{5,1},{9,13},{13,9},{2,6},{6,2},{1... | collective-permute-start | bytes 12296 | tf_op jit(solution)/shard_map/ppermute | solution.py:324
  27.7 1.0 %collective-permute-done.10.refs_1_ = f32[8,128]{1,0:T(8,128)S(1)} collective-permute-done((f32[8,128]{1,0:T(8,128)S(1)}, f32[8,128]{1,0:T(8,128)S(1)}, u32[]{:S(2)}, u32[]{:S(2)}) %collective-permute-start.10) | collective-permute-done | bytes 4128 | tf_op jit(solution)/shard_map/ppermute | solution.py:324
  28.7 0.7 %collective-permute-done.11.refs_2_ = f32[8,128]{1,0:T(8,128)S(1)} collective-permute-done((f32[8,128]{1,0:T(8,128)S(1)}, f32[8,128]{1,0:T(8,128)S(1)}, u32[]{:S(2)}, u32[]{:S(2)}) %collective-permute-start.11) | collective-permute-done | bytes 4128 | tf_op jit(solution)/shard_map/ppermute | solution.py:324
  29.4 0.1 collective-permute-done.12.refs_3_
  29.4 0.5 %last.1 = (f32[1,128]{1,0:T(1,128)}, f32[1,128]{1,0:T(1,128)}) custom-call(f32[8,128]{1,0:T(8,128)S(1)} %get-tuple-element.25.state_ref, f32[8,128]{1,0:T(8,128)S(1)} %get-tuple-element.26.refs_0_, f32[8,128]{1,0:T(8,128)S(1)} %collective-permute-done.10.refs_1_, f32[8,128]{1,0:T(8,128)S(1)} %collective-permute-done.11.refs_2_, ...), custom_call_target="tpu_custom_call" | custom-call | tf_op jit(solution)/shard_map/last/pallas_call | solution.py:450
  (18 shorter events, 0.1 us)
Async XLA Ops:
  0.6 5.9 %collective-permute-start = (bf16[128,2048]{1,0:T(8,128)(2,1)}, bf16[128,2048]{1,0:T(8,128)(2,1)S(1)}, u32[]{:S(2)}, u32[]{:S(2)}) collective-permute-start(bf16[128,2048]{1,0:T(8,128)(2,1)} %own_ref.1), channel_id=1, source_target_pairs={{0,1},{1,0},{2,3},{3,2},{4,5},{5,4},{6,7},{7,6},{8,9},{9,8},{10,11... | collective-permute-start | bytes 1572872 | tf_op jit(solution)/shard_map/ppermute | solution.py:351
  1.1 5.6 %copy-start = (f32[2048]{0:T(1024)S(1)}, f32[2048]{0:T(1024)}, u32[]{:S(2)}) copy-start(f32[2048]{0:T(1024)} %param.8) | copy-start | bytes 24580
  1.2 5.6 %copy-start.3 = (bf16[128,2048]{1,0:T(8,128)(2,1)S(1)}, bf16[128,2048]{1,0:T(8,128)(2,1)}, u32[]{:S(2)}) copy-start(bf16[128,2048]{1,0:T(8,128)(2,1)} %own_ref.1) | copy-start | bytes 1572868
  1.2 9.3 %copy-start.1 = (f32[128]{0:T(128)S(1)}, f32[128]{0:T(128)}, u32[]{:S(2)}) copy-start(f32[128]{0:T(128)} %param.7) | copy-start | bytes 1540
  1.2 9.3 %copy-start.2 = (f32[128]{0:T(128)S(1)}, f32[128]{0:T(128)}, u32[]{:S(2)}) copy-start(f32[128]{0:T(128)} %param.6) | copy-start | bytes 1540
  1.2 7.3 %collective-permute-start.3 = (f32[1,128]{1,0:T(1,128)}, f32[1,128]{1,0:T(1,128)S(1)}, u32[]{:S(2)}, u32[]{:S(2)}) collective-permute-start(f32[1,128]{1,0:T(1,128)} %bitcast.8), channel_id=1, source_target_pairs={{0,12},{4,8},{8,4},{12,0},{1,13},{5,9},{9,5},{13,1},{2,14},{6,10},... | collective-permute-start | bytes 1544 | tf_op jit(solution)/shard_map/ppermute | solution.py:324
  5.9 4.6 %collective-permute-start.2 = (f32[1,128]{1,0:T(1,128)}, f32[1,128]{1,0:T(1,128)S(1)}, u32[]{:S(2)}, u32[]{:S(2)}) collective-permute-start(f32[1,128]{1,0:T(1,128)} %bitcast.9), channel_id=1, source_target_pairs={{0,8},{4,12},{8,0},{12,4},{1,9},{5,13},{9,1},{13,5},{2,10},{6,14},... | collective-permute-start | bytes 1544 | tf_op jit(solution)/shard_map/ppermute | solution.py:324
  5.9 4.6 %collective-permute-start.1 = (f32[1,128]{1,0:T(1,128)}, f32[1,128]{1,0:T(1,128)S(1)}, u32[]{:S(2)}, u32[]{:S(2)}) collective-permute-start(f32[1,128]{1,0:T(1,128)} %bitcast.10), channel_id=1, source_target_pairs={{0,4},{4,0},{8,12},{12,8},{1,5},{5,1},{9,13},{13,9},{2,6},{6,2},{1... | collective-permute-start | bytes 1544 | tf_op jit(solution)/shard_map/ppermute | solution.py:324
  11.1 3.3 %collective-permute-start.6 = (f32[24,128]{1,0:T(8,128)S(1)}, f32[24,128]{1,0:T(8,128)S(1)}, u32[]{:S(2)}, u32[]{:S(2)}) collective-permute-start(f32[24,128]{1,0:T(8,128)S(1)} %first.1.refs_0_), channel_id=1, source_target_pairs={{0,3},{1,2},{2,1},{3,0},{4,7},{5,6},{6,5},{7,4},{8,11},{9,10},{10,... | collective-permute-start | bytes 36872 | tf_op jit(solution)/shard_map/ppermute | solution.py:324
  11.3 3.7 %collective-permute-start.5 = (f32[24,128]{1,0:T(8,128)S(1)}, f32[24,128]{1,0:T(8,128)S(1)}, u32[]{:S(2)}, u32[]{:S(2)}) collective-permute-start(f32[24,128]{1,0:T(8,128)S(1)} %first.1.refs_0_), channel_id=1, source_target_pairs={{0,2},{1,3},{2,0},{3,1},{4,6},{5,7},{6,4},{7,5},{8,10},{9,11},{10,... | collective-permute-start | bytes 36872 | tf_op jit(solution)/shard_map/ppermute | solution.py:324
  12.7 2.3 %collective-permute-start.4 = (f32[24,128]{1,0:T(8,128)S(1)}, f32[24,128]{1,0:T(8,128)S(1)}, u32[]{:S(2)}, u32[]{:S(2)}) collective-permute-start(f32[24,128]{1,0:T(8,128)S(1)} %first.1.refs_0_), channel_id=1, source_target_pairs={{0,1},{1,0},{2,3},{3,2},{4,5},{5,4},{6,7},{7,6},{8,9},{9,8},{10,11... | collective-permute-start | bytes 36872 | tf_op jit(solution)/shard_map/ppermute | solution.py:324
  15.0 6.1 %collective-permute-start.9 = (f32[16,128]{1,0:T(8,128)S(1)}, f32[16,128]{1,0:T(8,128)S(1)}, u32[]{:S(2)}, u32[]{:S(2)}) collective-permute-start(f32[16,128]{1,0:T(8,128)S(1)} %middle.1.refs_0_), channel_id=1, source_target_pairs={{0,12},{4,8},{8,4},{12,0},{1,13},{5,9},{9,5},{13,1},{2,14},{6,10},... | collective-permute-start | bytes 24584 | tf_op jit(solution)/shard_map/ppermute | solution.py:324
  17.5 4.5 %collective-permute-start.8 = (f32[16,128]{1,0:T(8,128)S(1)}, f32[16,128]{1,0:T(8,128)S(1)}, u32[]{:S(2)}, u32[]{:S(2)}) collective-permute-start(f32[16,128]{1,0:T(8,128)S(1)} %middle.1.refs_0_), channel_id=1, source_target_pairs={{0,8},{4,12},{8,0},{12,4},{1,9},{5,13},{9,1},{13,5},{2,10},{6,14},... | collective-permute-start | bytes 24584 | tf_op jit(solution)/shard_map/ppermute | solution.py:324
  17.5 4.5 %collective-permute-start.7 = (f32[16,128]{1,0:T(8,128)S(1)}, f32[16,128]{1,0:T(8,128)S(1)}, u32[]{:S(2)}, u32[]{:S(2)}) collective-permute-start(f32[16,128]{1,0:T(8,128)S(1)} %middle.1.refs_0_), channel_id=1, source_target_pairs={{0,4},{4,0},{8,12},{12,8},{1,5},{5,1},{9,13},{13,9},{2,6},{6,2},{1... | collective-permute-start | bytes 24584 | tf_op jit(solution)/shard_map/ppermute | solution.py:324
  23.3 5.4 %collective-permute-start.10 = (f32[8,128]{1,0:T(8,128)S(1)}, f32[8,128]{1,0:T(8,128)S(1)}, u32[]{:S(2)}, u32[]{:S(2)}) collective-permute-start(f32[8,128]{1,0:T(8,128)S(1)} %get-tuple-element.27), channel_id=1, source_target_pairs={{0,12},{4,8},{8,4},{12,0},{1,13},{5,9},{9,5},{13,1},{2,14},{6,10},... | collective-permute-start | bytes 12296 | tf_op jit(solution)/shard_map/ppermute | solution.py:324
  24.9 4.5 %collective-permute-start.11 = (f32[8,128]{1,0:T(8,128)S(1)}, f32[8,128]{1,0:T(8,128)S(1)}, u32[]{:S(2)}, u32[]{:S(2)}) collective-permute-start(f32[8,128]{1,0:T(8,128)S(1)} %get-tuple-element.28), channel_id=1, source_target_pairs={{0,8},{4,12},{8,0},{12,4},{1,9},{5,13},{9,1},{13,5},{2,10},{6,14},... | collective-permute-start | bytes 12296 | tf_op jit(solution)/shard_map/ppermute | solution.py:324
  25.8 3.6 %collective-permute-start.12 = (f32[8,128]{1,0:T(8,128)S(1)}, f32[8,128]{1,0:T(8,128)S(1)}, u32[]{:S(2)}, u32[]{:S(2)}) collective-permute-start(f32[8,128]{1,0:T(8,128)S(1)} %get-tuple-element.29), channel_id=1, source_target_pairs={{0,4},{4,0},{8,12},{12,8},{1,5},{5,1},{9,13},{13,9},{2,6},{6,2},{1... | collective-permute-start | bytes 12296 | tf_op jit(solution)/shard_map/ppermute | solution.py:324

commit v10 on v9

--- a/solution.py
+++ b/solution.py
@@ -22,20 +22,6 @@
 
 def first_slot(a, tiles):
     return a * tiles - (a * (a + 1)) // 2
-
-
-def for_each_pair(reach_tiles, class_ref, action):
-    tiles = class_ref.shape[0]
-
-    def one_pair(slot, carry):
-        a = jnp.int32(0)
-        for row in range(1, tiles - 1):
-            a = a + (slot >= first_slot(row, tiles)).astype(jnp.int32)
-        b = slot - first_slot(a, tiles) + a + 1
-        pl.when(class_ref[a, b] < reach_tiles)(lambda: action(slot, a, b))
-        return carry
-
-    lax.fori_loop(0, off_diagonal(tiles), one_pair, 0)
 
 
 def each_pair(reach_tiles, class_ref, action):
@@ -266,7 +252,7 @@
 def second_kernel(reach_tiles, inverse_members, peers, class_ref, share_ref, innovations_ref, error_ref, *refs):
     parts, refs = refs[:peers], refs[peers:]
     sent, refs = refs[:peers], refs[peers:]
-    state_ref, direction, residual, start, column, across, sums, product = refs
+    state_ref, direction, residual, start, whole_image, column, across, sums, product = refs
     row_index, within, per_row = place()
     innovations = innovations_ref[...]
     image = parts[0][...]
@@ -275,16 +261,20 @@
     norm_now = total_of(innovations * innovations)
     alpha = norm_now / total_of(innovations * image)
     residual_now = innovations - alpha * image
+    residual[...] = residual_now
+    spread_vector(residual, column)
     norm_next = total_of(residual_now * residual_now)
-    direction_now = residual_now + (norm_next / norm_now) * innovations
-    residual[...] = residual_now
+    ratio = norm_next / norm_now
+    direction_now = residual_now + ratio * innovations
     direction[...] = direction_now
     start[...] = alpha * innovations
-    spread_vector(direction, column)
-    shared = (class_ref, share_ref, direction, column, across, sums, product)
+    whole_image[...] = image
+    carried = ratio * total_of(direction_now * image)
+    shared = (class_ref, share_ref, residual, column, across, sums, product)
     apply_share(reach_tiles, inverse_members, *shared)
-    of_row = direction[pl.ds(row_index * per_row, per_row), :]
-    curvature = total_of(direction_now * product[...]) + total_of(error_ref[...] * of_row * of_row)
+    of_row = pl.ds(row_index * per_row, per_row)
+    curvature = total_of(direction[...] * product[...])
+    curvature = curvature + total_of(error_ref[...] * residual[of_row, :] * direction[of_row, :])
     for peer in range(peers):
         at = (row_index ^ peer) * per_row + within
         sent[peer][0:1, :] = product[pl.ds(at, 1), :]
@@ -293,15 +283,15 @@
     state_ref[0:1, :] = start[own, :]
     state_ref[1:2, :] = residual[own, :]
     state_ref[2:3, :] = direction[own, :]
-    state_ref[3:4, :] = error_ref[pl.ds(within, 1), :] * direction[own, :]
+    state_ref[3:4, :] = error_ref[pl.ds(within, 1), :] * residual[own, :] + ratio * whole_image[own, :]
     state_ref[4:5, :] = jnp.broadcast_to(norm_next, (1, LANES))
+    state_ref[5:6, :] = jnp.broadcast_to(carried, (1, LANES))
 
 
 def last_kernel(state_ref, *refs):
     parts, (solution_ref, residual_ref) = refs[:-2], refs[-2:]
-    image = state_ref[3:4, :] + parts[0][0:1, :]
-    curvature = parts[0][1:2, :]
-    for part in parts[1:]:
+    image, curvature = state_ref[3:4, :], state_ref[5:6, :]
+    for part in parts:
         image = image + part[0:1, :]
         curvature = curvature + part[1:2, :]
     alpha = state_ref[4:5, :] / curvature
@@ -328,6 +318,12 @@
 
 def nearest_first(count):
     return tuple(range(count))
+
+
+def farthest_pair_last(count):
+    masks = list(range(count))
+    masks[-2:] = masks[:-3:-1]
+    return tuple(masks)
 
 
 def farthest_first(count):
@@ -351,7 +347,7 @@
     mate = lax.ppermute(anomalies, "sub", [(0, 1), (1, 0)])
     chunk = innovations.reshape(1, LANES)
     error = obs_error.reshape(1, LANES)
-    chunk_order = nearest_first(row_count)
+    chunk_order = farthest_pair_last(row_count)
     chunks = exchange(row, chunk_order, [chunk] * row_count)
 
     work = [pltpu.VMEM((block_len, LANES), f32), pltpu.VMEM((8, total_obs), f32)]
@@ -438,7 +434,7 @@
         out_shape=[pltpu.VMEM((8, LANES), f32) for _ in range(row_count + 1)],
         in_specs=[SMEM_SPEC] + [VMEM_SPEC] * (row_count + 3),
         out_specs=[VMEM_SPEC] * (row_count + 1),
-        scratch_shapes=[pltpu.VMEM((pieces, LANES), f32)] * 3
+        scratch_shapes=[pltpu.VMEM((pieces, LANES), f32)] * 4
         + [pltpu.VMEM((total_obs, LANES), f32)]
         + work
         + [pltpu.VMEM((pieces, LANES), f32)],

time: 30.1 us -> 30 us (level)
  no operation moved by 1% of the time
where the time goes in v10:
time: 30 us; the launch traced here: 29.8 us
  starting transfers between devices  16.6 us (55%)
  waiting for transfers between devices  6.56 us (22%)
  Pallas kernels  5.96 us (20%)
  between operations  0.72 us (2%)
    ppermute x12, starting transfers between devices, exchange(): lax.ppermute(value, axes, [(i, i ^ mask) for i in range(count)])  16 us
    ppermute x12, waiting for transfers between devices, exchange(): lax.ppermute(value, axes, [(i, i ^ mask) for i in range(count)])  6.55 us
    pallas_call x1, Pallas kernels, vectors_only(): pl.pallas_call(functools.partial(strips_kernel, reach_tiles), out_shape=[...  1.72 us
    pallas_call x1, Pallas kernels, vectors_only(): pl.pallas_call(functools.partial(share_kernel, reach_tiles), out_shape=pl...  1.64 us
    pallas_call x1, Pallas kernels, vectors_only(): pl.pallas_call(functools.partial(second_kernel, reach_tiles, inverse_memb...  1.24 us
    pallas_call x1, Pallas kernels, vectors_only(): pl.pallas_call(functools.partial(first_kernel, reach_tiles, inverse_membe...  0.61 us
  transfers between devices with their start and end apart: 13, of which 7 were waited for; matrix products, arithmetic and copies ran while one was open for 0% of the time, Pallas kernels for 12%

profile of v10, /device:TPU:0, one launch (start us, length us, event | category | flops | bytes accessed | tf_op | source)
XLA Modules:
  0.0 29.8 jit_solution(10413304446073504516)
XLA Ops:
  0.6 0.5 %collective-permute-start = (bf16[128,2048]{1,0:T(8,128)(2,1)}, bf16[128,2048]{1,0:T(8,128)(2,1)S(1)}, u32[]{:S(2)}, u32[]{:S(2)}) collective-permute-start(bf16[128,2048]{1,0:T(8,128)(2,1)} %own_ref.1), channel_id=1, source_target_pairs={{0,1},{1,0},{2,3},{3,2},{4,5},{5,4},{6,7},{7,6},{8,9},{9,8},{10,11... | collective-permute-start | bytes 1572872 | tf_op jit(solution)/shard_map/ppermute | solution.py:347
  1.2 3.7 %collective-permute-start.3 = (f32[1,128]{1,0:T(1,128)}, f32[1,128]{1,0:T(1,128)S(1)}, u32[]{:S(2)}, u32[]{:S(2)}) collective-permute-start(f32[1,128]{1,0:T(1,128)} %bitcast.8), channel_id=1, source_target_pairs={{0,8},{4,12},{8,0},{12,4},{1,9},{5,13},{9,1},{13,5},{2,10},{6,14},... | collective-permute-start | bytes 1544 | tf_op jit(solution)/shard_map/ppermute | solution.py:314
  4.9 1.3 %collective-permute-start.2 = (f32[1,128]{1,0:T(1,128)}, f32[1,128]{1,0:T(1,128)S(1)}, u32[]{:S(2)}, u32[]{:S(2)}) collective-permute-start(f32[1,128]{1,0:T(1,128)} %bitcast.9), channel_id=1, source_target_pairs={{0,12},{4,8},{8,4},{12,0},{1,13},{5,9},{9,5},{13,1},{2,14},{6,10},... | collective-permute-start | bytes 1544 | tf_op jit(solution)/shard_map/ppermute | solution.py:314
  6.2 0.2 collective-permute-start.1
  6.6 1.7 %strips.1 = (f32[10,128,512]{2,1,0:T(8,128)S(1)}, f32[6,512,128]{2,1,0:T(8,128)S(1)}, s32[4,4]{1,0:T(4,128)S(4)}, bf16[256,2048]{1,0:T(8,128)(2,1)S(1)}, bf16[20...) custom-call(s32[4,4]{1,0:T(4,128)} %class_hbm.1, f32[1,2048]{1,0:T(1,128)S(1)} %bitcast.5, ...), custom_call_target="tpu_custom_call" | custom-call | flops 671088640 | bytes 5242880 | tf_op jit(solution)/shard_map/strips/pallas_call | solution.py:367
  8.4 1.9 %collective-permute-done.2.refs_2_ = f32[1,128]{1,0:T(1,128)S(1)} collective-permute-done((f32[1,128]{1,0:T(1,128)}, f32[1,128]{1,0:T(1,128)S(1)}, u32[]{:S(2)}, u32[]{:S(2)}) %collective-permute-start.2) | collective-permute-done | bytes 544 | tf_op jit(solution)/shard_map/ppermute | solution.py:314
  10.3 0.6 %first.1.refs_0_ = f32[24,128]{1,0:T(8,128)S(1)} custom-call(s32[4,4]{1,0:T(4,128)S(4)} %get-tuple-element.17.class_ref, f32[10,128,512]{2,1,0:T(8,128)S(1)} %get-tuple-element.21.row_strips, f32[6,512,128]{2,1,0:T(8,128)S(1)} %get-tuple-element.22.column_strips, f32[1,128]{1,0:T(1,128)S(1)} %bitcast.7, f32[1,128]{1,0:T(1,128)S(1)} %bitcast.11, ...), custom_call_target="tpu_custom_call" | custom-call | tf_op jit(solution)/shard_map/first/pallas_call | solution.py:389
  11.0 0.2 collective-permute-start.6
  11.2 1.4 %collective-permute-start.5 = (f32[24,128]{1,0:T(8,128)S(1)}, f32[24,128]{1,0:T(8,128)S(1)}, u32[]{:S(2)}, u32[]{:S(2)}) collective-permute-start(f32[24,128]{1,0:T(8,128)S(1)} %first.1.refs_0_), channel_id=1, source_target_pairs={{0,2},{1,3},{2,0},{3,1},{4,6},{5,7},{6,4},{7,5},{8,10},{9,11},{10,... | collective-permute-start | bytes 36872 | tf_op jit(solution)/shard_map/ppermute | solution.py:314
  12.6 0.3 collective-permute-start.4
  12.9 1.3 %collective-permute-done.6.refs_3_ = f32[24,128]{1,0:T(8,128)S(1)} collective-permute-done((f32[24,128]{1,0:T(8,128)S(1)}, f32[24,128]{1,0:T(8,128)S(1)}, u32[]{:S(2)}, u32[]{:S(2)}) %collective-permute-start.6) | collective-permute-done | bytes 12320 | tf_op jit(solution)/shard_map/ppermute | solution.py:314
  14.2 0.6 %collective-permute-done.5.refs_2_ = f32[24,128]{1,0:T(8,128)S(1)} collective-permute-done((f32[24,128]{1,0:T(8,128)S(1)}, f32[24,128]{1,0:T(8,128)S(1)}, u32[]{:S(2)}, u32[]{:S(2)}) %collective-permute-start.5) | collective-permute-done | bytes 12320 | tf_op jit(solution)/shard_map/ppermute | solution.py:314
  14.9 2.0 %collective-permute-start.9 = (f32[16,128]{1,0:T(8,128)S(1)}, f32[16,128]{1,0:T(8,128)S(1)}, u32[]{:S(2)}, u32[]{:S(2)}) collective-permute-start(f32[16,128]{1,0:T(8,128)S(1)} %middle.1.refs_0_), channel_id=1, source_target_pairs={{0,12},{4,8},{8,4},{12,0},{1,13},{5,9},{9,5},{13,1},{2,14},{6,10},... | collective-permute-start | bytes 24584 | tf_op jit(solution)/shard_map/ppermute | solution.py:314
  16.9 2.4 %collective-permute-start.7 = (f32[16,128]{1,0:T(8,128)S(1)}, f32[16,128]{1,0:T(8,128)S(1)}, u32[]{:S(2)}, u32[]{:S(2)}) collective-permute-start(f32[16,128]{1,0:T(8,128)S(1)} %middle.1.refs_0_), channel_id=1, source_target_pairs={{0,4},{4,0},{8,12},{12,8},{1,5},{5,1},{9,13},{13,9},{2,6},{6,2},{1... | collective-permute-start | bytes 24584 | tf_op jit(solution)/shard_map/ppermute | solution.py:314
  19.3 1.6 %share.1.share_ref = f32[10,512,512]{2,1,0:T(8,128)S(1)} custom-call(s32[4,4]{1,0:T(4,128)S(4)} %get-tuple-element.17.class_ref, f32[1,2048]{1,0:T(1,128)S(1)} %bitcast.6, bf16[256,2048]{1,0:T(8,128)(2,1)S(1)} %get-tuple-element.18.both, bf16[2048,256]{1,0:T(8,128)(2,1)S(1)} %get-tuple-element.19.turned, f32[2048,128]{1,0:T(8,128)S(1)} %get-tuple-element.20.column, ...), custom_call_target="tpu_custom_call" | custom-call | flops 1342177280 | bytes 10485760 | tf_op jit(solution)/shard_map/share/pallas_call | solution.py:419
  21.0 0.4 %collective-permute-done.8.refs_2_ = f32[16,128]{1,0:T(8,128)S(1)} collective-permute-done((f32[16,128]{1,0:T(8,128)S(1)}, f32[16,128]{1,0:T(8,128)S(1)}, u32[]{:S(2)}, u32[]{:S(2)}) %collective-permute-start.8) | collective-permute-done | bytes 8224 | tf_op jit(solution)/shard_map/ppermute | solution.py:314
  21.5 1.2 %second.1 = (f32[8,128]{1,0:T(8,128)S(1)}, f32[8,128]{1,0:T(8,128)S(1)}, f32[8,128]{1,0:T(8,128)S(1)}, f32[8,128]{1,0:T(8,128)S(1)}, f32[8,128]{1,0:T(8,128)S(1)}) custom-call(s32[4,4]{1,0:T(4,128)S(4)} %get-tuple-element.17.class_ref, f32[10,512,512]{2,1,0:T(8,128)S(1)} %share.1.share_ref, f32[16,128]{1,0:T(8,128)S(1)} %get-tuple-element.23.innovations_ref, ...), custom_call_target="tpu_custom_call" | custom-call | tf_op jit(solution)/shard_map/second/pallas_call | solution.py:432
  22.7 1.9 %collective-permute-start.10 = (f32[8,128]{1,0:T(8,128)S(1)}, f32[8,128]{1,0:T(8,128)S(1)}, u32[]{:S(2)}, u32[]{:S(2)}) collective-permute-start(f32[8,128]{1,0:T(8,128)S(1)} %get-tuple-element.27), channel_id=1, source_target_pairs={{0,12},{4,8},{8,4},{12,0},{1,13},{5,9},{9,5},{13,1},{2,14},{6,10},... | collective-permute-start | bytes 12296 | tf_op jit(solution)/shard_map/ppermute | solution.py:314
  24.6 1.1 %collective-permute-start.11 = (f32[8,128]{1,0:T(8,128)S(1)}, f32[8,128]{1,0:T(8,128)S(1)}, u32[]{:S(2)}, u32[]{:S(2)}) collective-permute-start(f32[8,128]{1,0:T(8,128)S(1)} %get-tuple-element.28), channel_id=1, source_target_pairs={{0,8},{4,12},{8,0},{12,4},{1,9},{5,13},{9,1},{13,5},{2,10},{6,14},... | collective-permute-start | bytes 12296 | tf_op jit(solution)/shard_map/ppermute | solution.py:314
  25.7 1.4 %collective-permute-start.12 = (f32[8,128]{1,0:T(8,128)S(1)}, f32[8,128]{1,0:T(8,128)S(1)}, u32[]{:S(2)}, u32[]{:S(2)}) collective-permute-start(f32[8,128]{1,0:T(8,128)S(1)} %get-tuple-element.29), channel_id=1, source_target_pairs={{0,4},{4,0},{8,12},{12,8},{1,5},{5,1},{9,13},{13,9},{2,6},{6,2},{1... | collective-permute-start | bytes 12296 | tf_op jit(solution)/shard_map/ppermute | solution.py:314
  27.1 1.0 %collective-permute-done.10.refs_1_ = f32[8,128]{1,0:T(8,128)S(1)} collective-permute-done((f32[8,128]{1,0:T(8,128)S(1)}, f32[8,128]{1,0:T(8,128)S(1)}, u32[]{:S(2)}, u32[]{:S(2)}) %collective-permute-start.10) | collective-permute-done | bytes 4128 | tf_op jit(solution)/shard_map/ppermute | solution.py:314
  28.1 1.0 %collective-permute-done.11.refs_2_ = f32[8,128]{1,0:T(8,128)S(1)} collective-permute-done((f32[8,128]{1,0:T(8,128)S(1)}, f32[8,128]{1,0:T(8,128)S(1)}, u32[]{:S(2)}, u32[]{:S(2)}) %collective-permute-start.11) | collective-permute-done | bytes 4128 | tf_op jit(solution)/shard_map/ppermute | solution.py:314
  29.1 0.2 collective-permute-done.12.refs_3_
  29.3 0.5 %last.1 = (f32[1,128]{1,0:T(1,128)}, f32[1,128]{1,0:T(1,128)}) custom-call(f32[8,128]{1,0:T(8,128)S(1)} %get-tuple-element.25.state_ref, f32[8,128]{1,0:T(8,128)S(1)} %get-tuple-element.26.refs_0_, f32[8,128]{1,0:T(8,128)S(1)} %collective-permute-done.10.refs_1_, f32[8,128]{1,0:T(8,128)S(1)} %collective-permute-done.11.refs_2_, ...), custom_call_target="tpu_custom_call" | custom-call | tf_op jit(solution)/shard_map/last/pallas_call | solution.py:446
  (18 shorter events, 0.3 us)
Async XLA Ops:
  0.6 5.8 %collective-permute-start = (bf16[128,2048]{1,0:T(8,128)(2,1)}, bf16[128,2048]{1,0:T(8,128)(2,1)S(1)}, u32[]{:S(2)}, u32[]{:S(2)}) collective-permute-start(bf16[128,2048]{1,0:T(8,128)(2,1)} %own_ref.1), channel_id=1, source_target_pairs={{0,1},{1,0},{2,3},{3,2},{4,5},{5,4},{6,7},{7,6},{8,9},{9,8},{10,11... | collective-permute-start | bytes 1572872 | tf_op jit(solution)/shard_map/ppermute | solution.py:347
  1.1 5.5 %copy-start = (f32[2048]{0:T(1024)S(1)}, f32[2048]{0:T(1024)}, u32[]{:S(2)}) copy-start(f32[2048]{0:T(1024)} %param.8) | copy-start | bytes 24580
  1.2 5.5 %copy-start.3 = (bf16[128,2048]{1,0:T(8,128)(2,1)S(1)}, bf16[128,2048]{1,0:T(8,128)(2,1)}, u32[]{:S(2)}) copy-start(bf16[128,2048]{1,0:T(8,128)(2,1)} %own_ref.1) | copy-start | bytes 1572868
  1.2 9.2 %copy-start.1 = (f32[128]{0:T(128)S(1)}, f32[128]{0:T(128)}, u32[]{:S(2)}) copy-start(f32[128]{0:T(128)} %param.7) | copy-start | bytes 1540
  1.2 9.2 %copy-start.2 = (f32[128]{0:T(128)S(1)}, f32[128]{0:T(128)}, u32[]{:S(2)}) copy-start(f32[128]{0:T(128)} %param.6) | copy-start | bytes 1540
  1.2 7.2 %collective-permute-start.3 = (f32[1,128]{1,0:T(1,128)}, f32[1,128]{1,0:T(1,128)S(1)}, u32[]{:S(2)}, u32[]{:S(2)}) collective-permute-start(f32[1,128]{1,0:T(1,128)} %bitcast.8), channel_id=1, source_target_pairs={{0,8},{4,12},{8,0},{12,4},{1,9},{5,13},{9,1},{13,5},{2,10},{6,14},... | collective-permute-start | bytes 1544 | tf_op jit(solution)/shard_map/ppermute | solution.py:314
  4.9 5.5 %collective-permute-start.2 = (f32[1,128]{1,0:T(1,128)}, f32[1,128]{1,0:T(1,128)S(1)}, u32[]{:S(2)}, u32[]{:S(2)}) collective-permute-start(f32[1,128]{1,0:T(1,128)} %bitcast.9), channel_id=1, source_target_pairs={{0,12},{4,8},{8,4},{12,0},{1,13},{5,9},{9,5},{13,1},{2,14},{6,10},... | collective-permute-start | bytes 1544 | tf_op jit(solution)/shard_map/ppermute | solution.py:314
  6.2 4.1 %collective-permute-start.1 = (f32[1,128]{1,0:T(1,128)}, f32[1,128]{1,0:T(1,128)S(1)}, u32[]{:S(2)}, u32[]{:S(2)}) collective-permute-start(f32[1,128]{1,0:T(1,128)} %bitcast.10), channel_id=1, source_target_pairs={{0,4},{4,0},{8,12},{12,8},{1,5},{5,1},{9,13},{13,9},{2,6},{6,2},{1... | collective-permute-start | bytes 1544 | tf_op jit(solution)/shard_map/ppermute | solution.py:314
  11.0 3.3 %collective-permute-start.6 = (f32[24,128]{1,0:T(8,128)S(1)}, f32[24,128]{1,0:T(8,128)S(1)}, u32[]{:S(2)}, u32[]{:S(2)}) collective-permute-start(f32[24,128]{1,0:T(8,128)S(1)} %first.1.refs_0_), channel_id=1, source_target_pairs={{0,3},{1,2},{2,1},{3,0},{4,7},{5,6},{6,5},{7,4},{8,11},{9,10},{10,... | collective-permute-start | bytes 36872 | tf_op jit(solution)/shard_map/ppermute | solution.py:314
  11.2 3.7 %collective-permute-start.5 = (f32[24,128]{1,0:T(8,128)S(1)}, f32[24,128]{1,0:T(8,128)S(1)}, u32[]{:S(2)}, u32[]{:S(2)}) collective-permute-start(f32[24,128]{1,0:T(8,128)S(1)} %first.1.refs_0_), channel_id=1, source_target_pairs={{0,2},{1,3},{2,0},{3,1},{4,6},{5,7},{6,4},{7,5},{8,10},{9,11},{10,... | collective-permute-start | bytes 36872 | tf_op jit(solution)/shard_map/ppermute | solution.py:314
  12.6 2.3 %collective-permute-start.4 = (f32[24,128]{1,0:T(8,128)S(1)}, f32[24,128]{1,0:T(8,128)S(1)}, u32[]{:S(2)}, u32[]{:S(2)}) collective-permute-start(f32[24,128]{1,0:T(8,128)S(1)} %first.1.refs_0_), channel_id=1, source_target_pairs={{0,1},{1,0},{2,3},{3,2},{4,5},{5,4},{6,7},{7,6},{8,9},{9,8},{10,11... | collective-permute-start | bytes 36872 | tf_op jit(solution)/shard_map/ppermute | solution.py:314
  14.9 6.1 %collective-permute-start.9 = (f32[16,128]{1,0:T(8,128)S(1)}, f32[16,128]{1,0:T(8,128)S(1)}, u32[]{:S(2)}, u32[]{:S(2)}) collective-permute-start(f32[16,128]{1,0:T(8,128)S(1)} %middle.1.refs_0_), channel_id=1, source_target_pairs={{0,12},{4,8},{8,4},{12,0},{1,13},{5,9},{9,5},{13,1},{2,14},{6,10},... | collective-permute-start | bytes 24584 | tf_op jit(solution)/shard_map/ppermute | solution.py:314
  16.9 4.5 %collective-permute-start.8 = (f32[16,128]{1,0:T(8,128)S(1)}, f32[16,128]{1,0:T(8,128)S(1)}, u32[]{:S(2)}, u32[]{:S(2)}) collective-permute-start(f32[16,128]{1,0:T(8,128)S(1)} %middle.1.refs_0_), channel_id=1, source_target_pairs={{0,8},{4,12},{8,0},{12,4},{1,9},{5,13},{9,1},{13,5},{2,10},{6,14},... | collective-permute-start | bytes 24584 | tf_op jit(solution)/shard_map/ppermute | solution.py:314
  16.9 4.5 %collective-permute-start.7 = (f32[16,128]{1,0:T(8,128)S(1)}, f32[16,128]{1,0:T(8,128)S(1)}, u32[]{:S(2)}, u32[]{:S(2)}) collective-permute-start(f32[16,128]{1,0:T(8,128)S(1)} %middle.1.refs_0_), channel_id=1, source_target_pairs={{0,4},{4,0},{8,12},{12,8},{1,5},{5,1},{9,13},{13,9},{2,6},{6,2},{1... | collective-permute-start | bytes 24584 | tf_op jit(solution)/shard_map/ppermute | solution.py:314
  22.7 5.4 %collective-permute-start.10 = (f32[8,128]{1,0:T(8,128)S(1)}, f32[8,128]{1,0:T(8,128)S(1)}, u32[]{:S(2)}, u32[]{:S(2)}) collective-permute-start(f32[8,128]{1,0:T(8,128)S(1)} %get-tuple-element.27), channel_id=1, source_target_pairs={{0,12},{4,8},{8,4},{12,0},{1,13},{5,9},{9,5},{13,1},{2,14},{6,10},... | collective-permute-start | bytes 12296 | tf_op jit(solution)/shard_map/ppermute | solution.py:314
  24.6 4.5 %collective-permute-start.11 = (f32[8,128]{1,0:T(8,128)S(1)}, f32[8,128]{1,0:T(8,128)S(1)}, u32[]{:S(2)}, u32[]{:S(2)}) collective-permute-start(f32[8,128]{1,0:T(8,128)S(1)} %get-tuple-element.28), channel_id=1, source_target_pairs={{0,8},{4,12},{8,0},{12,4},{1,9},{5,13},{9,1},{13,5},{2,10},{6,14},... | collective-permute-start | bytes 12296 | tf_op jit(solution)/shard_map/ppermute | solution.py:314
  25.7 3.6 %collective-permute-start.12 = (f32[8,128]{1,0:T(8,128)S(1)}, f32[8,128]{1,0:T(8,128)S(1)}, u32[]{:S(2)}, u32[]{:S(2)}) collective-permute-start(f32[8,128]{1,0:T(8,128)S(1)} %get-tuple-element.29), channel_id=1, source_target_pairs={{0,4},{4,0},{8,12},{12,8},{1,5},{5,1},{9,13},{13,9},{2,6},{6,2},{1... | collective-permute-start | bytes 12296 | tf_op jit(solution)/shard_map/ppermute | solution.py:314

commit v11 on v10

--- a/solution.py
+++ b/solution.py
@@ -235,7 +235,7 @@
 
 
 def gather_kernel(tiles, masks, *refs):
-    parts, (innovations_ref, error_ref) = refs[:-2], refs[-2:]
+    parts, (innovations_ref, error_ref, norm_ref) = refs[:-3], refs[-3:]
     _, within, per_row = place()
     pieces = innovations_ref.shape[0]
     for mask, part in zip(masks, parts):
@@ -243,13 +243,14 @@
         for a in range(tiles):
             innovations_ref[pl.ds(a * per_row + there, 1), :] = part[pieces + a : pieces + a + 1, :]
         error_ref[pl.ds(there, 1), :] = part[pieces + tiles : pieces + tiles + 1, :]
+    norm_ref[...] = jnp.broadcast_to(total_of(innovations_ref[...] * innovations_ref[...]), norm_ref.shape)
 
 
 def total_of(x):
     return jnp.sum(jnp.sum(x, axis=0, keepdims=True), axis=1, keepdims=True)
 
 
-def second_kernel(reach_tiles, inverse_members, peers, class_ref, share_ref, innovations_ref, error_ref, *refs):
+def second_kernel(reach_tiles, inverse_members, peers, class_ref, share_ref, innovations_ref, error_ref, norm_ref, *refs):
     parts, refs = refs[:peers], refs[peers:]
     sent, refs = refs[:peers], refs[peers:]
     state_ref, direction, residual, start, whole_image, column, across, sums, product = refs
@@ -258,7 +259,7 @@
     image = parts[0][...]
     for part in parts[1:]:
         image = image + part[...]
-    norm_now = total_of(innovations * innovations)
+    norm_now = norm_ref[:, 0:1]
     alpha = norm_now / total_of(innovations * image)
     residual_now = innovations - alpha * image
     residual[...] = residual_now
@@ -407,11 +408,11 @@
         name="middle",
     )(*payloads)
     parts = exchange(row, nearest_first(row_count), [part] * row_count)
-    whole, error = pl.pallas_call(
+    whole, error, norm = pl.pallas_call(
         functools.partial(gather_kernel, row_count, payload_order),
-        out_shape=[pltpu.VMEM((pieces, LANES), f32), pltpu.VMEM((per_row, LANES), f32)],
+        out_shape=[pltpu.VMEM(shape, f32) for shape in ((pieces, LANES), (per_row, LANES), (1, LANES))],
         in_specs=[VMEM_SPEC] * per_row,
-        out_specs=[VMEM_SPEC] * 2,
+        out_specs=[VMEM_SPEC] * 3,
         compiler_params=params,
         name="gather",
     )(*payloads)
@@ -432,7 +433,7 @@
     *sent, state = pl.pallas_call(
         functools.partial(second_kernel, reach_tiles, inverse_members, row_count),
         out_shape=[pltpu.VMEM((8, LANES), f32) for _ in range(row_count + 1)],
-        in_specs=[SMEM_SPEC] + [VMEM_SPEC] * (row_count + 3),
+        in_specs=[SMEM_SPEC] + [VMEM_SPEC] * (row_count + 4),
         out_specs=[VMEM_SPEC] * (row_count + 1),
         scratch_shapes=[pltpu.VMEM((pieces, LANES), f32)] * 4
         + [pltpu.VMEM((total_obs, LANES), f32)]
@@ -440,7 +441,7 @@
         + [pltpu.VMEM((pieces, LANES), f32)],
         compiler_params=params,
         name="second",
-    )(classes, share, whole, error, *parts)
+    )(classes, share, whole, error, norm, *parts)
     last_order = farthest_first(row_count)
     got = exchange(row, last_order, [sent[mask] for mask in last_order])
     solution_part, residual_part = pl.pallas_call(

time: 30 us -> 30.1 us (level)
  no operation moved by 1% of the time
where the time goes in v11:
time: 30.1 us; the launch traced here: 30 us
  starting transfers between devices  16.6 us (55%)
  waiting for transfers between devices  6.46 us (21%)
  Pallas kernels  6.23 us (21%)
  between operations  0.71 us (2%)
    ppermute x12, starting transfers between devices, exchange(): lax.ppermute(value, axes, [(i, i ^ mask) for i in range(count)])  16 us
    ppermute x12, waiting for transfers between devices, exchange(): lax.ppermute(value, axes, [(i, i ^ mask) for i in range(count)])  6.46 us
    pallas_call x1, Pallas kernels, vectors_only(): pl.pallas_call(functools.partial(strips_kernel, reach_tiles), out_shape=[...  1.72 us
    pallas_call x1, Pallas kernels, vectors_only(): pl.pallas_call(functools.partial(share_kernel, reach_tiles), out_shape=pl...  1.67 us
    pallas_call x1, Pallas kernels, vectors_only(): pl.pallas_call(functools.partial(second_kernel, reach_tiles, inverse_memb...  1.39 us
    pallas_call x1, Pallas kernels, vectors_only(): pl.pallas_call(functools.partial(first_kernel, reach_tiles, inverse_membe...  0.62 us
  transfers between devices with their start and end apart: 13, of which 7 were waited for; matrix products, arithmetic and copies ran while one was open for 0% of the time, Pallas kernels for 12%

profile of v11, /device:TPU:0, one launch (start us, length us, event | category | flops | bytes accessed | tf_op | source)
XLA Modules:
  0.0 30.0 jit_solution(1041262678958802439)
XLA Ops:
  0.6 0.5 %collective-permute-start = (bf16[128,2048]{1,0:T(8,128)(2,1)}, bf16[128,2048]{1,0:T(8,128)(2,1)S(1)}, u32[]{:S(2)}, u32[]{:S(2)}) collective-permute-start(bf16[128,2048]{1,0:T(8,128)(2,1)} %own_ref.1), channel_id=1, source_target_pairs={{0,1},{1,0},{2,3},{3,2},{4,5},{5,4},{6,7},{7,6},{8,9},{9,8},{10,11... | collective-permute-start | bytes 1572872 | tf_op jit(solution)/shard_map/ppermute | solution.py:348
  1.2 3.7 %collective-permute-start.3 = (f32[1,128]{1,0:T(1,128)}, f32[1,128]{1,0:T(1,128)S(1)}, u32[]{:S(2)}, u32[]{:S(2)}) collective-permute-start(f32[1,128]{1,0:T(1,128)} %bitcast.8), channel_id=1, source_target_pairs={{0,8},{4,12},{8,0},{12,4},{1,9},{5,13},{9,1},{13,5},{2,10},{6,14},... | collective-permute-start | bytes 1544 | tf_op jit(solution)/shard_map/ppermute | solution.py:315
  4.9 1.3 %collective-permute-start.2 = (f32[1,128]{1,0:T(1,128)}, f32[1,128]{1,0:T(1,128)S(1)}, u32[]{:S(2)}, u32[]{:S(2)}) collective-permute-start(f32[1,128]{1,0:T(1,128)} %bitcast.9), channel_id=1, source_target_pairs={{0,12},{4,8},{8,4},{12,0},{1,13},{5,9},{9,5},{13,1},{2,14},{6,10},... | collective-permute-start | bytes 1544 | tf_op jit(solution)/shard_map/ppermute | solution.py:315
  6.2 0.2 collective-permute-start.1
  6.6 1.7 %strips.1 = (f32[10,128,512]{2,1,0:T(8,128)S(1)}, f32[6,512,128]{2,1,0:T(8,128)S(1)}, s32[4,4]{1,0:T(4,128)S(4)}, bf16[256,2048]{1,0:T(8,128)(2,1)S(1)}, bf16[20...) custom-call(s32[4,4]{1,0:T(4,128)} %class_hbm.1, f32[1,2048]{1,0:T(1,128)S(1)} %bitcast.5, ...), custom_call_target="tpu_custom_call" | custom-call | flops 671088640 | bytes 5242880 | tf_op jit(solution)/shard_map/strips/pallas_call | solution.py:368
  8.4 1.9 %collective-permute-done.2.refs_2_ = f32[1,128]{1,0:T(1,128)S(1)} collective-permute-done((f32[1,128]{1,0:T(1,128)}, f32[1,128]{1,0:T(1,128)S(1)}, u32[]{:S(2)}, u32[]{:S(2)}) %collective-permute-start.2) | collective-permute-done | bytes 544 | tf_op jit(solution)/shard_map/ppermute | solution.py:315
  10.3 0.6 %first.1.refs_0_ = f32[24,128]{1,0:T(8,128)S(1)} custom-call(s32[4,4]{1,0:T(4,128)S(4)} %get-tuple-element.18.class_ref, f32[10,128,512]{2,1,0:T(8,128)S(1)} %get-tuple-element.22.row_strips, f32[6,512,128]{2,1,0:T(8,128)S(1)} %get-tuple-element.23.column_strips, f32[1,128]{1,0:T(1,128)S(1)} %bitcast.7, f32[1,128]{1,0:T(1,128)S(1)} %bitcast.11, ...), custom_call_target="tpu_custom_call" | custom-call | tf_op jit(solution)/shard_map/first/pallas_call | solution.py:390
  11.0 0.2 collective-permute-start.6
  11.2 1.4 %collective-permute-start.5 = (f32[24,128]{1,0:T(8,128)S(1)}, f32[24,128]{1,0:T(8,128)S(1)}, u32[]{:S(2)}, u32[]{:S(2)}) collective-permute-start(f32[24,128]{1,0:T(8,128)S(1)} %first.1.refs_0_), channel_id=1, source_target_pairs={{0,2},{1,3},{2,0},{3,1},{4,6},{5,7},{6,4},{7,5},{8,10},{9,11},{10,... | collective-permute-start | bytes 36872 | tf_op jit(solution)/shard_map/ppermute | solution.py:315
  12.6 0.3 collective-permute-start.4
  12.9 1.3 %collective-permute-done.6.refs_3_ = f32[24,128]{1,0:T(8,128)S(1)} collective-permute-done((f32[24,128]{1,0:T(8,128)S(1)}, f32[24,128]{1,0:T(8,128)S(1)}, u32[]{:S(2)}, u32[]{:S(2)}) %collective-permute-start.6) | collective-permute-done | bytes 12320 | tf_op jit(solution)/shard_map/ppermute | solution.py:315
  14.2 0.6 %collective-permute-done.5.refs_2_ = f32[24,128]{1,0:T(8,128)S(1)} collective-permute-done((f32[24,128]{1,0:T(8,128)S(1)}, f32[24,128]{1,0:T(8,128)S(1)}, u32[]{:S(2)}, u32[]{:S(2)}) %collective-permute-start.5) | collective-permute-done | bytes 12320 | tf_op jit(solution)/shard_map/ppermute | solution.py:315
  14.9 2.0 %collective-permute-start.9 = (f32[16,128]{1,0:T(8,128)S(1)}, f32[16,128]{1,0:T(8,128)S(1)}, u32[]{:S(2)}, u32[]{:S(2)}) collective-permute-start(f32[16,128]{1,0:T(8,128)S(1)} %middle.1.refs_0_), channel_id=1, source_target_pairs={{0,12},{4,8},{8,4},{12,0},{1,13},{5,9},{9,5},{13,1},{2,14},{6,10},... | collective-permute-start | bytes 24584 | tf_op jit(solution)/shard_map/ppermute | solution.py:315
  16.9 2.4 %collective-permute-start.7 = (f32[16,128]{1,0:T(8,128)S(1)}, f32[16,128]{1,0:T(8,128)S(1)}, u32[]{:S(2)}, u32[]{:S(2)}) collective-permute-start(f32[16,128]{1,0:T(8,128)S(1)} %middle.1.refs_0_), channel_id=1, source_target_pairs={{0,4},{4,0},{8,12},{12,8},{1,5},{5,1},{9,13},{13,9},{2,6},{6,2},{1... | collective-permute-start | bytes 24584 | tf_op jit(solution)/shard_map/ppermute | solution.py:315
  19.3 1.7 %share.1.share_ref = f32[10,512,512]{2,1,0:T(8,128)S(1)} custom-call(s32[4,4]{1,0:T(4,128)S(4)} %get-tuple-element.18.class_ref, f32[1,2048]{1,0:T(1,128)S(1)} %bitcast.6, bf16[256,2048]{1,0:T(8,128)(2,1)S(1)} %get-tuple-element.19.both, bf16[2048,256]{1,0:T(8,128)(2,1)S(1)} %get-tuple-element.20.turned, f32[2048,128]{1,0:T(8,128)S(1)} %get-tuple-element.21.column, ...), custom_call_target="tpu_custom_call" | custom-call | flops 1342177280 | bytes 10485760 | tf_op jit(solution)/shard_map/share/pallas_call | solution.py:420
  21.1 0.3 %collective-permute-done.8.refs_2_ = f32[16,128]{1,0:T(8,128)S(1)} collective-permute-done((f32[16,128]{1,0:T(8,128)S(1)}, f32[16,128]{1,0:T(8,128)S(1)}, u32[]{:S(2)}, u32[]{:S(2)}) %collective-permute-start.8) | collective-permute-done | bytes 8224 | tf_op jit(solution)/shard_map/ppermute | solution.py:315
  21.5 1.4 %second.1 = (f32[8,128]{1,0:T(8,128)S(1)}, f32[8,128]{1,0:T(8,128)S(1)}, f32[8,128]{1,0:T(8,128)S(1)}, f32[8,128]{1,0:T(8,128)S(1)}, f32[8,128]{1,0:T(8,128)S(1)}) custom-call(s32[4,4]{1,0:T(4,128)S(4)} %get-tuple-element.18.class_ref, f32[10,512,512]{2,1,0:T(8,128)S(1)} %share.1.share_ref, f32[16,128]{1,0:T(8,128)S(1)} %get-tuple-element.24.innovations_ref, ...), custom_call_target="tpu_custom_call" | custom-call | tf_op jit(solution)/shard_map/second/pallas_call | solution.py:433
  22.9 1.9 %collective-permute-start.10 = (f32[8,128]{1,0:T(8,128)S(1)}, f32[8,128]{1,0:T(8,128)S(1)}, u32[]{:S(2)}, u32[]{:S(2)}) collective-permute-start(f32[8,128]{1,0:T(8,128)S(1)} %get-tuple-element.29), channel_id=1, source_target_pairs={{0,12},{4,8},{8,4},{12,0},{1,13},{5,9},{9,5},{13,1},{2,14},{6,10},... | collective-permute-start | bytes 12296 | tf_op jit(solution)/shard_map/ppermute | solution.py:315
  24.7 1.1 %collective-permute-start.11 = (f32[8,128]{1,0:T(8,128)S(1)}, f32[8,128]{1,0:T(8,128)S(1)}, u32[]{:S(2)}, u32[]{:S(2)}) collective-permute-start(f32[8,128]{1,0:T(8,128)S(1)} %get-tuple-element.30), channel_id=1, source_target_pairs={{0,8},{4,12},{8,0},{12,4},{1,9},{5,13},{9,1},{13,5},{2,10},{6,14},... | collective-permute-start | bytes 12296 | tf_op jit(solution)/shard_map/ppermute | solution.py:315
  25.8 1.4 %collective-permute-start.12 = (f32[8,128]{1,0:T(8,128)S(1)}, f32[8,128]{1,0:T(8,128)S(1)}, u32[]{:S(2)}, u32[]{:S(2)}) collective-permute-start(f32[8,128]{1,0:T(8,128)S(1)} %get-tuple-element.31), channel_id=1, source_target_pairs={{0,4},{4,0},{8,12},{12,8},{1,5},{5,1},{9,13},{13,9},{2,6},{6,2},{1... | collective-permute-start | bytes 12296 | tf_op jit(solution)/shard_map/ppermute | solution.py:315
  27.2 1.0 %collective-permute-done.10.refs_1_ = f32[8,128]{1,0:T(8,128)S(1)} collective-permute-done((f32[8,128]{1,0:T(8,128)S(1)}, f32[8,128]{1,0:T(8,128)S(1)}, u32[]{:S(2)}, u32[]{:S(2)}) %collective-permute-start.10) | collective-permute-done | bytes 4128 | tf_op jit(solution)/shard_map/ppermute | solution.py:315
  28.3 1.0 %collective-permute-done.11.refs_2_ = f32[8,128]{1,0:T(8,128)S(1)} collective-permute-done((f32[8,128]{1,0:T(8,128)S(1)}, f32[8,128]{1,0:T(8,128)S(1)}, u32[]{:S(2)}, u32[]{:S(2)}) %collective-permute-start.11) | collective-permute-done | bytes 4128 | tf_op jit(solution)/shard_map/ppermute | solution.py:315
  29.2 0.2 collective-permute-done.12.refs_3_
  29.4 0.5 %last.1 = (f32[1,128]{1,0:T(1,128)}, f32[1,128]{1,0:T(1,128)}) custom-call(f32[8,128]{1,0:T(8,128)S(1)} %get-tuple-element.27.state_ref, f32[8,128]{1,0:T(8,128)S(1)} %get-tuple-element.28.refs_0_, f32[8,128]{1,0:T(8,128)S(1)} %collective-permute-done.10.refs_1_, f32[8,128]{1,0:T(8,128)S(1)} %collective-permute-done.11.refs_2_, ...), custom_call_target="tpu_custom_call" | custom-call | tf_op jit(solution)/shard_map/last/pallas_call | solution.py:447
  (18 shorter events, 0.3 us)
Async XLA Ops:
  0.6 5.8 %collective-permute-start = (bf16[128,2048]{1,0:T(8,128)(2,1)}, bf16[128,2048]{1,0:T(8,128)(2,1)S(1)}, u32[]{:S(2)}, u32[]{:S(2)}) collective-permute-start(bf16[128,2048]{1,0:T(8,128)(2,1)} %own_ref.1), channel_id=1, source_target_pairs={{0,1},{1,0},{2,3},{3,2},{4,5},{5,4},{6,7},{7,6},{8,9},{9,8},{10,11... | collective-permute-start | bytes 1572872 | tf_op jit(solution)/shard_map/ppermute | solution.py:348
  1.1 5.5 %copy-start = (f32[2048]{0:T(1024)S(1)}, f32[2048]{0:T(1024)}, u32[]{:S(2)}) copy-start(f32[2048]{0:T(1024)} %param.8) | copy-start | bytes 24580
  1.2 5.5 %copy-start.3 = (bf16[128,2048]{1,0:T(8,128)(2,1)S(1)}, bf16[128,2048]{1,0:T(8,128)(2,1)}, u32[]{:S(2)}) copy-start(bf16[128,2048]{1,0:T(8,128)(2,1)} %own_ref.1) | copy-start | bytes 1572868
  1.2 9.2 %copy-start.1 = (f32[128]{0:T(128)S(1)}, f32[128]{0:T(128)}, u32[]{:S(2)}) copy-start(f32[128]{0:T(128)} %param.7) | copy-start | bytes 1540
  1.2 9.2 %copy-start.2 = (f32[128]{0:T(128)S(1)}, f32[128]{0:T(128)}, u32[]{:S(2)}) copy-start(f32[128]{0:T(128)} %param.6) | copy-start | bytes 1540
  1.2 7.2 %collective-permute-start.3 = (f32[1,128]{1,0:T(1,128)}, f32[1,128]{1,0:T(1,128)S(1)}, u32[]{:S(2)}, u32[]{:S(2)}) collective-permute-start(f32[1,128]{1,0:T(1,128)} %bitcast.8), channel_id=1, source_target_pairs={{0,8},{4,12},{8,0},{12,4},{1,9},{5,13},{9,1},{13,5},{2,10},{6,14},... | collective-permute-start | bytes 1544 | tf_op jit(solution)/shard_map/ppermute | solution.py:315
  4.9 5.5 %collective-permute-start.2 = (f32[1,128]{1,0:T(1,128)}, f32[1,128]{1,0:T(1,128)S(1)}, u32[]{:S(2)}, u32[]{:S(2)}) collective-permute-start(f32[1,128]{1,0:T(1,128)} %bitcast.9), channel_id=1, source_target_pairs={{0,12},{4,8},{8,4},{12,0},{1,13},{5,9},{9,5},{13,1},{2,14},{6,10},... | collective-permute-start | bytes 1544 | tf_op jit(solution)/shard_map/ppermute | solution.py:315
  6.2 4.1 %collective-permute-start.1 = (f32[1,128]{1,0:T(1,128)}, f32[1,128]{1,0:T(1,128)S(1)}, u32[]{:S(2)}, u32[]{:S(2)}) collective-permute-start(f32[1,128]{1,0:T(1,128)} %bitcast.10), channel_id=1, source_target_pairs={{0,4},{4,0},{8,12},{12,8},{1,5},{5,1},{9,13},{13,9},{2,6},{6,2},{1... | collective-permute-start | bytes 1544 | tf_op jit(solution)/shard_map/ppermute | solution.py:315
  11.0 3.3 %collective-permute-start.6 = (f32[24,128]{1,0:T(8,128)S(1)}, f32[24,128]{1,0:T(8,128)S(1)}, u32[]{:S(2)}, u32[]{:S(2)}) collective-permute-start(f32[24,128]{1,0:T(8,128)S(1)} %first.1.refs_0_), channel_id=1, source_target_pairs={{0,3},{1,2},{2,1},{3,0},{4,7},{5,6},{6,5},{7,4},{8,11},{9,10},{10,... | collective-permute-start | bytes 36872 | tf_op jit(solution)/shard_map/ppermute | solution.py:315
  11.2 3.7 %collective-permute-start.5 = (f32[24,128]{1,0:T(8,128)S(1)}, f32[24,128]{1,0:T(8,128)S(1)}, u32[]{:S(2)}, u32[]{:S(2)}) collective-permute-start(f32[24,128]{1,0:T(8,128)S(1)} %first.1.refs_0_), channel_id=1, source_target_pairs={{0,2},{1,3},{2,0},{3,1},{4,6},{5,7},{6,4},{7,5},{8,10},{9,11},{10,... | collective-permute-start | bytes 36872 | tf_op jit(solution)/shard_map/ppermute | solution.py:315
  12.6 2.3 %collective-permute-start.4 = (f32[24,128]{1,0:T(8,128)S(1)}, f32[24,128]{1,0:T(8,128)S(1)}, u32[]{:S(2)}, u32[]{:S(2)}) collective-permute-start(f32[24,128]{1,0:T(8,128)S(1)} %first.1.refs_0_), channel_id=1, source_target_pairs={{0,1},{1,0},{2,3},{3,2},{4,5},{5,4},{6,7},{7,6},{8,9},{9,8},{10,11... | collective-permute-start | bytes 36872 | tf_op jit(solution)/shard_map/ppermute | solution.py:315
  14.9 6.2 %collective-permute-start.9 = (f32[16,128]{1,0:T(8,128)S(1)}, f32[16,128]{1,0:T(8,128)S(1)}, u32[]{:S(2)}, u32[]{:S(2)}) collective-permute-start(f32[16,128]{1,0:T(8,128)S(1)} %middle.1.refs_0_), channel_id=1, source_target_pairs={{0,12},{4,8},{8,4},{12,0},{1,13},{5,9},{9,5},{13,1},{2,14},{6,10},... | collective-permute-start | bytes 24584 | tf_op jit(solution)/shard_map/ppermute | solution.py:315
  16.9 4.5 %collective-permute-start.8 = (f32[16,128]{1,0:T(8,128)S(1)}, f32[16,128]{1,0:T(8,128)S(1)}, u32[]{:S(2)}, u32[]{:S(2)}) collective-permute-start(f32[16,128]{1,0:T(8,128)S(1)} %middle.1.refs_0_), channel_id=1, source_target_pairs={{0,8},{4,12},{8,0},{12,4},{1,9},{5,13},{9,1},{13,5},{2,10},{6,14},... | collective-permute-start | bytes 24584 | tf_op jit(solution)/shard_map/ppermute | solution.py:315
  16.9 4.5 %collective-permute-start.7 = (f32[16,128]{1,0:T(8,128)S(1)}, f32[16,128]{1,0:T(8,128)S(1)}, u32[]{:S(2)}, u32[]{:S(2)}) collective-permute-start(f32[16,128]{1,0:T(8,128)S(1)} %middle.1.refs_0_), channel_id=1, source_target_pairs={{0,4},{4,0},{8,12},{12,8},{1,5},{5,1},{9,13},{13,9},{2,6},{6,2},{1... | collective-permute-start | bytes 24584 | tf_op jit(solution)/shard_map/ppermute | solution.py:315
  22.9 5.4 %collective-permute-start.10 = (f32[8,128]{1,0:T(8,128)S(1)}, f32[8,128]{1,0:T(8,128)S(1)}, u32[]{:S(2)}, u32[]{:S(2)}) collective-permute-start(f32[8,128]{1,0:T(8,128)S(1)} %get-tuple-element.29), channel_id=1, source_target_pairs={{0,12},{4,8},{8,4},{12,0},{1,13},{5,9},{9,5},{13,1},{2,14},{6,10},... | collective-permute-start | bytes 12296 | tf_op jit(solution)/shard_map/ppermute | solution.py:315
  24.7 4.5 %collective-permute-start.11 = (f32[8,128]{1,0:T(8,128)S(1)}, f32[8,128]{1,0:T(8,128)S(1)}, u32[]{:S(2)}, u32[]{:S(2)}) collective-permute-start(f32[8,128]{1,0:T(8,128)S(1)} %get-tuple-element.30), channel_id=1, source_target_pairs={{0,8},{4,12},{8,0},{12,4},{1,9},{5,13},{9,1},{13,5},{2,10},{6,14},... | collective-permute-start | bytes 12296 | tf_op jit(solution)/shard_map/ppermute | solution.py:315
  25.8 3.6 %collective-permute-start.12 = (f32[8,128]{1,0:T(8,128)S(1)}, f32[8,128]{1,0:T(8,128)S(1)}, u32[]{:S(2)}, u32[]{:S(2)}) collective-permute-start(f32[8,128]{1,0:T(8,128)S(1)} %get-tuple-element.31), channel_id=1, source_target_pairs={{0,4},{4,0},{8,12},{12,8},{1,5},{5,1},{9,13},{13,9},{2,6},{6,2},{1... | collective-permute-start | bytes 12296 | tf_op jit(solution)/shard_map/ppermute | solution.py:315
